TPU v7x, 256 devices: a whole 4x4x8 slice. The times are simulated.
256 devices in a mesh: seq: 64 (over y, z_hi, x, core), adapter: 4 (over z_lo).
Axes of the slice: x: 4, y: 4, z: 8 (z_hi: 2, z_lo: 4; z = z_hi * 4 + z_lo), core: 2. Of those that a mesh axis runs over, the one named last changes fastest.
Arguments:
- hidden: bfloat16 [8, 8192, 8192], P('adapter', 'seq'), may hold values from -6 to 6
- response_base_queries: bfloat16 [8, 8192, 1024], P('adapter', 'seq'), may hold values from -6 to 6
- attention_output_gradient: bfloat16 [8, 8192, 1024], P('adapter', 'seq'), may hold values from -6 to 6
- keys: bfloat16 [49152, 128], P('seq'), may hold values from -6 to 6
- values: bfloat16 [49152, 128], P('seq'), may hold values from -6 to 6
- adapter_down_weight: bfloat16 [8, 16, 8192], P('adapter'), may hold values from -0.0625 to 0.0625
- adapter_up_weight: bfloat16 [8, 16, 1024], P('adapter'), may hold values from -1.5 to 1.5
- lengths: int32 [8], P('adapter'), may hold values from 4096 to 8192
- offsets: int32 [8, 8192], P('adapter', 'seq'), may hold values from 0 to 49151, as said below
Outputs:
- adapter_down_gradient: float32 [8, 16, 8192], P('adapter', None, 'seq')
- adapter_up_gradient: float32 [8, 16, 1024], P('adapter')
- prompt_key_gradient: float32 [49152, 128], P(('seq', 'adapter'))
- prompt_value_gradient: float32 [49152, 128], P(('seq', 'adapter'))
Inputs may be any that keep to these rules, and one draw needn't show every extreme that they name: Row r of every adapter has offsets in [(r // 128) * 768, (r // 128 + 1) * 768).
All inputs are finite; a program needn't handle non-finite values.
Results may differ from a plain program's by a relative error of at most 0.025.
The roundings to bfloat16 on the way count: a program that leaves them out, or rounds other values in their place, can miss the bound.
Values may be sent and summed in bfloat16 or wider, within the bound.
No kernel may reach another device: no remote copies, remote signals or barrier semaphores. Data moves between devices by JAX's collectives and lax.ppermute only.
A program may use at most 192 MiB of HBM per device.

v0:
```python
import functools

import jax
import jax.numpy as jnp
from jax import lax
from jax.experimental import pallas as pl
from jax.experimental.pallas import tpu as pltpu
from jax.sharding import PartitionSpec as P

adapter_scale = 2.0
masked_score = -1.0e30
log2_e = 1.4426950408889634
both_axes = ("seq", "adapter")
row_n_seq = 8

NN = ((1,), (0,))
NT = ((1,), (1,))


def dot(a, b, dims):
    return lax.dot_general(a, b, (dims, ((), ())), preferred_element_type=jnp.float32)


def moved(value, by_even, by_odd):
    peers, planes = lax.axis_size("seq"), lax.axis_size("adapter")
    pairs = []
    for s in range(peers):
        t = s + (by_odd if s % 2 else by_even)
        if 0 <= t < peers:
            for a in range(planes):
                b = a if t // row_n_seq == s // row_n_seq else planes - 1 - a
                pairs.append((s * planes + a, t * planes + b))
    return lax.ppermute(value, both_axes, pairs)


def grouped(value, groups):
    return lax.all_to_all(value, "seq", 0, 0, axis_index_groups=groups, tiled=True)


def attention_kernel(
    where_ref, rel_ref, base_ref, grad_ref, low_ref, up_ref, kv_own, kv_mid, kv_far, kv_swap,
    dquery_ref, own_ref, mid_ref, far_ref, swap_ref,
    window, key_t, score, dprob, dscore_low, acc,
    *, stretch, chunk, rows, adapters, head_dim, heads,
):
    head = pl.program_id(0)
    factor = head_dim**-0.5
    shift = factor * log2_e
    parts = stretch // chunk
    wide = rows * adapters
    block = where_ref[0]
    odd = lax.rem(block, 2) == 1
    spans = [slice(d * stretch, (d + 1) * stretch) for d in range(4)]

    @pl.when(head == 0)
    def _():
        acc[...] = jnp.zeros_like(acc)
        window[spans[0], :] = kv_own[...]
        window[spans[2], :] = kv_mid[...]

        @pl.when(odd)
        def _():
            window[spans[1], :] = kv_far[...]
            window[spans[3], :] = kv_swap[...]

        @pl.when(jnp.logical_not(odd))
        def _():
            window[spans[1], :] = kv_swap[...]
            window[spans[3], :] = kv_far[...]

        for span in spans:
            key_t[:, span] = window[span, :head_dim].T

    query_list = []
    grad_list = []
    line = block * rows + lax.broadcasted_iota(jnp.int32, (rows, head_dim), 0)
    for a in range(adapters):
        raised = dot(low_ref[a], up_ref[a], NN)
        query_list.append(
            (base_ref[a].astype(jnp.float32) + adapter_scale * raised).astype(jnp.bfloat16)
        )
        live = line < where_ref[1 + a]
        grad_list.append(
            jnp.where(live, grad_ref[a].astype(jnp.float32), 0.0).astype(jnp.bfloat16)
        )
    query = jnp.concatenate(query_list, axis=0)
    grad = jnp.concatenate(grad_list, axis=0)
    rel = rel_ref[...]
    place = lax.broadcasted_iota(jnp.int32, (chunk, wide), 0)
    bias3 = jnp.where(block >= 3, 0.0, masked_score)

    def fold(x, op):
        return op(x.reshape(x.shape[0] // 8, 8, x.shape[1]), axis=0)

    peak = None
    for d in range(3):
        high = None
        for c in range(parts):
            at = slice(d * stretch + c * chunk, d * stretch + (c + 1) * chunk)
            s = dot(window[at, :head_dim], query, NT)
            dp = dot(window[at, head_dim:], grad, NT)
            if d == 0:
                early = rel >= place + c * chunk
                far = slice(3 * stretch + c * chunk, 3 * stretch + (c + 1) * chunk)
                s = jnp.where(early, s, dot(window[far, :head_dim], query, NT) + bias3)
                dp = jnp.where(early, dp, dot(window[far, head_dim:], grad, NT))
            score[at, :] = s
            dprob[at, :] = dp
            top = fold(s, jnp.max)
            high = top if high is None else jnp.maximum(high, top)
        if d:
            high = jnp.where(block >= d, high, masked_score)
        peak = high if peak is None else jnp.maximum(peak, high)
    peak = jnp.max(peak, axis=0, keepdims=True)
    total = jnp.zeros((8, wide), jnp.float32)
    delta = jnp.zeros((8, wide), jnp.float32)
    for d in range(3):
        level = peak if d == 0 else jnp.where(block >= d, peak, -masked_score)
        for c in range(parts):
            at = slice(d * stretch + c * chunk, d * stretch + (c + 1) * chunk)
            e = jnp.exp2((score[at, :] - level) * shift)
            score[at, :] = e
            total = total + fold(e, jnp.sum)
            delta = delta + fold(e * dprob[at, :], jnp.sum)
    scale = 1.0 / jnp.sum(total, axis=0, keepdims=True)
    delta = jnp.sum(delta, axis=0, keepdims=True) * scale
    zero = jnp.zeros((chunk, wide), jnp.float32)
    for d in range(3):
        for c in range(parts):
            at = slice(d * stretch + c * chunk, d * stretch + (c + 1) * chunk)
            p = score[at, :] * scale
            ds = p * (dprob[at, :] - delta)
            if d == 0:
                early = rel >= place + c * chunk
                pieces = (
                    (0, jnp.where(early, p, zero), jnp.where(early, ds, zero)),
                    (3, jnp.where(early, zero, p), jnp.where(early, zero, ds)),
                )
            else:
                pieces = ((d, p, ds),)
            for e, p_e, ds_e in pieces:
                to = slice(e * stretch + c * chunk, e * stretch + (c + 1) * chunk)
                p_e = p_e.astype(jnp.bfloat16)
                ds_e = ds_e.astype(jnp.bfloat16)
                dscore_low[to, :] = ds_e
                acc[to, :head_dim] += dot(ds_e, query, NN)
                acc[to, head_dim:] += dot(p_e, grad, NN)
    dquery = (dot(key_t[...], dscore_low[...], NN).T * factor).astype(jnp.bfloat16)
    for a in range(adapters):
        dquery_ref[a] = dquery[a * rows : (a + 1) * rows]

    @pl.when(head == heads - 1)
    def _():
        def put(out, span):
            out[:, :head_dim] = (acc[span, :head_dim] * factor).astype(out.dtype)
            out[:, head_dim:] = acc[span, head_dim:].astype(out.dtype)

        put(own_ref, spans[0])
        put(mid_ref, spans[2])

        @pl.when(odd)
        def _():
            put(far_ref, spans[1])
            put(swap_ref, spans[3])

        @pl.when(jnp.logical_not(odd))
        def _():
            put(far_ref, spans[3])
            put(swap_ref, spans[1])


def attention_grads(where, rel, base, grad, low, up, own, mid, far, swap):
    adapters, rows, features = base.shape
    stretch, both = own.shape
    head_dim = both // 2
    heads = features // head_dim
    rank = low.shape[2]
    wide = rows * adapters
    body = functools.partial(
        attention_kernel,
        stretch=stretch,
        chunk=256,
        rows=rows,
        adapters=adapters,
        head_dim=head_dim,
        heads=heads,
    )
    per_head = pl.BlockSpec((adapters, rows, head_dim), lambda h, w: (0, 0, h))

    def whole(*shape):
        return pl.BlockSpec(shape, lambda h, w: (0,) * len(shape))

    return pl.pallas_call(
        body,
        grid_spec=pltpu.PrefetchScalarGridSpec(
            num_scalar_prefetch=1,
            grid=(heads,),
            in_specs=[
                whole(1, wide),
                per_head,
                per_head,
                whole(adapters, rows, rank),
                pl.BlockSpec((adapters, rank, head_dim), lambda h, w: (0, 0, h)),
            ]
            + [whole(stretch, both)] * 4,
            out_specs=[per_head] + [whole(stretch, both)] * 4,
            scratch_shapes=[
                pltpu.VMEM((4 * stretch, both), jnp.bfloat16),
                pltpu.VMEM((head_dim, 4 * stretch), jnp.bfloat16),
                pltpu.VMEM((3 * stretch, wide), jnp.float32),
                pltpu.VMEM((3 * stretch, wide), jnp.float32),
                pltpu.VMEM((4 * stretch, wide), jnp.bfloat16),
                pltpu.VMEM((4 * stretch, both), jnp.float32),
            ],
        ),
        out_shape=[
            jax.ShapeDtypeStruct(base.shape, jnp.bfloat16),
            jax.ShapeDtypeStruct((stretch, both), jnp.float32),
            jax.ShapeDtypeStruct((stretch, both), jnp.float32),
            jax.ShapeDtypeStruct((stretch, both), jnp.bfloat16),
            jax.ShapeDtypeStruct((stretch, both), jnp.bfloat16),
        ],
        compiler_params=pltpu.CompilerParams(
            dimension_semantics=("arbitrary",), vmem_limit_bytes=44 * 1024 * 1024
        ),
        name="attention_grads",
    )(where, rel, base, grad, low, up, own, mid, far, swap)


def adapter_kernel(dquery_ref, low_ref, up_ref, hidden_ref, out_ref, small, *, adapters, rank, lanes, inner):
    step = pl.program_id(0)
    outer = pl.num_programs(0)

    @pl.when(step == 0)
    def _():
        for a in range(adapters):
            at = slice(a * rank, (a + 1) * rank)
            small[at, :] = dot(up_ref[a], dquery_ref[a], NT).astype(jnp.bfloat16)
            low_t = low_ref[a].astype(jnp.float32).T.astype(jnp.bfloat16)
            piece = adapter_scale * dot(low_t, dquery_ref[a], NN)
            for i in range(inner):
                out_ref[i, outer, at, :] = piece[:, i * lanes : (i + 1) * lanes].astype(out_ref.dtype)

    for a in range(adapters):
        at = slice(a * rank, (a + 1) * rank)
        piece = adapter_scale * dot(small[at, :], hidden_ref[a], NN)
        for i in range(inner):
            out_ref[i, step, at, :] = piece[:, i * lanes : (i + 1) * lanes].astype(out_ref.dtype)


def adapter_grads(dquery, low, up, hidden, inner, outer):
    adapters, rows, features = dquery.shape
    rank = low.shape[2]
    width = hidden.shape[2]
    lanes = width // (inner * outer)

    def whole(*shape):
        return pl.BlockSpec(shape, lambda g: (0,) * len(shape))

    return pl.pallas_call(
        functools.partial(adapter_kernel, adapters=adapters, rank=rank, lanes=lanes, inner=inner),
        grid=(outer,),
        in_specs=[
            whole(adapters, rows, features),
            whole(adapters, rows, rank),
            whole(adapters, rank, features),
            pl.BlockSpec((adapters, rows, inner * lanes), lambda g: (0, 0, g)),
        ],
        out_specs=whole(inner, outer + 1, adapters * rank, lanes),
        out_shape=jax.ShapeDtypeStruct((inner, outer + 1, adapters * rank, lanes), jnp.bfloat16),
        scratch_shapes=[pltpu.VMEM((adapters * rank, rows), jnp.bfloat16)],
        compiler_params=pltpu.CompilerParams(
            dimension_semantics=("arbitrary",), vmem_limit_bytes=24 * 1024 * 1024
        ),
        name="adapter_grads",
    )(dquery, low, up, hidden)


def local(
    hidden,
    response_base_queries,
    attention_output_gradient,
    keys,
    values,
    adapter_down_weight,
    adapter_up_weight,
    lengths,
    offsets,
):
    adapt_n, row_n, feature_n = response_base_queries.shape
    rank = adapter_down_weight.shape[1]
    stretch_n, head_dim = keys.shape
    seq_index = lax.axis_index("seq")
    planes = lax.axis_size("adapter")
    inner = row_n_seq
    outer = lax.axis_size("seq") // inner

    own = jnp.concatenate([keys, values], axis=1)
    mid = moved(own, 2, 2)
    far = moved(own, 1, 3)
    swap = moved(mid, 1, -1)

    low = jnp.einsum(
        "tbu,tyu->tby", hidden, adapter_down_weight, preferred_element_type=jnp.float32
    ).astype(jnp.bfloat16)
    where = jnp.concatenate([seq_index[None].astype(jnp.int32), lengths])
    rel = (offsets - seq_index * stretch_n).reshape(1, adapt_n * row_n)
    dquery, own_part, mid_part, far_part, swap_part = attention_grads(
        where,
        rel,
        response_base_queries,
        attention_output_gradient,
        low,
        adapter_up_weight,
        own,
        mid,
        far,
        swap,
    )
    far_back = moved(far_part, -3, -1)
    swap_back = moved(swap_part, 1, -1)
    mid_back = moved((mid_part + swap_back.astype(jnp.float32)).astype(jnp.bfloat16), -2, -2)
    prompt = own_part + far_back.astype(jnp.float32) + mid_back.astype(jnp.float32)
    prompt = prompt.astype(jnp.bfloat16).reshape(planes, stretch_n // planes, 2 * head_dim)
    prompt = lax.all_to_all(prompt, "adapter", 0, 0, tiled=True).astype(jnp.float32).sum(0)

    blocks = adapter_grads(dquery, low, adapter_up_weight, hidden, inner, outer)
    near = [[g * inner + i for i in range(inner)] for g in range(outer)]
    across = [[g * inner + i for g in range(outer)] for i in range(inner)]
    blocks = grouped(blocks, near).astype(jnp.float32).sum(0)
    up_copies = jnp.broadcast_to(blocks[outer:], blocks[:outer].shape)
    blocks = grouped(jnp.stack([blocks[:outer], up_copies], axis=1), across).sum(0)
    down = blocks[0].reshape(adapt_n, rank, -1)
    up_blocks = grouped(jnp.broadcast_to(blocks[1:], (inner,) + blocks.shape[1:]), near)
    up_gradient = up_blocks.reshape(inner, adapt_n, rank, -1).transpose(1, 2, 0, 3)
    return (
        down,
        up_gradient.reshape(adapt_n, rank, feature_n),
        prompt[:, :head_dim],
        prompt[:, head_dim:],
    )


def solution(mesh):
    return jax.shard_map(
        local,
        mesh=mesh,
        in_specs=(
            P("adapter", "seq", None),
            P("adapter", "seq", None),
            P("adapter", "seq", None),
            P("seq", None),
            P("seq", None),
            P("adapter", None, None),
            P("adapter", None, None),
            P("adapter"),
            P("adapter", "seq"),
        ),
        out_specs=(
            P("adapter", None, "seq"),
            P("adapter", None, None),
            P(("seq", "adapter"), None),
            P(("seq", "adapter"), None),
        ),
        check_vma=False,
    )
```

profile of v0, /device:TPU:1, one launch (start us, length us, event | category | flops | bytes accessed | tf_op | source)
XLA Modules:
  0.0 149.3 jit_solution(1756814164278507195)
XLA Ops:
  0.6 0.0 copy-start
  0.6 0.0 copy-start.3
  0.7 0.0 copy-start.2
  0.7 1.1 constant_dynamic-update-slice_fusion.1
  1.7 1.0 constant_dynamic-update-slice_fusion.kv_own
  2.7 4.0 %collective-permute-start = (bf16[768,256]{1,0:T(8,128)(2,1)S(1)}, bf16[768,256]{1,0:T(8,128)(2,1)S(1)}, u32[]{:S(2)}, u32[]{:S(2)}) collective-permute-start(bf16[768,256]{1,0:T(8,128)(2,1)S(1)} %constant_dynamic-update-slice_fusion.kv_own), channel_id=1, source_target_pairs={{0,8},{1,9},{2,10},{3,11},{4,12},{5,13},{6,14},{7,15},{8,16},{9,17... | collective-permute-start | bytes 1179656 | tf_op jit(solution)/shard_map/ppermute | solution.py:33
  6.7 5.2 %collective-permute-start.1 = (bf16[768,256]{1,0:T(8,128)(2,1)S(1)}, bf16[768,256]{1,0:T(8,128)(2,1)S(1)}, u32[]{:S(2)}, u32[]{:S(2)}) collective-permute-start(bf16[768,256]{1,0:T(8,128)(2,1)S(1)} %constant_dynamic-update-slice_fusion.kv_own), channel_id=1, source_target_pairs={{0,4},{1,5},{2,6},{3,7},{4,16},{5,17},{6,18},{7,19},{8,12},{9,13},... | collective-permute-start | bytes 1179656 | tf_op jit(solution)/shard_map/ppermute | solution.py:33
  11.9 0.0 copy-start.8
  11.9 0.0 copy-start.1
  11.9 0.8 broadcast_subtract_fusion
  12.8 1.7 %collective-permute-done.kv_mid = bf16[768,256]{1,0:T(8,128)(2,1)S(1)} collective-permute-done((bf16[768,256]{1,0:T(8,128)(2,1)S(1)}, bf16[768,256]{1,0:T(8,128)(2,1)S(1)}, u32[]{:S(2)}, u32[]{:S(2)}) %collective-permute-start) | collective-permute-done | bytes 393248 | tf_op jit(solution)/shard_map/ppermute | solution.py:33
  14.4 0.0 copy-start.4
  14.4 2.7 %collective-permute-start.2 = (bf16[768,256]{1,0:T(8,128)(2,1)S(1)}, bf16[768,256]{1,0:T(8,128)(2,1)S(1)}, u32[]{:S(2)}, u32[]{:S(2)}) collective-permute-start(bf16[768,256]{1,0:T(8,128)(2,1)S(1)} %collective-permute-done.kv_mid), channel_id=1, source_target_pairs={{0,4},{1,5},{2,6},{3,7},{4,0},{5,1},{6,2},{7,3},{8,12},{9,13},{10,... | collective-permute-start | bytes 1179656 | tf_op jit(solution)/shard_map/ppermute | solution.py:33
  17.1 0.7 pad_add_fusion.where_ref
  17.9 0.0 copy-done
  17.9 3.4 %convolution_convert_fusion.low_ref = bf16[2,128,16]{2,1,0:T(8,128)(2,1)S(1)} fusion(bf16[2,128,8192]{2,1,0:T(8,128)(2,1)} %hidden_ref.1, bf16[2,16,8192]{2,1,0:T(8,128)(2,1)S(1)} %copy-done), kind=kOutput, calls=%fused_computation.1 | convolution fusion | flops 67112960 | bytes 4726784 | tf_op jit(solution)/shard_map/tbu,tyu->tby/dot_general | solution.py:303
  21.3 0.0 collective-permute-done.1.kv_far
  21.3 0.0 copy-start.6
  21.3 0.7 copy-done.6
  22.0 0.0 collective-permute-done.2.kv_swap
  22.0 0.0 copy-done.4
  22.0 0.0 copy-done.3
  22.0 0.0 copy-done.2
  22.1 0.0 copy-done.8
  22.1 0.0 copy-start.5
  22.1 1.0 copy-done.5
  23.1 0.0 copy-start.7
  23.1 1.0 copy-done.7
  24.1 29.7 %attention_grads.1 = (bf16[2,128,1024]{2,1,0:T(8,128)(2,1)S(1)}, f32[768,256]{1,0:T(8,128)S(1)}, f32[768,256]{1,0:T(8,128)S(1)}, bf16[768,256]{1,0:T(8,128)(2,1)S(1)}, bf16[768,256]{1,0:T(8,128)(2,1)S(1)}) custom-call(s32[3]{0:T(128)S(1)} %pad_add_fusion.where_ref, s32[1,256]{1,0:T(1,128)S(1)} %bitcast.19, bf16[2,128,1024]{2,1,0:T(8,128)(2,1)S(1)} %copy-done.2, ...), custom_call_target="tpu_custom_call" | custom-call | tf_op jit(solution)/shard_map/attention_grads/pallas_call | solution.py:193
  53.8 0.0 copy-start.9
  53.8 0.8 copy-done.9
  54.6 0.0 copy-start.11
  54.6 0.8 copy-done.11
  55.3 0.0 copy-done.1
  55.3 0.0 copy-start.12
  55.3 0.0 copy-start.10
  55.3 3.0 %adapter_grads.1 = bf16[8,9,32,128]{3,2,1,0:T(8,128)(2,1)} custom-call(bf16[2,128,1024]{2,1,0:T(8,128)(2,1)S(1)} %get-tuple-element.9.dquery_ref, bf16[2,128,16]{2,1,0:T(8,128)(2,1)S(1)} %convolution_convert_fusion.low_ref, bf16[2,16,1024]{2,1,0:T(8,128)(2,1)S(1)} %copy-done.8, bf16[2,128,8192]{2,1,0:T(8,128)(2,1)S(1)} %copy-done.1), custom_call_target="tpu_custom_call" | custom-call | tf_op jit(solution)/shard_map/adapter_grads/pallas_call | solution.py:260
  58.3 21.1 %all-to-all-start = ((bf16[8,9,32,128]{3,2,1,0:T(8,128)(2,1)}), bf16[8,9,32,128]{3,2,1,0:T(8,128)(2,1)S(1)}, u32[]{:S(2)}, u32[]{:S(2)}) async-start(bf16[8,9,32,128]{3,2,1,0:T(8,128)(2,1)} %adapter_grads.1), calls=%async_computation | async-start | bytes 1179648 | tf_op jit(solution)/shard_map/all_to_all | solution.py:37
  79.4 0.0 copy-done.12
  79.4 0.1 collective-permute-start.4
  79.5 10.1 %all-to-all-done = bf16[8,9,32,128]{3,2,1,0:T(8,128)(2,1)S(1)} async-done(((bf16[8,9,32,128]{3,2,1,0:T(8,128)(2,1)}), bf16[8,9,32,128]{3,2,1,0:T(8,128)(2,1)S(1)}, u32[]{:S(2)}, u32[]{:S(2)}) %all-to-all-start) | async-done | bytes 589856 | tf_op jit(solution)/shard_map/all_to_all | solution.py:37
  89.6 0.1 convert_reduce_fusion
  89.7 0.7 pad_maximum_fusion
  90.4 10.2 %all-to-all-start.1 = ((f32[8,2,32,128]{3,2,1,0:T(8,128)}), f32[8,2,32,128]{3,2,1,0:T(8,128)S(1)}, u32[]{:S(2)}, u32[]{:S(2)}) async-start(f32[8,2,32,128]{3,2,1,0:T(8,128)} %pad_maximum_fusion), calls=%async_computation.1 | async-start | bytes 524288 | tf_op jit(solution)/shard_map/all_to_all | solution.py:37
  100.6 0.0 copy-done.10
  100.6 3.1 %collective-permute-start.3 = (bf16[768,256]{1,0:T(8,128)(2,1)S(1)}, bf16[768,256]{1,0:T(8,128)(2,1)S(1)}, u32[]{:S(2)}, u32[]{:S(2)}) collective-permute-start(bf16[768,256]{1,0:T(8,128)(2,1)S(1)} %copy-done.10), channel_id=1, source_target_pairs={{4,0},{5,1},{6,2},{7,3},{12,8},{13,9},{14,10},{15,11},{16,4},{17,5... | collective-permute-start | bytes 1179656 | tf_op jit(solution)/shard_map/ppermute | solution.py:33
  103.7 0.0 collective-permute-done.4
  103.7 1.1 add_convert_fusion.1
  104.8 1.3 collective-permute-start.5
  106.1 17.4 %all-to-all-done.1 = f32[8,2,32,128]{3,2,1,0:T(8,128)S(1)} async-done(((f32[8,2,32,128]{3,2,1,0:T(8,128)}), f32[8,2,32,128]{3,2,1,0:T(8,128)S(1)}, u32[]{:S(2)}, u32[]{:S(2)}) %all-to-all-start.1) | async-done | bytes 262176 | tf_op jit(solution)/shard_map/all_to_all | solution.py:37
  123.5 0.6 slice_bitcast_fusion.1
  124.2 0.7 broadcast_in_dim.12
  124.8 3.9 %all-to-all-start.2 = ((f32[8,32,128]{2,1,0:T(8,128)}), f32[8,32,128]{2,1,0:T(8,128)S(1)}, u32[]{:S(2)}, u32[]{:S(2)}) async-start(f32[8,32,128]{2,1,0:T(8,128)} %broadcast_in_dim.12), calls=%async_computation.2 | async-start | bytes 262144 | tf_op jit(solution)/shard_map/all_to_all | solution.py:37
  128.7 0.0 collective-permute-done.3
  128.7 0.0 collective-permute-done.5
  128.7 0.9 add_convert_fusion
  129.6 4.4 %all-to-all-done.2 = f32[8,32,128]{2,1,0:T(8,128)S(1)} async-done(((f32[8,32,128]{2,1,0:T(8,128)}), f32[8,32,128]{2,1,0:T(8,128)S(1)}, u32[]{:S(2)}, u32[]{:S(2)}) %all-to-all-start.2) | async-done | bytes 131104 | tf_op jit(solution)/shard_map/all_to_all | solution.py:37
  134.0 3.5 %all-to-all-start.3 = ((bf16[4,192,256]{2,1,0:T(8,128)(2,1)}), bf16[4,192,256]{2,1,0:T(8,128)(2,1)S(1)}, u32[]{:S(2)}, u32[]{:S(2)}) async-start(bf16[4,192,256]{2,1,0:T(8,128)(2,1)} %bitcast.8), calls=%async_computation.3 | async-start | bytes 786432 | tf_op jit(solution)/shard_map/all_to_all | solution.py:325
  137.4 0.7 copy.19
  138.1 10.5 %all-to-all-done.3 = bf16[4,192,256]{2,1,0:T(8,128)(2,1)S(1)} async-done(((bf16[4,192,256]{2,1,0:T(8,128)(2,1)}), bf16[4,192,256]{2,1,0:T(8,128)(2,1)S(1)}, u32[]{:S(2)}, u32[]{:S(2)}) %all-to-all-start.3) | async-done | bytes 393248 | tf_op jit(solution)/shard_map/all_to_all | solution.py:325
  148.7 0.7 fusion
  (5 shorter events, 0.1 us)
Async XLA Ops:
  0.6 17.2 %copy-start = (bf16[2,16,8192]{2,1,0:T(8,128)(2,1)S(1)}, bf16[2,16,8192]{2,1,0:T(8,128)(2,1)}, u32[]{:S(2)}) copy-start(bf16[2,16,8192]{2,1,0:T(8,128)(2,1)} %param.14) | copy-start | bytes 1572868
  0.6 21.4 %copy-start.3 = (bf16[2,128,1024]{2,1,0:T(8,128)(2,1)S(1)}, bf16[2,128,1024]{2,1,0:T(8,128)(2,1)}, u32[]{:S(2)}) copy-start(bf16[2,128,1024]{2,1,0:T(8,128)(2,1)} %grad_ref.1) | copy-start | bytes 1572868
  0.7 21.4 %copy-start.2 = (bf16[2,128,1024]{2,1,0:T(8,128)(2,1)S(1)}, bf16[2,128,1024]{2,1,0:T(8,128)(2,1)}, u32[]{:S(2)}) copy-start(bf16[2,128,1024]{2,1,0:T(8,128)(2,1)} %base_ref.1) | copy-start | bytes 1572868
  2.7 11.7 %collective-permute-start = (bf16[768,256]{1,0:T(8,128)(2,1)S(1)}, bf16[768,256]{1,0:T(8,128)(2,1)S(1)}, u32[]{:S(2)}, u32[]{:S(2)}) collective-permute-start(bf16[768,256]{1,0:T(8,128)(2,1)S(1)} %constant_dynamic-update-slice_fusion.kv_own), channel_id=1, source_target_pairs={{0,8},{1,9},{2,10},{3,11},{4,12},{5,13},{6,14},{7,15},{8,16},{9,17... | collective-permute-start | bytes 1179656 | tf_op jit(solution)/shard_map/ppermute | solution.py:33
  6.7 14.6 %collective-permute-start.1 = (bf16[768,256]{1,0:T(8,128)(2,1)S(1)}, bf16[768,256]{1,0:T(8,128)(2,1)S(1)}, u32[]{:S(2)}, u32[]{:S(2)}) collective-permute-start(bf16[768,256]{1,0:T(8,128)(2,1)S(1)} %constant_dynamic-update-slice_fusion.kv_own), channel_id=1, source_target_pairs={{0,4},{1,5},{2,6},{3,7},{4,16},{5,17},{6,18},{7,19},{8,12},{9,13},... | collective-permute-start | bytes 1179656 | tf_op jit(solution)/shard_map/ppermute | solution.py:33
  11.9 10.2 %copy-start.8 = (bf16[2,16,1024]{2,1,0:T(8,128)(2,1)S(1)}, bf16[2,16,1024]{2,1,0:T(8,128)(2,1)}, u32[]{:S(2)}) copy-start(bf16[2,16,1024]{2,1,0:T(8,128)(2,1)} %up_ref.3) | copy-start | bytes 196612
  11.9 43.4 %copy-start.1 = (bf16[2,128,8192]{2,1,0:T(8,128)(2,1)S(1)}, bf16[2,128,8192]{2,1,0:T(8,128)(2,1)}, u32[]{:S(2)}) copy-start(bf16[2,128,8192]{2,1,0:T(8,128)(2,1)} %hidden_ref.1) | copy-start | bytes 12582916
  14.4 7.6 %copy-start.4 = (bf16[768,256]{1,0:T(8,128)(2,1)}, bf16[768,256]{1,0:T(8,128)(2,1)S(1)}, u32[]{:S(2)}) copy-start(bf16[768,256]{1,0:T(8,128)(2,1)S(1)} %collective-permute-done.kv_mid) | copy-start | bytes 1179652
  14.4 7.6 %collective-permute-start.2 = (bf16[768,256]{1,0:T(8,128)(2,1)S(1)}, bf16[768,256]{1,0:T(8,128)(2,1)S(1)}, u32[]{:S(2)}, u32[]{:S(2)}) collective-permute-start(bf16[768,256]{1,0:T(8,128)(2,1)S(1)} %collective-permute-done.kv_mid), channel_id=1, source_target_pairs={{0,4},{1,5},{2,6},{3,7},{4,0},{5,1},{6,2},{7,3},{8,12},{9,13},{10,... | collective-permute-start | bytes 1179656 | tf_op jit(solution)/shard_map/ppermute | solution.py:33
  21.3 0.7 copy-start.6
  22.1 1.0 copy-start.5
  23.1 1.0 copy-start.7
  53.8 0.8 copy-start.9
  54.6 0.8 copy-start.11
  55.3 24.1 %copy-start.12 = (bf16[768,256]{1,0:T(8,128)(2,1)S(1)}, bf16[768,256]{1,0:T(8,128)(2,1)}, u32[]{:S(2)}) copy-start(bf16[768,256]{1,0:T(8,128)(2,1)} %copy-done.11) | copy-start | bytes 1179652
  55.3 45.3 %copy-start.10 = (bf16[768,256]{1,0:T(8,128)(2,1)S(1)}, bf16[768,256]{1,0:T(8,128)(2,1)}, u32[]{:S(2)}) copy-start(bf16[768,256]{1,0:T(8,128)(2,1)} %copy-done.9) | copy-start | bytes 1179652
  58.3 31.2 %all-to-all-start = ((bf16[8,9,32,128]{3,2,1,0:T(8,128)(2,1)}), bf16[8,9,32,128]{3,2,1,0:T(8,128)(2,1)S(1)}, u32[]{:S(2)}, u32[]{:S(2)}) async-start(bf16[8,9,32,128]{3,2,1,0:T(8,128)(2,1)} %adapter_grads.1), calls=%async_computation | async-start | bytes 1179648 | tf_op jit(solution)/shard_map/all_to_all | solution.py:37
  79.4 24.3 %collective-permute-start.4 = (bf16[768,256]{1,0:T(8,128)(2,1)S(1)}, bf16[768,256]{1,0:T(8,128)(2,1)}, u32[]{:S(2)}, u32[]{:S(2)}) collective-permute-start(bf16[768,256]{1,0:T(8,128)(2,1)S(1)} %copy-done.12), channel_id=1, source_target_pairs={{0,4},{1,5},{2,6},{3,7},{4,0},{5,1},{6,2},{7,3},{8,12},{9,13},{10,... | collective-permute-start | bytes 1179656 | tf_op jit(solution)/shard_map/ppermute | solution.py:33
  90.4 33.1 %all-to-all-start.1 = ((f32[8,2,32,128]{3,2,1,0:T(8,128)}), f32[8,2,32,128]{3,2,1,0:T(8,128)S(1)}, u32[]{:S(2)}, u32[]{:S(2)}) async-start(f32[8,2,32,128]{3,2,1,0:T(8,128)} %pad_maximum_fusion), calls=%async_computation.1 | async-start | bytes 524288 | tf_op jit(solution)/shard_map/all_to_all | solution.py:37
  100.6 28.1 %collective-permute-start.3 = (bf16[768,256]{1,0:T(8,128)(2,1)S(1)}, bf16[768,256]{1,0:T(8,128)(2,1)S(1)}, u32[]{:S(2)}, u32[]{:S(2)}) collective-permute-start(bf16[768,256]{1,0:T(8,128)(2,1)S(1)} %copy-done.10), channel_id=1, source_target_pairs={{4,0},{5,1},{6,2},{7,3},{12,8},{13,9},{14,10},{15,11},{16,4},{17,5... | collective-permute-start | bytes 1179656 | tf_op jit(solution)/shard_map/ppermute | solution.py:33
  104.8 23.9 %collective-permute-start.5 = (bf16[768,256]{1,0:T(8,128)(2,1)S(1)}, bf16[768,256]{1,0:T(8,128)(2,1)S(1)}, u32[]{:S(2)}, u32[]{:S(2)}) collective-permute-start(bf16[768,256]{1,0:T(8,128)(2,1)S(1)} %add_convert_fusion.1), channel_id=1, source_target_pairs={{8,0},{9,1},{10,2},{11,3},{12,4},{13,5},{14,6},{15,7},{16,8},{17,9... | collective-permute-start | bytes 1179656 | tf_op jit(solution)/shard_map/ppermute | solution.py:33
  124.8 9.2 %all-to-all-start.2 = ((f32[8,32,128]{2,1,0:T(8,128)}), f32[8,32,128]{2,1,0:T(8,128)S(1)}, u32[]{:S(2)}, u32[]{:S(2)}) async-start(f32[8,32,128]{2,1,0:T(8,128)} %broadcast_in_dim.12), calls=%async_computation.2 | async-start | bytes 262144 | tf_op jit(solution)/shard_map/all_to_all | solution.py:37
  134.0 14.6 %all-to-all-start.3 = ((bf16[4,192,256]{2,1,0:T(8,128)(2,1)}), bf16[4,192,256]{2,1,0:T(8,128)(2,1)S(1)}, u32[]{:S(2)}, u32[]{:S(2)}) async-start(bf16[4,192,256]{2,1,0:T(8,128)(2,1)} %bitcast.8), calls=%async_computation.3 | async-start | bytes 786432 | tf_op jit(solution)/shard_map/all_to_all | solution.py:325
where the time goes:
time: 150 us; the launch traced here: 149 us
  starting transfers between devices  54.9 us (37%)
  waiting for transfers between devices  44.1 us (29%)
  Pallas kernels  32.7 us (22%)
  local copies, waits for them, and re-layouts  8.98 us (6%)
  other arithmetic  4.37 us (3%)
  matrix products  3.4 us (2%)
    all_to_all x3, starting transfers between devices, grouped(): lax.all_to_all(value, 'seq', 0, 0, axis_index_groups=groups, tiled=True)  35.1 us
    all_to_all x3, waiting for transfers between devices, grouped(): lax.all_to_all(value, 'seq', 0, 0, axis_index_groups=groups, tiled=True)  31.9 us
    pallas_call x1, Pallas kernels, attention_grads(): pl.pallas_call(body, grid_spec=pltpu.PrefetchScalarGridSpec(num_scalar_pr...  29.7 us
    ppermute x6, starting transfers between devices, moved(): return lax.ppermute(value, both_axes, pairs)  16.3 us
    all_to_all x1, waiting for transfers between devices, local(): lax.all_to_all(prompt, 'adapter', 0, 0, tiled=True).astype(jnp.float32)  10.5 us
    unnamed x27, local copies, waits for them, and re-layouts  5.36 us
    all_to_all x1, starting transfers between devices, local(): lax.all_to_all(prompt, 'adapter', 0, 0, tiled=True).astype(jnp.float32)  3.46 us
    dot_general x1, matrix products, local(): jnp.einsum('tbu,tyu->tby', hidden, adapter_down_weight, preferred_element...  3.4 us
  transfers between devices with their start and end apart: 10, of which 5 were waited for; matrix products, arithmetic and copies ran while one was open for 6% of the time, Pallas kernels for 0%

commit v1 on v0

v1 whole, which is shorter than its diff:
```python
import functools

import jax
import jax.numpy as jnp
from jax import lax
from jax.experimental import pallas as pl
from jax.experimental.pallas import tpu as pltpu
from jax.sharding import PartitionSpec as P

adapter_scale = 2.0
masked_score = -1.0e30
log2_e = 1.4426950408889634
both_axes = ("seq", "adapter")
row_n_seq = 8

NN = ((1,), (0,))
NT = ((1,), (1,))


def dot(a, b, dims):
    return lax.dot_general(a, b, (dims, ((), ())), preferred_element_type=jnp.float32)


def moved(value, by_even, by_odd):
    peers, planes = lax.axis_size("seq"), lax.axis_size("adapter")
    pairs = []
    for s in range(peers):
        t = s + (by_odd if s % 2 else by_even)
        if 0 <= t < peers:
            for a in range(planes):
                b = a if t // row_n_seq == s // row_n_seq else planes - 1 - a
                pairs.append((s * planes + a, t * planes + b))
    return lax.ppermute(value, both_axes, pairs)


def grouped(value, groups):
    return lax.all_to_all(value, "seq", 0, 0, axis_index_groups=groups, tiled=True)


def spans_of(stretch, count=4):
    return [slice(d * stretch, (d + 1) * stretch) for d in range(count)]


def fill_window(window, odd, own, mid, far, swap):
    spans = spans_of(own.shape[0])
    window[spans[0], :] = own[...]
    window[spans[2], :] = mid[...]

    @pl.when(odd)
    def _():
        window[spans[1], :] = far[...]
        window[spans[3], :] = swap[...]

    @pl.when(jnp.logical_not(odd))
    def _():
        window[spans[1], :] = swap[...]
        window[spans[3], :] = far[...]


def fill_plain(window, blocks):
    for span, block in zip(spans_of(blocks[0].shape[0]), blocks):
        window[span, :] = block[...]


def empty_window(acc, odd, factor, own, mid, far, swap):
    spans = spans_of(own.shape[0])

    def put(out, span):
        out[...] = (acc[span, :] * factor).astype(out.dtype)

    put(own, spans[0])
    put(mid, spans[2])

    @pl.when(odd)
    def _():
        put(far, spans[1])
        put(swap, spans[3])

    @pl.when(jnp.logical_not(odd))
    def _():
        put(far, spans[3])
        put(swap, spans[1])


def fold(x, op):
    return op(x.reshape(x.shape[0] // 8, 8, x.shape[1]), axis=0)


def chunks(stretch, chunk):
    for d in range(3):
        for c in range(0, stretch, chunk):
            yield d, c, slice(d * stretch + c, d * stretch + c + chunk)


def prob_kernel(
    where_ref, rel_ref, base_ref, grad_ref, low_ref, up_ref, own, mid, far, swap,
    raised_ref, scale_ref, query_ref, grad_use_ref, own_part, part_1, part_2, part_3,
    window, acc,
    *, stretch, chunk, rows, adapters, head_dim, heads,
):
    head = pl.program_id(0)
    shift = head_dim**-0.5 * log2_e
    wide = rows * adapters
    block = where_ref[0]
    odd = lax.rem(block, 2) == 1

    @pl.when(head == 0)
    def _():
        acc[...] = jnp.zeros_like(acc)
        fill_window(window, odd, own, mid, far, swap)

    line = block * rows + lax.broadcasted_iota(jnp.int32, (rows, head_dim), 0)
    for a in range(adapters):
        at = slice(a * rows, (a + 1) * rows)
        up = dot(low_ref[a], up_ref[a], NN)
        query_ref[at, :] = (base_ref[a].astype(jnp.float32) + adapter_scale * up).astype(
            jnp.bfloat16
        )
        live = line < where_ref[1 + a]
        grad_use_ref[at, :] = jnp.where(live, grad_ref[a].astype(jnp.float32), 0.0).astype(
            jnp.bfloat16
        )
    query = query_ref[...]
    grad = grad_use_ref[...]
    rel = rel_ref[...]
    place = lax.broadcasted_iota(jnp.int32, (chunk, wide), 0)
    bias3 = jnp.where(block >= 3, 0.0, masked_score)

    highs = [None] * 3
    for d, c, at in chunks(stretch, chunk):
        s = dot(window[at, :], query, NT)
        if d == 0:
            far_at = slice(3 * stretch + c, 3 * stretch + c + chunk)
            s = jnp.where(rel >= place + c, s, dot(window[far_at, :], query, NT) + bias3)
        raised_ref[0, at, :] = s
        top = fold(s, jnp.max)
        highs[d] = top if highs[d] is None else jnp.maximum(highs[d], top)
    peak = highs[0]
    for d in (1, 2):
        peak = jnp.maximum(peak, jnp.where(block >= d, highs[d], masked_score))
    peak = jnp.max(peak, axis=0, keepdims=True)
    total = jnp.zeros((8, wide), jnp.float32)
    levels = [peak] + [jnp.where(block >= d, peak, -masked_score) for d in (1, 2)]
    for d, c, at in chunks(stretch, chunk):
        e = jnp.exp2((raised_ref[0, at, :] - levels[d]) * shift)
        raised_ref[0, at, :] = e
        total = total + fold(e, jnp.sum)
    scale = 1.0 / jnp.sum(total, axis=0, keepdims=True)
    scale_ref[0] = scale
    for d, c, at in chunks(stretch, chunk):
        p = raised_ref[0, at, :] * scale
        if d == 0:
            early = rel >= place + c
            zero = jnp.zeros_like(p)
            far_at = slice(3 * stretch + c, 3 * stretch + c + chunk)
            late = jnp.where(early, zero, p).astype(jnp.bfloat16)
            acc[far_at, :] += dot(late, grad, NN)
            p = jnp.where(early, p, zero)
        acc[at, :] += dot(p.astype(jnp.bfloat16), grad, NN)

    @pl.when(head == heads - 1)
    def _():
        for span, out in zip(spans_of(stretch), (own_part, part_1, part_2, part_3)):
            out[...] = acc[span, :].astype(out.dtype)


def dscore_kernel(
    where_ref, rel_ref, raised_ref, scale_ref, query_ref, grad_use_ref,
    own, mid, far, swap, own_v, back_1, back_2, back_3,
    dquery_ref, own_part, mid_part, far_part, swap_part,
    window, window_v, key_t, dprob, dscore_low, acc,
    *, stretch, chunk, rows, adapters, head_dim, heads,
):
    head = pl.program_id(0)
    factor = head_dim**-0.5
    wide = rows * adapters
    odd = lax.rem(where_ref[0], 2) == 1

    @pl.when(head == 0)
    def _():
        acc[...] = jnp.zeros_like(acc)
        fill_window(window, odd, own, mid, far, swap)
        fill_plain(window_v, (own_v, back_1, back_2, back_3))
        for span in spans_of(stretch):
            key_t[:, span] = window[span, :].T

    query = query_ref[...]
    grad = grad_use_ref[...]
    rel = rel_ref[...]
    scale = scale_ref[0]
    place = lax.broadcasted_iota(jnp.int32, (chunk, wide), 0)
    delta = jnp.zeros((8, wide), jnp.float32)
    for d, c, at in chunks(stretch, chunk):
        dp = dot(window_v[at, :], grad, NT)
        if d == 0:
            far_at = slice(3 * stretch + c, 3 * stretch + c + chunk)
            dp = jnp.where(rel >= place + c, dp, dot(window_v[far_at, :], grad, NT))
        dprob[at, :] = dp
        delta = delta + fold(raised_ref[0, at, :] * dp, jnp.sum)
    delta = jnp.sum(delta, axis=0, keepdims=True) * scale
    for d, c, at in chunks(stretch, chunk):
        ds = (raised_ref[0, at, :] * scale) * (dprob[at, :] - delta)
        if d == 0:
            early = rel >= place + c
            zero = jnp.zeros_like(ds)
            far_at = slice(3 * stretch + c, 3 * stretch + c + chunk)
            late = jnp.where(early, zero, ds).astype(jnp.bfloat16)
            dscore_low[far_at, :] = late
            acc[far_at, :] += dot(late, query, NN)
            ds = jnp.where(early, ds, zero)
        low = ds.astype(jnp.bfloat16)
        dscore_low[at, :] = low
        acc[at, :] += dot(low, query, NN)
    dquery = (dot(key_t[...], dscore_low[...], NN).T * factor).astype(jnp.bfloat16)
    for a in range(adapters):
        dquery_ref[a] = dquery[a * rows : (a + 1) * rows]

    @pl.when(head == heads - 1)
    def _():
        empty_window(acc, odd, factor, own_part, mid_part, far_part, swap_part)


def sizes_of(base, own):
    adapters, rows, features = base.shape
    stretch, head_dim = own.shape
    return dict(
        stretch=stretch,
        chunk=256,
        rows=rows,
        adapters=adapters,
        head_dim=head_dim,
        heads=features // head_dim,
    )


def whole(*shape):
    return pl.BlockSpec(shape, lambda h, w: (0,) * len(shape))


def parts_of(stretch, head_dim, wide_n):
    return [
        jax.ShapeDtypeStruct((stretch, head_dim), jnp.float32 if d < wide_n else jnp.bfloat16)
        for d in range(4)
    ]


def prob_pass(where, rel, base, grad, low, up, own, mid, far, swap):
    sizes = sizes_of(base, own)
    adapters, rows, heads = sizes["adapters"], sizes["rows"], sizes["heads"]
    stretch, head_dim = own.shape
    rank, wide = low.shape[2], rows * adapters
    per_head = pl.BlockSpec((adapters, rows, head_dim), lambda h, w: (0, 0, h))
    flat = pl.BlockSpec((wide, head_dim), lambda h, w: (0, h))
    return pl.pallas_call(
        functools.partial(prob_kernel, **sizes),
        grid_spec=pltpu.PrefetchScalarGridSpec(
            num_scalar_prefetch=1,
            grid=(heads,),
            in_specs=[
                whole(1, wide),
                per_head,
                per_head,
                whole(adapters, rows, rank),
                pl.BlockSpec((adapters, rank, head_dim), lambda h, w: (0, 0, h)),
            ]
            + [whole(stretch, head_dim)] * 4,
            out_specs=[
                pl.BlockSpec((1, 3 * stretch, wide), lambda h, w: (h, 0, 0)),
                pl.BlockSpec((1, 1, wide), lambda h, w: (h, 0, 0)),
                flat,
                flat,
            ]
            + [whole(stretch, head_dim)] * 4,
            scratch_shapes=[
                pltpu.VMEM((4 * stretch, head_dim), jnp.bfloat16),
                pltpu.VMEM((4 * stretch, head_dim), jnp.float32),
            ],
        ),
        out_shape=[
            jax.ShapeDtypeStruct((heads, 3 * stretch, wide), jnp.float32),
            jax.ShapeDtypeStruct((heads, 1, wide), jnp.float32),
            jax.ShapeDtypeStruct((wide, heads * head_dim), jnp.bfloat16),
            jax.ShapeDtypeStruct((wide, heads * head_dim), jnp.bfloat16),
        ]
        + parts_of(stretch, head_dim, 1),
        compiler_params=pltpu.CompilerParams(
            dimension_semantics=("arbitrary",), vmem_limit_bytes=32 * 1024 * 1024
        ),
        name="prob_pass",
    )(where, rel, base, grad, low, up, own, mid, far, swap)


def dscore_pass(where, rel, base, raised, scale, query, grad_use, key_blocks, value_blocks):
    sizes = sizes_of(base, key_blocks[0])
    adapters, rows, heads = sizes["adapters"], sizes["rows"], sizes["heads"]
    stretch, head_dim = key_blocks[0].shape
    wide = rows * adapters
    flat = pl.BlockSpec((wide, head_dim), lambda h, w: (0, h))
    return pl.pallas_call(
        functools.partial(dscore_kernel, **sizes),
        grid_spec=pltpu.PrefetchScalarGridSpec(
            num_scalar_prefetch=1,
            grid=(heads,),
            in_specs=[
                whole(1, wide),
                pl.BlockSpec((1, 3 * stretch, wide), lambda h, w: (h, 0, 0)),
                pl.BlockSpec((1, 1, wide), lambda h, w: (h, 0, 0)),
                flat,
                flat,
            ]
            + [whole(stretch, head_dim)] * 8,
            out_specs=[pl.BlockSpec((adapters, rows, head_dim), lambda h, w: (0, 0, h))]
            + [whole(stretch, head_dim)] * 4,
            scratch_shapes=[
                pltpu.VMEM((4 * stretch, head_dim), jnp.bfloat16),
                pltpu.VMEM((4 * stretch, head_dim), jnp.bfloat16),
                pltpu.VMEM((head_dim, 4 * stretch), jnp.bfloat16),
                pltpu.VMEM((3 * stretch, wide), jnp.float32),
                pltpu.VMEM((4 * stretch, wide), jnp.bfloat16),
                pltpu.VMEM((4 * stretch, head_dim), jnp.float32),
            ],
        ),
        out_shape=[jax.ShapeDtypeStruct(base.shape, jnp.bfloat16)] + parts_of(stretch, head_dim, 2),
        compiler_params=pltpu.CompilerParams(
            dimension_semantics=("arbitrary",), vmem_limit_bytes=32 * 1024 * 1024
        ),
        name="dscore_pass",
    )(where, rel, raised, scale, query, grad_use, *key_blocks, *value_blocks)


def adapter_kernel(
    where_ref, dquery_ref, low_ref, up_ref, hidden_ref, keep_ref, send_ref, small,
    *, adapters, rank, lanes, chips,
):
    step = pl.program_id(0)
    outer = pl.num_programs(0)
    odd = lax.rem(where_ref[0], 2)

    def put(core, place, at, value):
        @pl.when(odd == core)
        def _():
            keep_ref[place, at, :] = value

        @pl.when(odd != core)
        def _():
            send_ref[place, at, :] = value.astype(send_ref.dtype)

    @pl.when(step == 0)
    def _():
        for a in range(adapters):
            at = slice(a * rank, (a + 1) * rank)
            small[at, :] = dot(up_ref[a], dquery_ref[a], NT).astype(jnp.bfloat16)
            low_t = low_ref[a].astype(jnp.float32).T.astype(jnp.bfloat16)
            piece = adapter_scale * dot(low_t, dquery_ref[a], NN)
            for i in range(2 * chips):
                put(i // chips, chips * outer + i % chips, at, piece[:, i * lanes : (i + 1) * lanes])

    for a in range(adapters):
        at = slice(a * rank, (a + 1) * rank)
        piece = adapter_scale * dot(small[at, :], hidden_ref[a], NN)
        for i in range(2 * chips):
            put(i % 2, (i // 2) * outer + step, at, piece[:, i * lanes : (i + 1) * lanes])


def adapter_grads(where, dquery, low, up, hidden, chips, outer):
    adapters, rows, features = dquery.shape
    rank = low.shape[2]
    width = hidden.shape[2]
    lanes = width // (2 * chips * outer)
    shape = ((outer + 1) * chips, adapters * rank, lanes)
    return pl.pallas_call(
        functools.partial(adapter_kernel, adapters=adapters, rank=rank, lanes=lanes, chips=chips),
        grid_spec=pltpu.PrefetchScalarGridSpec(
            num_scalar_prefetch=1,
            grid=(outer,),
            in_specs=[
                whole(adapters, rows, features),
                whole(adapters, rows, rank),
                whole(adapters, rank, features),
                pl.BlockSpec((adapters, rows, 2 * chips * lanes), lambda g, w: (0, 0, g)),
            ],
            out_specs=[whole(*shape), whole(*shape)],
            scratch_shapes=[pltpu.VMEM((adapters * rank, rows), jnp.bfloat16)],
        ),
        out_shape=[
            jax.ShapeDtypeStruct(shape, jnp.float32),
            jax.ShapeDtypeStruct(shape, jnp.bfloat16),
        ],
        compiler_params=pltpu.CompilerParams(
            dimension_semantics=("arbitrary",), vmem_limit_bytes=24 * 1024 * 1024
        ),
        name="adapter_grads",
    )(where, dquery, low, up, hidden)


def local(
    hidden,
    response_base_queries,
    attention_output_gradient,
    keys,
    values,
    adapter_down_weight,
    adapter_up_weight,
    lengths,
    offsets,
):
    adapt_n, row_n, feature_n = response_base_queries.shape
    rank = adapter_down_weight.shape[1]
    stretch_n, head_dim = keys.shape
    seq_index = lax.axis_index("seq")
    odd = seq_index % 2 == 1
    planes = lax.axis_size("adapter")
    chips = row_n_seq // 2
    outer = lax.axis_size("seq") // row_n_seq

    mid_k, far_k = moved(keys, 2, 2), moved(keys, 1, 3)
    value_blocks = [values] + [moved(values, d, d) for d in (1, 2, 3)]
    low = jnp.einsum(
        "tbu,tyu->tby", hidden, adapter_down_weight, preferred_element_type=jnp.float32
    ).astype(jnp.bfloat16)
    where = jnp.concatenate([seq_index[None].astype(jnp.int32), lengths])
    rel = (offsets - seq_index * stretch_n).reshape(1, adapt_n * row_n)
    mid_k, low, where, rel = lax.optimization_barrier((mid_k, low, where, rel))
    swap_k = moved(mid_k, 1, -1)
    key_blocks = (keys, mid_k, far_k, swap_k)
    raised, scale, query, grad_use, *value_parts = prob_pass(
        where,
        rel,
        response_base_queries,
        attention_output_gradient,
        low,
        adapter_up_weight,
        *key_blocks,
    )
    value_backs = [moved(part, -d, -d) for d, part in enumerate(value_parts) if d]
    dquery, own_dk, mid_dk, far_dk, swap_dk = dscore_pass(
        where,
        rel,
        response_base_queries,
        raised,
        scale,
        query,
        grad_use,
        key_blocks,
        value_blocks,
    )
    keep, send = adapter_grads(where, dquery, low, adapter_up_weight, hidden, chips, outer)
    far_back = moved(far_dk, -3, -1)
    swap_back = moved(swap_dk, 1, -1)
    swap_back, _ = lax.optimization_barrier((swap_back, send))
    mid_dk = (mid_dk + swap_back.astype(jnp.float32)).astype(jnp.bfloat16)

    n_down = chips * outer
    lanes = keep.shape[2]
    at_core = keep + moved(send, 1, -1).astype(jnp.float32)
    at_core = at_core.astype(jnp.bfloat16)
    up_copies = jnp.broadcast_to(at_core[None, n_down:], (chips, chips) + at_core.shape[1:])
    at_core = jnp.concatenate(
        [at_core[:n_down].reshape(chips, outer, adapt_n * rank, lanes), up_copies], axis=1
    )
    at_core, _ = lax.optimization_barrier((at_core, mid_dk))
    mid_back = moved(mid_dk, -2, -2)
    along_x = [[(g * chips + x) * 2 + c for x in range(chips)] for g in range(outer) for c in range(2)]
    at_chip = grouped(at_core, along_x).astype(jnp.float32).sum(0).astype(jnp.bfloat16)
    up_copies = jnp.broadcast_to(at_chip[None, outer:], (outer, chips) + at_chip.shape[1:])
    at_chip = jnp.concatenate([at_chip[:outer, None], up_copies], axis=1)
    mid_back, far_back, value_backs, _ = lax.optimization_barrier(
        (mid_back, far_back, value_backs, at_chip)
    )
    across = [[g * row_n_seq + i for g in range(outer)] for i in range(row_n_seq)]
    summed = grouped(at_chip, across).astype(jnp.float32).sum(0)

    key_total = own_dk + far_back.astype(jnp.float32) + mid_back.astype(jnp.float32)
    value_total = value_parts[0] + sum(back.astype(jnp.float32) for back in value_backs)
    prompt = jnp.stack([key_total, value_total]).astype(jnp.bfloat16)
    prompt = prompt.reshape(2, planes, stretch_n // planes, head_dim)
    prompt = lax.all_to_all(prompt, "adapter", 1, 1, tiled=True).astype(jnp.float32).sum(1)

    down = summed[0].reshape(adapt_n, rank, lanes)
    up_mine = summed[1:]
    up_other = moved(up_mine, 1, -1)
    up_blocks = jnp.concatenate(
        [jnp.where(odd, up_other, up_mine), jnp.where(odd, up_mine, up_other)], axis=0
    )
    up_blocks = up_blocks.reshape(2 * chips, adapt_n, rank, lanes).transpose(1, 2, 0, 3)
    return (down, up_blocks.reshape(adapt_n, rank, feature_n), prompt[0], prompt[1])


def solution(mesh):
    return jax.shard_map(
        local,
        mesh=mesh,
        in_specs=(
            P("adapter", "seq", None),
            P("adapter", "seq", None),
            P("adapter", "seq", None),
            P("seq", None),
            P("seq", None),
            P("adapter", None, None),
            P("adapter", None, None),
            P("adapter"),
            P("adapter", "seq"),
        ),
        out_specs=(
            P("adapter", None, "seq"),
            P("adapter", None, None),
            P(("seq", "adapter"), None),
            P(("seq", "adapter"), None),
        ),
        check_vma=False,
    )
```

time: 150 us -> 153 us (1.020)
  the two profiles are of different devices: /device:TPU:1 before, /device:TPU:22 now
where the time goes in v1:
time: 153 us; the launch traced here: 152 us
  starting transfers between devices  55.2 us (36%)
  Pallas kernels  40 us (26%)
  waiting for transfers between devices  38.8 us (25%)
  local copies, waits for them, and re-layouts  8.54 us (6%)
  other arithmetic  5.15 us (3%)
  matrix products  3.4 us (2%)
    ppermute x14, starting transfers between devices, moved(): return lax.ppermute(value, both_axes, pairs)  36.3 us
    ppermute x14, waiting for transfers between devices, moved(): return lax.ppermute(value, both_axes, pairs)  30.7 us
    pallas_call x1, Pallas kernels, dscore_pass(): pl.pallas_call(functools.partial(dscore_kernel, **sizes), grid_spec=pltpu...  20.6 us
    pallas_call x1, Pallas kernels, prob_pass(): pl.pallas_call(functools.partial(prob_kernel, **sizes), grid_spec=pltpu.P...  15.4 us
    all_to_all x2, starting transfers between devices, grouped(): lax.all_to_all(value, 'seq', 0, 0, axis_index_groups=groups, tiled=True)  15.4 us
    all_to_all x1, waiting for transfers between devices, local(): lax.all_to_all(prompt, 'adapter', 1, 1, tiled=True).astype(jnp.float32)  8.16 us
    unnamed x18, local copies, waits for them, and re-layouts  6.48 us
    pallas_call x1, Pallas kernels, adapter_grads(): pl.pallas_call(functools.partial(adapter_kernel, adapters=adapters, rank=...  3.98 us
  transfers between devices with their start and end apart: 17, of which 5 were waited for; matrix products, arithmetic and copies ran while one was open for 6% of the time, Pallas kernels for 13%

profile of v1, /device:TPU:22, one launch (start us, length us, event | category | flops | bytes accessed | tf_op | source)
XLA Modules:
  0.0 152.1 jit_solution(10315534339801003581)
XLA Ops:
  0.6 0.0 copy-start
  0.6 0.0 copy-start.3
  0.7 0.0 copy-start.8
  0.7 0.0 copy-start.7
  0.7 0.0 copy-start.6
  0.7 0.0 copy-start.5
  0.7 0.0 copy-start.4
  0.7 2.1 %collective-permute-start.1 = (bf16[768,128]{1,0:T(8,128)(2,1)}, bf16[768,128]{1,0:T(8,128)(2,1)S(1)}, u32[]{:S(2)}, u32[]{:S(2)}) collective-permute-start(bf16[768,128]{1,0:T(8,128)(2,1)} %own.3), channel_id=1, source_target_pairs={{0,4},{1,5},{2,6},{3,7},{4,16},{5,17},{6,18},{7,19},{8,12},{9,13},... | collective-permute-start | bytes 589832 | tf_op jit(solution)/shard_map/ppermute | solution.py:33
  2.8 7.7 %collective-permute-start = (bf16[768,128]{1,0:T(8,128)(2,1)}, bf16[768,128]{1,0:T(8,128)(2,1)S(1)}, u32[]{:S(2)}, u32[]{:S(2)}) collective-permute-start(bf16[768,128]{1,0:T(8,128)(2,1)} %own.3), channel_id=1, source_target_pairs={{0,8},{1,9},{2,10},{3,11},{4,12},{5,13},{6,14},{7,15},{8,16},{9,17... | collective-permute-start | bytes 589832 | tf_op jit(solution)/shard_map/ppermute | solution.py:33
  10.5 0.7 pad_add_fusion.where_ref
  11.2 0.0 copy-done
  11.2 3.4 %convolution_convert_fusion.low_ref = bf16[2,128,16]{2,1,0:T(8,128)(2,1)S(1)} fusion(bf16[2,128,8192]{2,1,0:T(8,128)(2,1)} %hidden_ref.1, bf16[2,16,8192]{2,1,0:T(8,128)(2,1)S(1)} %copy-done), kind=kOutput, calls=%fused_computation | convolution fusion | flops 67112960 | bytes 4726784 | tf_op jit(solution)/shard_map/tbu,tyu->tby/dot_general | solution.py:418
  14.6 7.7 %collective-permute-done.mid = bf16[768,128]{1,0:T(8,128)(2,1)S(1)} collective-permute-done((bf16[768,128]{1,0:T(8,128)(2,1)}, bf16[768,128]{1,0:T(8,128)(2,1)S(1)}, u32[]{:S(2)}, u32[]{:S(2)}) %collective-permute-start) | collective-permute-done | bytes 196640 | tf_op jit(solution)/shard_map/ppermute | solution.py:33
  22.3 0.7 collective-permute-start.2
  23.0 0.0 copy-done.7
  23.0 7.3 %collective-permute-start.4 = (bf16[768,128]{1,0:T(8,128)(2,1)S(1)}, bf16[768,128]{1,0:T(8,128)(2,1)S(1)}, u32[]{:S(2)}, u32[]{:S(2)}) collective-permute-start(bf16[768,128]{1,0:T(8,128)(2,1)S(1)} %copy-done.7), channel_id=1, source_target_pairs={{0,8},{1,9},{2,10},{3,11},{4,12},{5,13},{6,14},{7,15},{8,16},{9,17... | collective-permute-start | bytes 589832 | tf_op jit(solution)/shard_map/ppermute | solution.py:33
  30.3 1.9 %collective-permute-start.3 = (bf16[768,128]{1,0:T(8,128)(2,1)S(1)}, bf16[768,128]{1,0:T(8,128)(2,1)S(1)}, u32[]{:S(2)}, u32[]{:S(2)}) collective-permute-start(bf16[768,128]{1,0:T(8,128)(2,1)S(1)} %copy-done.7), channel_id=1, source_target_pairs={{0,4},{1,5},{2,6},{3,7},{4,8},{5,9},{6,10},{7,11},{8,12},{9,13},{1... | collective-permute-start | bytes 589832 | tf_op jit(solution)/shard_map/ppermute | solution.py:33
  32.2 1.9 %collective-permute-start.5 = (bf16[768,128]{1,0:T(8,128)(2,1)S(1)}, bf16[768,128]{1,0:T(8,128)(2,1)S(1)}, u32[]{:S(2)}, u32[]{:S(2)}) collective-permute-start(bf16[768,128]{1,0:T(8,128)(2,1)S(1)} %copy-done.7), channel_id=1, source_target_pairs={{0,12},{1,13},{2,14},{3,15},{4,16},{5,17},{6,18},{7,19},{8,20},{9,... | collective-permute-start | bytes 589832 | tf_op jit(solution)/shard_map/ppermute | solution.py:33
  34.2 0.0 collective-permute-done.1.far
  34.2 0.0 collective-permute-done.2.swap
  34.2 0.0 copy-done.3
  34.2 0.0 copy-done.6
  34.2 0.0 copy-done.5
  34.2 0.0 copy-done.4
  34.2 15.4 %prob_pass.1 = (f32[8,2304,256]{2,1,0:T(8,128)S(1)}, f32[8,1,256]{2,1,0:T(1,128)S(1)}, bf16[256,1024]{1,0:T(8,128)(2,1)S(1)}, bf16[256,1024]{1,0:T(8,128)(2,1)S(...) custom-call(s32[3]{0:T(128)S(1)} %pad_add_fusion.where_ref, ...), custom_call_target="tpu_custom_call" | custom-call | tf_op jit(solution)/shard_map/prob_pass/pallas_call | solution.py:254
  49.7 6.4 %copy-done.1 = f32[8,2304,256]{2,1,0:T(8,128)} copy-done((f32[8,2304,256]{2,1,0:T(8,128)}, f32[8,2304,256]{2,1,0:T(8,128)S(1)}, u32[]{:S(2)}) %copy-start.1) | copy-done | bytes 18874392
  56.1 0.0 collective-permute-done.4.back_2
  56.1 0.0 collective-permute-done.3.back_1
  56.1 0.0 collective-permute-done.5.back_3
  56.1 0.0 copy-start.2
  56.1 20.6 %dscore_pass.1 = (bf16[2,128,1024]{2,1,0:T(8,128)(2,1)S(1)}, f32[768,128]{1,0:T(8,128)S(1)}, f32[768,128]{1,0:T(8,128)S(1)}, bf16[768,128]{1,0:T(8,128)(2,1)S(1)}, bf16[768,128]{1,0:T(8,128)(2,1)S(1)}) custom-call(s32[3]{0:T(128)S(1)} %pad_add_fusion.where_ref, s32[1,256]{1,0:T(1,128)S(1)} %bitcast.26, f32[8,2304,256]{2,1,0:T(8,128)} %copy-done.1, ...), custom_call_target="tpu_custom_call" | custom-call | tf_op jit(solution)/shard_map/dscore_pass/pallas_call | solution.py:299
  76.7 0.2 collective-permute-start.7
  77.0 4.0 %adapter_grads.1 = (f32[36,32,128]{2,1,0:T(8,128)S(1)}, bf16[36,32,128]{2,1,0:T(8,128)(2,1)S(1)}) custom-call(s32[3]{0:T(128)S(1)} %pad_add_fusion.where_ref, bf16[2,128,1024]{2,1,0:T(8,128)(2,1)S(1)} %get-tuple-element.38.dquery_ref, bf16[2,128,16]{2,1,0:T(8,128)(2,1)S(1)} %convolution_convert_fusion.low_ref, bf16[2,16,1024]{2,1,0:T(8,128)(2,1)S(1)} %copy-done.6, ...), custom_call_target="tpu_custom_call" | custom-call | tf_op jit(solution)/shard_map/adapter_grads/pallas_call | solution.py:371
  80.9 0.5 collective-permute-start.6
  81.4 0.0 collective-permute-done.7
  81.4 0.7 add_convert_fusion.3
  82.1 0.5 collective-permute-done.6
  82.6 0.1 add_convert_fusion
  82.8 0.8 pad_maximum_fusion
  83.6 5.9 %all-to-all-start = ((bf16[4,12,32,128]{3,2,1,0:T(8,128)(2,1)}), bf16[4,12,32,128]{3,2,1,0:T(8,128)(2,1)S(1)}, u32[]{:S(2)}, u32[]{:S(2)}) async-start(bf16[4,12,32,128]{3,2,1,0:T(8,128)(2,1)} %pad_maximum_fusion), calls=%async_computation | async-start | bytes 786432 | tf_op jit(solution)/shard_map/all_to_all | solution.py:37
  89.5 3.2 %collective-permute-start.10 = (bf16[768,128]{1,0:T(8,128)(2,1)S(1)}, bf16[768,128]{1,0:T(8,128)(2,1)S(1)}, u32[]{:S(2)}, u32[]{:S(2)}) collective-permute-start(bf16[768,128]{1,0:T(8,128)(2,1)S(1)} %get-tuple-element.46), channel_id=1, source_target_pairs={{4,0},{5,1},{6,2},{7,3},{12,8},{13,9},{14,10},{15,11},{16,4},{17,5... | collective-permute-start | bytes 589832 | tf_op jit(solution)/shard_map/ppermute | solution.py:33
  92.7 1.9 %collective-permute-start.11 = (bf16[768,128]{1,0:T(8,128)(2,1)S(1)}, bf16[768,128]{1,0:T(8,128)(2,1)S(1)}, u32[]{:S(2)}, u32[]{:S(2)}) collective-permute-start(bf16[768,128]{1,0:T(8,128)(2,1)S(1)} %get-tuple-element.47), channel_id=1, source_target_pairs={{4,0},{5,1},{6,2},{7,3},{8,4},{9,5},{10,6},{11,7},{12,8},{13,9},{1... | collective-permute-start | bytes 589832 | tf_op jit(solution)/shard_map/ppermute | solution.py:33
  94.6 2.1 %collective-permute-start.12 = (bf16[768,128]{1,0:T(8,128)(2,1)S(1)}, bf16[768,128]{1,0:T(8,128)(2,1)S(1)}, u32[]{:S(2)}, u32[]{:S(2)}) collective-permute-start(bf16[768,128]{1,0:T(8,128)(2,1)S(1)} %get-tuple-element.48), channel_id=1, source_target_pairs={{8,0},{9,1},{10,2},{11,3},{12,4},{13,5},{14,6},{15,7},{16,8},{17,9... | collective-permute-start | bytes 589832 | tf_op jit(solution)/shard_map/ppermute | solution.py:33
  96.8 3.6 %collective-permute-start.13 = (bf16[768,128]{1,0:T(8,128)(2,1)S(1)}, bf16[768,128]{1,0:T(8,128)(2,1)S(1)}, u32[]{:S(2)}, u32[]{:S(2)}) collective-permute-start(bf16[768,128]{1,0:T(8,128)(2,1)S(1)} %get-tuple-element.49), channel_id=1, source_target_pairs={{12,0},{13,1},{14,2},{15,3},{16,4},{17,5},{18,6},{19,7},{20,8},{21... | collective-permute-start | bytes 589832 | tf_op jit(solution)/shard_map/ppermute | solution.py:33
  100.4 3.1 %collective-permute-start.9 = (bf16[768,128]{1,0:T(8,128)(2,1)}, bf16[768,128]{1,0:T(8,128)(2,1)}, u32[]{:S(2)}, u32[]{:S(2)}) collective-permute-start(bf16[768,128]{1,0:T(8,128)(2,1)} %add_convert_fusion.3), channel_id=1, source_target_pairs={{8,0},{9,1},{10,2},{11,3},{12,4},{13,5},{14,6},{15,7},{16,8},{17,9... | collective-permute-start | bytes 589832 | tf_op jit(solution)/shard_map/ppermute | solution.py:33
  103.6 0.0 all-to-all-done
  103.6 0.1 reduce_sum.30
  103.7 0.8 pad_maximum_fusion.2
  104.5 9.5 %all-to-all-start.1 = ((bf16[8,5,32,128]{3,2,1,0:T(8,128)(2,1)}), bf16[8,5,32,128]{3,2,1,0:T(8,128)(2,1)S(1)}, u32[]{:S(2)}, u32[]{:S(2)}) async-start(bf16[8,5,32,128]{3,2,1,0:T(8,128)(2,1)} %pad_maximum_fusion.2), calls=%async_computation.1 | async-start | bytes 655360 | tf_op jit(solution)/shard_map/all_to_all | solution.py:37
  114.0 0.0 collective-permute-done.10
  114.0 0.0 collective-permute-done.11
  114.0 17.2 %collective-permute-done.12 = bf16[768,128]{1,0:T(8,128)(2,1)S(1)} collective-permute-done((bf16[768,128]{1,0:T(8,128)(2,1)S(1)}, bf16[768,128]{1,0:T(8,128)(2,1)S(1)}, u32[]{:S(2)}, u32[]{:S(2)}) %collective-permute-start.12) | collective-permute-done | bytes 196640 | tf_op jit(solution)/shard_map/ppermute | solution.py:33
  131.2 0.0 collective-permute-done.13
  131.2 5.3 %collective-permute-done.9 = bf16[768,128]{1,0:T(8,128)(2,1)} collective-permute-done((bf16[768,128]{1,0:T(8,128)(2,1)}, bf16[768,128]{1,0:T(8,128)(2,1)}, u32[]{:S(2)}, u32[]{:S(2)}) %collective-permute-start.9) | collective-permute-done | bytes 196640 | tf_op jit(solution)/shard_map/ppermute | solution.py:33
  136.5 1.1 add_convert_fusion.1
  137.6 0.8 pad_maximum_fusion.1
  138.3 0.0 all-to-all-done.1
  138.3 3.5 %all-to-all-start.2 = ((bf16[2,4,192,128]{3,2,0,1:T(8,128)(2,1)}), bf16[2,4,192,128]{3,2,0,1:T(8,128)(2,1)S(1)}, u32[]{:S(2)}, u32[]{:S(2)}) async-start(bf16[2,4,192,128]{3,2,0,1:T(8,128)(2,1)} %pad_maximum_fusion.1), calls=%async_computation.2 | async-start | bytes 786432 | tf_op jit(solution)/shard_map/all_to_all | solution.py:477
  141.9 0.6 slice.36
  142.5 0.0 collective-permute-start.8
  142.5 8.2 %all-to-all-done.2 = bf16[2,4,192,128]{3,2,0,1:T(8,128)(2,1)S(1)} async-done(((bf16[2,4,192,128]{3,2,0,1:T(8,128)(2,1)}), bf16[2,4,192,128]{3,2,0,1:T(8,128)(2,1)S(1)}, u32[]{:S(2)}, u32[]{:S(2)}) %all-to-all-start.2) | async-done | bytes 393248 | tf_op jit(solution)/shard_map/all_to_all | solution.py:477
  150.7 0.7 slice_bitcast_fusion
  151.4 0.0 collective-permute-done.8
  151.4 0.7 copy.28
  (15 shorter events, 0.2 us)
Async XLA Ops:
  0.6 10.6 %copy-start = (bf16[2,16,8192]{2,1,0:T(8,128)(2,1)S(1)}, bf16[2,16,8192]{2,1,0:T(8,128)(2,1)}, u32[]{:S(2)}) copy-start(bf16[2,16,8192]{2,1,0:T(8,128)(2,1)} %param.14) | copy-start | bytes 1572868
  0.6 33.6 %copy-start.3 = (bf16[768,128]{1,0:T(8,128)(2,1)S(1)}, bf16[768,128]{1,0:T(8,128)(2,1)}, u32[]{:S(2)}) copy-start(bf16[768,128]{1,0:T(8,128)(2,1)} %own.3) | copy-start | bytes 589828
  0.7 13.9 %copy-start.8 = (s32[2,128]{1,0:T(2,128)S(1)}, s32[2,128]{1,0:T(2,128)}, u32[]{:S(2)}) copy-start(s32[2,128]{1,0:T(2,128)} %param.17) | copy-start | bytes 3076
  0.7 22.3 %copy-start.7 = (bf16[768,128]{1,0:T(8,128)(2,1)S(1)}, bf16[768,128]{1,0:T(8,128)(2,1)}, u32[]{:S(2)}) copy-start(bf16[768,128]{1,0:T(8,128)(2,1)} %own_v.1) | copy-start | bytes 589828
  0.7 33.5 %copy-start.6 = (bf16[2,16,1024]{2,1,0:T(8,128)(2,1)S(1)}, bf16[2,16,1024]{2,1,0:T(8,128)(2,1)}, u32[]{:S(2)}) copy-start(bf16[2,16,1024]{2,1,0:T(8,128)(2,1)} %up_ref.3) | copy-start | bytes 196612
  0.7 33.5 %copy-start.5 = (bf16[2,128,1024]{2,1,0:T(8,128)(2,1)S(1)}, bf16[2,128,1024]{2,1,0:T(8,128)(2,1)}, u32[]{:S(2)}) copy-start(bf16[2,128,1024]{2,1,0:T(8,128)(2,1)} %grad_ref.1) | copy-start | bytes 1572868
  0.7 33.5 %copy-start.4 = (bf16[2,128,1024]{2,1,0:T(8,128)(2,1)S(1)}, bf16[2,128,1024]{2,1,0:T(8,128)(2,1)}, u32[]{:S(2)}) copy-start(bf16[2,128,1024]{2,1,0:T(8,128)(2,1)} %base_ref.1) | copy-start | bytes 1572868
  0.7 33.5 %collective-permute-start.1 = (bf16[768,128]{1,0:T(8,128)(2,1)}, bf16[768,128]{1,0:T(8,128)(2,1)S(1)}, u32[]{:S(2)}, u32[]{:S(2)}) collective-permute-start(bf16[768,128]{1,0:T(8,128)(2,1)} %own.3), channel_id=1, source_target_pairs={{0,4},{1,5},{2,6},{3,7},{4,16},{5,17},{6,18},{7,19},{8,12},{9,13},... | collective-permute-start | bytes 589832 | tf_op jit(solution)/shard_map/ppermute | solution.py:33
  2.8 19.5 %collective-permute-start = (bf16[768,128]{1,0:T(8,128)(2,1)}, bf16[768,128]{1,0:T(8,128)(2,1)S(1)}, u32[]{:S(2)}, u32[]{:S(2)}) collective-permute-start(bf16[768,128]{1,0:T(8,128)(2,1)} %own.3), channel_id=1, source_target_pairs={{0,8},{1,9},{2,10},{3,11},{4,12},{5,13},{6,14},{7,15},{8,16},{9,17... | collective-permute-start | bytes 589832 | tf_op jit(solution)/shard_map/ppermute | solution.py:33
  22.3 11.9 %collective-permute-start.2 = (bf16[768,128]{1,0:T(8,128)(2,1)S(1)}, bf16[768,128]{1,0:T(8,128)(2,1)S(1)}, u32[]{:S(2)}, u32[]{:S(2)}) collective-permute-start(bf16[768,128]{1,0:T(8,128)(2,1)S(1)} %collective-permute-done.mid), channel_id=1, source_target_pairs={{0,4},{1,5},{2,6},{3,7},{4,0},{5,1},{6,2},{7,3},{8,12},{9,13},{10,... | collective-permute-start | bytes 589832 | tf_op jit(solution)/shard_map/ppermute | solution.py:33
  23.0 33.1 %collective-permute-start.4 = (bf16[768,128]{1,0:T(8,128)(2,1)S(1)}, bf16[768,128]{1,0:T(8,128)(2,1)S(1)}, u32[]{:S(2)}, u32[]{:S(2)}) collective-permute-start(bf16[768,128]{1,0:T(8,128)(2,1)S(1)} %copy-done.7), channel_id=1, source_target_pairs={{0,8},{1,9},{2,10},{3,11},{4,12},{5,13},{6,14},{7,15},{8,16},{9,17... | collective-permute-start | bytes 589832 | tf_op jit(solution)/shard_map/ppermute | solution.py:33
  30.3 25.8 %collective-permute-start.3 = (bf16[768,128]{1,0:T(8,128)(2,1)S(1)}, bf16[768,128]{1,0:T(8,128)(2,1)S(1)}, u32[]{:S(2)}, u32[]{:S(2)}) collective-permute-start(bf16[768,128]{1,0:T(8,128)(2,1)S(1)} %copy-done.7), channel_id=1, source_target_pairs={{0,4},{1,5},{2,6},{3,7},{4,8},{5,9},{6,10},{7,11},{8,12},{9,13},{1... | collective-permute-start | bytes 589832 | tf_op jit(solution)/shard_map/ppermute | solution.py:33
  32.2 23.9 %collective-permute-start.5 = (bf16[768,128]{1,0:T(8,128)(2,1)S(1)}, bf16[768,128]{1,0:T(8,128)(2,1)S(1)}, u32[]{:S(2)}, u32[]{:S(2)}) collective-permute-start(bf16[768,128]{1,0:T(8,128)(2,1)S(1)} %copy-done.7), channel_id=1, source_target_pairs={{0,12},{1,13},{2,14},{3,15},{4,16},{5,17},{6,18},{7,19},{8,20},{9,... | collective-permute-start | bytes 589832 | tf_op jit(solution)/shard_map/ppermute | solution.py:33
  49.7 6.4 %copy-start.1 = (f32[8,2304,256]{2,1,0:T(8,128)}, f32[8,2304,256]{2,1,0:T(8,128)S(1)}, u32[]{:S(2)}) copy-start(f32[8,2304,256]{2,1,0:T(8,128)S(1)} %get-tuple-element.34.raised_ref) | copy-start | bytes 56623108
  56.1 20.8 %copy-start.2 = (bf16[2,128,8192]{2,1,0:T(8,128)(2,1)S(1)}, bf16[2,128,8192]{2,1,0:T(8,128)(2,1)}, u32[]{:S(2)}) copy-start(bf16[2,128,8192]{2,1,0:T(8,128)(2,1)} %hidden_ref.1) | copy-start | bytes 12582916
  76.7 4.7 %collective-permute-start.7 = (bf16[768,128]{1,0:T(8,128)(2,1)S(1)}, bf16[768,128]{1,0:T(8,128)(2,1)S(1)}, u32[]{:S(2)}, u32[]{:S(2)}) collective-permute-start(bf16[768,128]{1,0:T(8,128)(2,1)S(1)} %get-tuple-element.42), channel_id=1, source_target_pairs={{0,4},{1,5},{2,6},{3,7},{4,0},{5,1},{6,2},{7,3},{8,12},{9,13},{10,... | collective-permute-start | bytes 589832 | tf_op jit(solution)/shard_map/ppermute | solution.py:33
  80.9 1.7 %collective-permute-start.6 = (bf16[36,32,128]{2,1,0:T(8,128)(2,1)S(1)}, bf16[36,32,128]{2,1,0:T(8,128)(2,1)S(1)}, u32[]{:S(2)}, u32[]{:S(2)}) collective-permute-start(bf16[36,32,128]{2,1,0:T(8,128)(2,1)S(1)} %get-tuple-element.40), channel_id=1, source_target_pairs={{0,4},{1,5},{2,6},{3,7},{4,0},{5,1},{6,2},{7,3},{8,12},{9,13},{10,... | collective-permute-start | bytes 884744 | tf_op jit(solution)/shard_map/ppermute | solution.py:33
  83.6 20.0 %all-to-all-start = ((bf16[4,12,32,128]{3,2,1,0:T(8,128)(2,1)}), bf16[4,12,32,128]{3,2,1,0:T(8,128)(2,1)S(1)}, u32[]{:S(2)}, u32[]{:S(2)}) async-start(bf16[4,12,32,128]{3,2,1,0:T(8,128)(2,1)} %pad_maximum_fusion), calls=%async_computation | async-start | bytes 786432 | tf_op jit(solution)/shard_map/all_to_all | solution.py:37
  89.5 24.5 %collective-permute-start.10 = (bf16[768,128]{1,0:T(8,128)(2,1)S(1)}, bf16[768,128]{1,0:T(8,128)(2,1)S(1)}, u32[]{:S(2)}, u32[]{:S(2)}) collective-permute-start(bf16[768,128]{1,0:T(8,128)(2,1)S(1)} %get-tuple-element.46), channel_id=1, source_target_pairs={{4,0},{5,1},{6,2},{7,3},{12,8},{13,9},{14,10},{15,11},{16,4},{17,5... | collective-permute-start | bytes 589832 | tf_op jit(solution)/shard_map/ppermute | solution.py:33
  92.7 21.3 %collective-permute-start.11 = (bf16[768,128]{1,0:T(8,128)(2,1)S(1)}, bf16[768,128]{1,0:T(8,128)(2,1)S(1)}, u32[]{:S(2)}, u32[]{:S(2)}) collective-permute-start(bf16[768,128]{1,0:T(8,128)(2,1)S(1)} %get-tuple-element.47), channel_id=1, source_target_pairs={{4,0},{5,1},{6,2},{7,3},{8,4},{9,5},{10,6},{11,7},{12,8},{13,9},{1... | collective-permute-start | bytes 589832 | tf_op jit(solution)/shard_map/ppermute | solution.py:33
  94.6 36.5 %collective-permute-start.12 = (bf16[768,128]{1,0:T(8,128)(2,1)S(1)}, bf16[768,128]{1,0:T(8,128)(2,1)S(1)}, u32[]{:S(2)}, u32[]{:S(2)}) collective-permute-start(bf16[768,128]{1,0:T(8,128)(2,1)S(1)} %get-tuple-element.48), channel_id=1, source_target_pairs={{8,0},{9,1},{10,2},{11,3},{12,4},{13,5},{14,6},{15,7},{16,8},{17,9... | collective-permute-start | bytes 589832 | tf_op jit(solution)/shard_map/ppermute | solution.py:33
  96.8 34.4 %collective-permute-start.13 = (bf16[768,128]{1,0:T(8,128)(2,1)S(1)}, bf16[768,128]{1,0:T(8,128)(2,1)S(1)}, u32[]{:S(2)}, u32[]{:S(2)}) collective-permute-start(bf16[768,128]{1,0:T(8,128)(2,1)S(1)} %get-tuple-element.49), channel_id=1, source_target_pairs={{12,0},{13,1},{14,2},{15,3},{16,4},{17,5},{18,6},{19,7},{20,8},{21... | collective-permute-start | bytes 589832 | tf_op jit(solution)/shard_map/ppermute | solution.py:33
  100.4 36.1 %collective-permute-start.9 = (bf16[768,128]{1,0:T(8,128)(2,1)}, bf16[768,128]{1,0:T(8,128)(2,1)}, u32[]{:S(2)}, u32[]{:S(2)}) collective-permute-start(bf16[768,128]{1,0:T(8,128)(2,1)} %add_convert_fusion.3), channel_id=1, source_target_pairs={{8,0},{9,1},{10,2},{11,3},{12,4},{13,5},{14,6},{15,7},{16,8},{17,9... | collective-permute-start | bytes 589832 | tf_op jit(solution)/shard_map/ppermute | solution.py:33
  104.5 33.9 %all-to-all-start.1 = ((bf16[8,5,32,128]{3,2,1,0:T(8,128)(2,1)}), bf16[8,5,32,128]{3,2,1,0:T(8,128)(2,1)S(1)}, u32[]{:S(2)}, u32[]{:S(2)}) async-start(bf16[8,5,32,128]{3,2,1,0:T(8,128)(2,1)} %pad_maximum_fusion.2), calls=%async_computation.1 | async-start | bytes 655360 | tf_op jit(solution)/shard_map/all_to_all | solution.py:37
  138.3 12.3 %all-to-all-start.2 = ((bf16[2,4,192,128]{3,2,0,1:T(8,128)(2,1)}), bf16[2,4,192,128]{3,2,0,1:T(8,128)(2,1)S(1)}, u32[]{:S(2)}, u32[]{:S(2)}) async-start(bf16[2,4,192,128]{3,2,0,1:T(8,128)(2,1)} %pad_maximum_fusion.1), calls=%async_computation.2 | async-start | bytes 786432 | tf_op jit(solution)/shard_map/all_to_all | solution.py:477
  142.5 8.9 %collective-permute-start.8 = (f32[4,32,128]{2,1,0:T(8,128)S(1)}, f32[4,32,128]{2,1,0:T(8,128)S(1)}, u32[]{:S(2)}, u32[]{:S(2)}) collective-permute-start(f32[4,32,128]{2,1,0:T(8,128)S(1)} %slice.37), channel_id=1, source_target_pairs={{0,4},{1,5},{2,6},{3,7},{4,0},{5,1},{6,2},{7,3},{8,12},{9,13},{10,... | collective-permute-start | bytes 196616 | tf_op jit(solution)/shard_map/ppermute | solution.py:33

commit v2 on v0

--- a/solution.py
+++ b/solution.py
@@ -221,15 +221,32 @@
             jax.ShapeDtypeStruct((stretch, both), jnp.bfloat16),
         ],
         compiler_params=pltpu.CompilerParams(
-            dimension_semantics=("arbitrary",), vmem_limit_bytes=44 * 1024 * 1024
+            dimension_semantics=("arbitrary",), vmem_limit_bytes=28 * 1024 * 1024
         ),
         name="attention_grads",
     )(where, rel, base, grad, low, up, own, mid, far, swap)
 
 
-def adapter_kernel(dquery_ref, low_ref, up_ref, hidden_ref, out_ref, small, *, adapters, rank, lanes, inner):
+def whole(*shape):
+    return pl.BlockSpec(shape, lambda h, w: (0,) * len(shape))
+
+
+def adapter_kernel(
+    where_ref, dquery_ref, low_ref, up_ref, hidden_ref, keep_ref, send_ref, small,
+    *, adapters, rank, lanes, chips,
+):
     step = pl.program_id(0)
     outer = pl.num_programs(0)
+    odd = lax.rem(where_ref[0], 2)
+
+    def put(core, place, at, value):
+        @pl.when(odd == core)
+        def _():
+            keep_ref[place, at, :] = value
+
+        @pl.when(odd != core)
+        def _():
+            send_ref[place, at, :] = value.astype(send_ref.dtype)
 
     @pl.when(step == 0)
     def _():
@@ -238,42 +255,45 @@
             small[at, :] = dot(up_ref[a], dquery_ref[a], NT).astype(jnp.bfloat16)
             low_t = low_ref[a].astype(jnp.float32).T.astype(jnp.bfloat16)
             piece = adapter_scale * dot(low_t, dquery_ref[a], NN)
-            for i in range(inner):
-                out_ref[i, outer, at, :] = piece[:, i * lanes : (i + 1) * lanes].astype(out_ref.dtype)
+            for i in range(2 * chips):
+                put(i // chips, chips * outer + i % chips, at, piece[:, i * lanes : (i + 1) * lanes])
 
     for a in range(adapters):
         at = slice(a * rank, (a + 1) * rank)
         piece = adapter_scale * dot(small[at, :], hidden_ref[a], NN)
-        for i in range(inner):
-            out_ref[i, step, at, :] = piece[:, i * lanes : (i + 1) * lanes].astype(out_ref.dtype)
-
-
-def adapter_grads(dquery, low, up, hidden, inner, outer):
+        for i in range(2 * chips):
+            put(i % 2, (i // 2) * outer + step, at, piece[:, i * lanes : (i + 1) * lanes])
+
+
+def adapter_grads(where, dquery, low, up, hidden, chips, outer):
     adapters, rows, features = dquery.shape
     rank = low.shape[2]
     width = hidden.shape[2]
-    lanes = width // (inner * outer)
-
-    def whole(*shape):
-        return pl.BlockSpec(shape, lambda g: (0,) * len(shape))
-
+    lanes = width // (2 * chips * outer)
+    shape = ((outer + 1) * chips, adapters * rank, lanes)
     return pl.pallas_call(
-        functools.partial(adapter_kernel, adapters=adapters, rank=rank, lanes=lanes, inner=inner),
-        grid=(outer,),
-        in_specs=[
-            whole(adapters, rows, features),
-            whole(adapters, rows, rank),
-            whole(adapters, rank, features),
-            pl.BlockSpec((adapters, rows, inner * lanes), lambda g: (0, 0, g)),
+        functools.partial(adapter_kernel, adapters=adapters, rank=rank, lanes=lanes, chips=chips),
+        grid_spec=pltpu.PrefetchScalarGridSpec(
+            num_scalar_prefetch=1,
+            grid=(outer,),
+            in_specs=[
+                whole(adapters, rows, features),
+                whole(adapters, rows, rank),
+                whole(adapters, rank, features),
+                pl.BlockSpec((adapters, rows, 2 * chips * lanes), lambda g, w: (0, 0, g)),
+            ],
+            out_specs=[whole(*shape), whole(*shape)],
+            scratch_shapes=[pltpu.VMEM((adapters * rank, rows), jnp.bfloat16)],
+        ),
+        out_shape=[
+            jax.ShapeDtypeStruct(shape, jnp.float32),
+            jax.ShapeDtypeStruct(shape, jnp.bfloat16),
         ],
-        out_specs=whole(inner, outer + 1, adapters * rank, lanes),
-        out_shape=jax.ShapeDtypeStruct((inner, outer + 1, adapters * rank, lanes), jnp.bfloat16),
-        scratch_shapes=[pltpu.VMEM((adapters * rank, rows), jnp.bfloat16)],
         compiler_params=pltpu.CompilerParams(
             dimension_semantics=("arbitrary",), vmem_limit_bytes=24 * 1024 * 1024
         ),
         name="adapter_grads",
-    )(dquery, low, up, hidden)
+    )(where, dquery, low, up, hidden)
 
 
 def local(
@@ -291,20 +311,21 @@
     rank = adapter_down_weight.shape[1]
     stretch_n, head_dim = keys.shape
     seq_index = lax.axis_index("seq")
+    odd = seq_index % 2 == 1
     planes = lax.axis_size("adapter")
-    inner = row_n_seq
-    outer = lax.axis_size("seq") // inner
+    chips = row_n_seq // 2
+    outer = lax.axis_size("seq") // row_n_seq
 
     own = jnp.concatenate([keys, values], axis=1)
+    far = moved(own, 1, 3)
     mid = moved(own, 2, 2)
-    far = moved(own, 1, 3)
-    swap = moved(mid, 1, -1)
-
     low = jnp.einsum(
         "tbu,tyu->tby", hidden, adapter_down_weight, preferred_element_type=jnp.float32
     ).astype(jnp.bfloat16)
     where = jnp.concatenate([seq_index[None].astype(jnp.int32), lengths])
     rel = (offsets - seq_index * stretch_n).reshape(1, adapt_n * row_n)
+    mid, low, where, rel = lax.optimization_barrier((mid, low, where, rel))
+    swap = moved(mid, 1, -1)
     dquery, own_part, mid_part, far_part, swap_part = attention_grads(
         where,
         rel,
@@ -319,23 +340,49 @@
     )
     far_back = moved(far_part, -3, -1)
     swap_back = moved(swap_part, 1, -1)
-    mid_back = moved((mid_part + swap_back.astype(jnp.float32)).astype(jnp.bfloat16), -2, -2)
+    keep, send = adapter_grads(where, dquery, low, adapter_up_weight, hidden, chips, outer)
+    swap_back, keep, send = lax.optimization_barrier((swap_back, keep, send))
+    mid_part = (mid_part + swap_back.astype(jnp.float32)).astype(jnp.bfloat16)
+    mid_back = moved(mid_part, -2, -2)
+
+    n_down = chips * outer
+    lanes = keep.shape[2]
+    at_core = keep + moved(send, 1, -1).astype(jnp.float32)
+    at_core = at_core.astype(jnp.bfloat16)
+    up_copies = jnp.broadcast_to(at_core[None, n_down:], (chips, chips) + at_core.shape[1:])
+    at_core = jnp.concatenate(
+        [at_core[:n_down].reshape(chips, outer, adapt_n * rank, lanes), up_copies], axis=1
+    )
+    along_x = [[(g * chips + x) * 2 + c for x in range(chips)] for g in range(outer) for c in range(2)]
+    at_chip = grouped(at_core, along_x)
+    at_chip, far_back = lax.optimization_barrier((at_chip, far_back))
+    at_chip = at_chip.astype(jnp.float32).sum(0).astype(jnp.bfloat16)
+    up_copies = jnp.broadcast_to(at_chip[None, outer:], (outer, chips) + at_chip.shape[1:])
+    at_chip = jnp.concatenate([at_chip[:outer, None], up_copies], axis=1)
+    across = [[g * row_n_seq + i for g in range(outer)] for i in range(row_n_seq)]
+    summed = grouped(at_chip, across)
     prompt = own_part + far_back.astype(jnp.float32) + mid_back.astype(jnp.float32)
-    prompt = prompt.astype(jnp.bfloat16).reshape(planes, stretch_n // planes, 2 * head_dim)
-    prompt = lax.all_to_all(prompt, "adapter", 0, 0, tiled=True).astype(jnp.float32).sum(0)
-
-    blocks = adapter_grads(dquery, low, adapter_up_weight, hidden, inner, outer)
-    near = [[g * inner + i for i in range(inner)] for g in range(outer)]
-    across = [[g * inner + i for g in range(outer)] for i in range(inner)]
-    blocks = grouped(blocks, near).astype(jnp.float32).sum(0)
-    up_copies = jnp.broadcast_to(blocks[outer:], blocks[:outer].shape)
-    blocks = grouped(jnp.stack([blocks[:outer], up_copies], axis=1), across).sum(0)
-    down = blocks[0].reshape(adapt_n, rank, -1)
-    up_blocks = grouped(jnp.broadcast_to(blocks[1:], (inner,) + blocks.shape[1:]), near)
-    up_gradient = up_blocks.reshape(inner, adapt_n, rank, -1).transpose(1, 2, 0, 3)
+    prompt = prompt.reshape(planes, stretch_n // planes, 2 * head_dim)
+    plane = lax.axis_index("adapter")
+    total = lax.dynamic_index_in_dim(prompt, plane, 0, False)
+    shares = []
+    for other in range(1, planes):
+        share = lax.dynamic_index_in_dim(prompt, plane ^ other, 0, False).astype(jnp.bfloat16)
+        shares.append(lax.ppermute(share, "adapter", [(a, a ^ other) for a in range(planes)]))
+    summed, shares = lax.optimization_barrier((summed, shares))
+    prompt = total + sum(share.astype(jnp.float32) for share in shares)
+    summed = summed.astype(jnp.float32).sum(0)
+
+    down = summed[0].reshape(adapt_n, rank, lanes)
+    up_mine = summed[1:]
+    up_other = moved(up_mine, 1, -1)
+    up_blocks = jnp.concatenate(
+        [jnp.where(odd, up_other, up_mine), jnp.where(odd, up_mine, up_other)], axis=0
+    )
+    up_blocks = up_blocks.reshape(2 * chips, adapt_n, rank, lanes).transpose(1, 2, 0, 3)
     return (
         down,
-        up_gradient.reshape(adapt_n, rank, feature_n),
+        up_blocks.reshape(adapt_n, rank, feature_n),
         prompt[:, :head_dim],
         prompt[:, head_dim:],
     )

time: 150 us -> 121 us (0.81)
  waiting for transfers between devices: 44.1 us -> 15.2 us
  Pallas kernels: 32.7 us -> 34.5 us
    all_to_all x3 -> x2, waiting for transfers between devices: 31.9 us -> 6.78 us  [grouped(): lax.all_to_all(value, 'seq', 0, 0, axis_index_groups=groups, tiled=True)]
    all_to_all x1 -> x0, waiting for transfers between devices: 10.5 us -> none  [local(): lax.all_to_all(prompt, 'adapter', 0, 0, tiled=True).astype(jnp.float32)]
    all_to_all x3 -> x2, starting transfers between devices: 35.1 us -> 27.3 us  [grouped(): lax.all_to_all(value, 'seq', 0, 0, axis_index_groups=groups, tiled=True)]
    ppermute x6 -> x8, starting transfers between devices: 16.3 us -> 22.7 us  [moved(): return lax.ppermute(value, both_axes, pairs)]
    ppermute x0 -> x3, waiting for transfers between devices: none -> 3.75 us  [local(): lax.ppermute(share, 'adapter', [(a, a ^ other) for a in range(planes)])]
    ppermute x0 -> x3, starting transfers between devices: none -> 3.63 us  [local(): lax.ppermute(share, 'adapter', [(a, a ^ other) for a in range(planes)])]
    all_to_all x1 -> x0, starting transfers between devices: 3.46 us -> none  [local(): lax.all_to_all(prompt, 'adapter', 0, 0, tiled=True).astype(jnp.float32)]
    ppermute x6 -> x8, waiting for transfers between devices: 1.7 us -> 4.7 us  [moved(): return lax.ppermute(value, both_axes, pairs)]
  transfers between devices with their start and end apart: 10 -> 13, of which waited for: 5 -> 5; matrix products, arithmetic and copies ran while one was open for 6% -> 8% of each run, Pallas kernels for 0% -> 3%
where the time goes in v2:
time: 121 us; the launch traced here: 120 us
  starting transfers between devices  53.6 us (44%)
  Pallas kernels  34.5 us (29%)
  waiting for transfers between devices  15.2 us (13%)
  local copies, waits for them, and re-layouts  7.65 us (6%)
  other arithmetic  4.75 us (4%)
  matrix products  3.4 us (3%)
    pallas_call x1, Pallas kernels, attention_grads(): pl.pallas_call(body, grid_spec=pltpu.PrefetchScalarGridSpec(num_scalar_pr...  30.5 us
    all_to_all x2, starting transfers between devices, grouped(): lax.all_to_all(value, 'seq', 0, 0, axis_index_groups=groups, tiled=True)  27.3 us
    ppermute x8, starting transfers between devices, moved(): return lax.ppermute(value, both_axes, pairs)  22.7 us
    all_to_all x2, waiting for transfers between devices, grouped(): lax.all_to_all(value, 'seq', 0, 0, axis_index_groups=groups, tiled=True)  6.78 us
    ppermute x8, waiting for transfers between devices, moved(): return lax.ppermute(value, both_axes, pairs)  4.7 us
    unnamed x19, local copies, waits for them, and re-layouts  4.57 us
    pallas_call x1, Pallas kernels, adapter_grads(): pl.pallas_call(functools.partial(adapter_kernel, adapters=adapters, rank=...  3.99 us
    ppermute x3, waiting for transfers between devices, local(): lax.ppermute(share, 'adapter', [(a, a ^ other) for a in range(planes)])  3.75 us
  transfers between devices with their start and end apart: 13, of which 5 were waited for; matrix products, arithmetic and copies ran while one was open for 8% of the time, Pallas kernels for 3%

profile of v2, /device:TPU:1, one launch (start us, length us, event | category | flops | bytes accessed | tf_op | source)
XLA Modules:
  0.0 120.1 jit_solution(12510531512376353142)
XLA Ops:
  0.6 0.0 copy-start
  0.6 0.0 copy-start.2
  0.7 0.0 copy-start.3
  0.7 1.1 constant_dynamic-update-slice_fusion.1
  1.7 1.0 constant_dynamic-update-slice_fusion.kv_own
  2.7 4.0 %collective-permute-start = (bf16[768,256]{1,0:T(8,128)(2,1)S(1)}, bf16[768,256]{1,0:T(8,128)(2,1)S(1)}, u32[]{:S(2)}, u32[]{:S(2)}) collective-permute-start(bf16[768,256]{1,0:T(8,128)(2,1)S(1)} %constant_dynamic-update-slice_fusion.kv_own), channel_id=1, source_target_pairs={{0,8},{1,9},{2,10},{3,11},{4,12},{5,13},{6,14},{7,15},{8,16},{9,17... | collective-permute-start | bytes 1179656 | tf_op jit(solution)/shard_map/ppermute | solution.py:33
  6.7 5.2 %collective-permute-start.1 = (bf16[768,256]{1,0:T(8,128)(2,1)S(1)}, bf16[768,256]{1,0:T(8,128)(2,1)S(1)}, u32[]{:S(2)}, u32[]{:S(2)}) collective-permute-start(bf16[768,256]{1,0:T(8,128)(2,1)S(1)} %constant_dynamic-update-slice_fusion.kv_own), channel_id=1, source_target_pairs={{0,4},{1,5},{2,6},{3,7},{4,16},{5,17},{6,18},{7,19},{8,12},{9,13},... | collective-permute-start | bytes 1179656 | tf_op jit(solution)/shard_map/ppermute | solution.py:33
  11.9 0.0 copy-start.8
  11.9 0.0 copy-start.1
  11.9 0.8 broadcast_subtract_fusion
  12.8 1.2 pad_add_fusion.where_ref
  13.9 0.0 copy-done
  13.9 3.4 %convolution_convert_fusion.low_ref = bf16[2,128,16]{2,1,0:T(8,128)(2,1)S(1)} fusion(bf16[2,128,8192]{2,1,0:T(8,128)(2,1)} %hidden_ref.1, bf16[2,16,8192]{2,1,0:T(8,128)(2,1)S(1)} %copy-done), kind=kOutput, calls=%fused_computation | convolution fusion | flops 67112960 | bytes 4726784 | tf_op jit(solution)/shard_map/tbu,tyu->tby/dot_general | solution.py:322
  17.3 0.0 collective-permute-done.kv_mid
  17.3 0.1 collective-permute-start.2
  17.4 0.0 copy-start.4
  17.5 0.7 copy-done.4
  18.2 1.6 %collective-permute-done.1.kv_far = bf16[768,256]{1,0:T(8,128)(2,1)S(1)} collective-permute-done((bf16[768,256]{1,0:T(8,128)(2,1)S(1)}, bf16[768,256]{1,0:T(8,128)(2,1)S(1)}, u32[]{:S(2)}, u32[]{:S(2)}) %collective-permute-start.1) | collective-permute-done | bytes 393248 | tf_op jit(solution)/shard_map/ppermute | solution.py:33
  19.8 0.0 copy-start.6
  19.8 0.7 copy-done.6
  20.6 0.0 collective-permute-done.2.kv_swap
  20.6 0.0 copy-done.2
  20.6 0.0 copy-done.3
  20.6 0.0 copy-done.8
  20.6 0.0 copy-start.5
  20.6 1.0 copy-done.5
  21.6 0.0 copy-start.7
  21.6 1.0 copy-done.7
  22.6 30.5 %attention_grads.1 = (bf16[2,128,1024]{2,1,0:T(8,128)(2,1)S(1)}, f32[768,256]{1,0:T(8,128)S(1)}, f32[768,256]{1,0:T(8,128)S(1)}, bf16[768,256]{1,0:T(8,128)(2,1)}, bf16[768,256]{1,0:T(8,128)(2,1)S(1)}) custom-call(s32[3]{0:T(128)S(1)} %pad_add_fusion.where_ref, s32[1,256]{1,0:T(1,128)S(1)} %bitcast.24, bf16[2,128,1024]{2,1,0:T(8,128)(2,1)S(1)} %copy-done.2, ...), custom_call_target="tpu_custom_call" | custom-call | tf_op jit(solution)/shard_map/attention_grads/pallas_call | solution.py:193
  53.1 0.0 collective-permute-start.3
  53.1 0.0 copy-done.1
  53.1 4.0 %adapter_grads.1 = (f32[36,32,128]{2,1,0:T(8,128)S(1)}, bf16[36,32,128]{2,1,0:T(8,128)(2,1)S(1)}) custom-call(s32[3]{0:T(128)S(1)} %pad_add_fusion.where_ref, bf16[2,128,1024]{2,1,0:T(8,128)(2,1)S(1)} %get-tuple-element.29.dquery_ref, bf16[2,128,16]{2,1,0:T(8,128)(2,1)S(1)} %convolution_convert_fusion.low_ref, bf16[2,16,1024]{2,1,0:T(8,128)(2,1)S(1)} %copy-done.8, ...), custom_call_target="tpu_custom_call" | custom-call | tf_op jit(solution)/shard_map/adapter_grads/pallas_call | solution.py:274
  57.1 0.0 collective-permute-done.3
  57.1 0.6 collective-permute-start.4
  57.7 1.9 %collective-permute-start.5 = (bf16[768,256]{1,0:T(8,128)(2,1)}, bf16[768,256]{1,0:T(8,128)(2,1)S(1)}, u32[]{:S(2)}, u32[]{:S(2)}) collective-permute-start(bf16[768,256]{1,0:T(8,128)(2,1)} %get-tuple-element.34), channel_id=1, source_target_pairs={{4,0},{5,1},{6,2},{7,3},{12,8},{13,9},{14,10},{15,11},{16,4},{17,5... | collective-permute-start | bytes 1179656 | tf_op jit(solution)/shard_map/ppermute | solution.py:33
  59.6 0.0 collective-permute-done.4
  59.6 0.1 add_convert_fusion.1
  59.7 0.8 pad_maximum_fusion
  60.6 20.7 %all-to-all-start = ((bf16[4,12,32,128]{3,2,1,0:T(8,128)(2,1)}), bf16[4,12,32,128]{3,2,1,0:T(8,128)(2,1)S(1)}, u32[]{:S(2)}, u32[]{:S(2)}) async-start(bf16[4,12,32,128]{3,2,1,0:T(8,128)(2,1)} %pad_maximum_fusion), calls=%async_computation | async-start | bytes 786432 | tf_op jit(solution)/shard_map/all_to_all | solution.py:37
  81.2 0.8 add_convert_fusion
  82.1 1.3 %collective-permute-start.6 = (bf16[768,256]{1,0:T(8,128)(2,1)}, bf16[768,256]{1,0:T(8,128)(2,1)S(1)}, u32[]{:S(2)}, u32[]{:S(2)}) collective-permute-start(bf16[768,256]{1,0:T(8,128)(2,1)} %add_convert_fusion), channel_id=1, source_target_pairs={{8,0},{9,1},{10,2},{11,3},{12,4},{13,5},{14,6},{15,7},{16,8},{17,9... | collective-permute-start | bytes 1179656 | tf_op jit(solution)/shard_map/ppermute | solution.py:33
  83.3 0.0 collective-permute-done.5
  83.4 6.8 %all-to-all-done = bf16[4,12,32,128]{3,2,1,0:T(8,128)(2,1)S(1)} async-done(((bf16[4,12,32,128]{3,2,1,0:T(8,128)(2,1)}), bf16[4,12,32,128]{3,2,1,0:T(8,128)(2,1)S(1)}, u32[]{:S(2)}, u32[]{:S(2)}) %all-to-all-start) | async-done | bytes 393248 | tf_op jit(solution)/shard_map/all_to_all | solution.py:37
  90.1 0.1 reduce_sum.21
  90.3 0.7 pad_maximum_fusion.1
  91.0 6.6 %all-to-all-start.1 = ((bf16[8,5,32,128]{3,2,1,0:T(8,128)(2,1)}), bf16[8,5,32,128]{3,2,1,0:T(8,128)(2,1)S(1)}, u32[]{:S(2)}, u32[]{:S(2)}) async-start(bf16[8,5,32,128]{3,2,1,0:T(8,128)(2,1)} %pad_maximum_fusion.1), calls=%async_computation.1 | async-start | bytes 655360 | tf_op jit(solution)/shard_map/all_to_all | solution.py:37
  97.7 3.1 %collective-permute-done.6 = bf16[768,256]{1,0:T(8,128)(2,1)S(1)} collective-permute-done((bf16[768,256]{1,0:T(8,128)(2,1)}, bf16[768,256]{1,0:T(8,128)(2,1)S(1)}, u32[]{:S(2)}, u32[]{:S(2)}) %collective-permute-start.6) | collective-permute-done | bytes 393248 | tf_op jit(solution)/shard_map/ppermute | solution.py:33
  100.7 0.1 convert_add_fusion
  100.9 0.1 collective-permute-start.7
  101.0 1.9 %collective-permute-start.8 = (bf16[192,256]{1,0:T(8,128)(2,1)S(1)}, bf16[192,256]{1,0:T(8,128)(2,1)S(1)}, u32[]{:S(2)}, u32[]{:S(2)}) collective-permute-start(bf16[192,256]{1,0:T(8,128)(2,1)S(1)} %get-tuple-element.45), channel_id=1, source_target_pairs={{0,2},{1,3},{2,0},{3,1},{4,6},{5,7},{6,4},{7,5},{8,10},{9,11},{10,... | collective-permute-start | bytes 294920 | tf_op jit(solution)/shard_map/ppermute | solution.py:371
  102.9 1.6 %collective-permute-start.9 = (bf16[192,256]{1,0:T(8,128)(2,1)S(1)}, bf16[192,256]{1,0:T(8,128)(2,1)S(1)}, u32[]{:S(2)}, u32[]{:S(2)}) collective-permute-start(bf16[192,256]{1,0:T(8,128)(2,1)S(1)} %get-tuple-element.44), channel_id=1, source_target_pairs={{0,3},{1,2},{2,1},{3,0},{4,7},{5,6},{6,5},{7,4},{8,11},{9,10},{10,... | collective-permute-start | bytes 294920 | tf_op jit(solution)/shard_map/ppermute | solution.py:371
  104.5 1.6 %collective-permute-done.7 = bf16[192,256]{1,0:T(8,128)(2,1)S(1)} collective-permute-done((bf16[192,256]{1,0:T(8,128)(2,1)S(1)}, bf16[192,256]{1,0:T(8,128)(2,1)S(1)}, u32[]{:S(2)}, u32[]{:S(2)}) %collective-permute-start.7) | collective-permute-done | bytes 98336 | tf_op jit(solution)/shard_map/ppermute | solution.py:371
  106.1 0.0 collective-permute-done.8
  106.1 2.2 %collective-permute-done.9 = bf16[192,256]{1,0:T(8,128)(2,1)S(1)} collective-permute-done((bf16[192,256]{1,0:T(8,128)(2,1)S(1)}, bf16[192,256]{1,0:T(8,128)(2,1)S(1)}, u32[]{:S(2)}, u32[]{:S(2)}) %collective-permute-start.9) | collective-permute-done | bytes 98336 | tf_op jit(solution)/shard_map/ppermute | solution.py:371
  108.3 0.0 all-to-all-done.1
  108.4 9.7 %collective-permute-start.10 = (f32[4,32,128]{2,1,0:T(8,128)S(1)}, f32[4,32,128]{2,1,0:T(8,128)S(1)}, u32[]{:S(2)}, u32[]{:S(2)}) collective-permute-start(f32[4,32,128]{2,1,0:T(8,128)S(1)} %slice.37), channel_id=1, source_target_pairs={{0,4},{1,5},{2,6},{3,7},{4,0},{5,1},{6,2},{7,3},{8,12},{9,13},{10,... | collective-permute-start | bytes 196616 | tf_op jit(solution)/shard_map/ppermute | solution.py:33
  118.1 0.7 fusion.3
  118.8 0.6 slice.36
  119.4 0.0 collective-permute-done.10
  119.4 0.7 copy.21
  (12 shorter events, 0.2 us)
Async XLA Ops:
  0.6 13.3 %copy-start = (bf16[2,16,8192]{2,1,0:T(8,128)(2,1)S(1)}, bf16[2,16,8192]{2,1,0:T(8,128)(2,1)}, u32[]{:S(2)}) copy-start(bf16[2,16,8192]{2,1,0:T(8,128)(2,1)} %param.14) | copy-start | bytes 1572868
  0.6 19.9 %copy-start.2 = (bf16[2,128,1024]{2,1,0:T(8,128)(2,1)S(1)}, bf16[2,128,1024]{2,1,0:T(8,128)(2,1)}, u32[]{:S(2)}) copy-start(bf16[2,128,1024]{2,1,0:T(8,128)(2,1)} %base_ref.1) | copy-start | bytes 1572868
  0.7 19.9 %copy-start.3 = (bf16[2,128,1024]{2,1,0:T(8,128)(2,1)S(1)}, bf16[2,128,1024]{2,1,0:T(8,128)(2,1)}, u32[]{:S(2)}) copy-start(bf16[2,128,1024]{2,1,0:T(8,128)(2,1)} %grad_ref.1) | copy-start | bytes 1572868
  2.7 14.6 %collective-permute-start = (bf16[768,256]{1,0:T(8,128)(2,1)S(1)}, bf16[768,256]{1,0:T(8,128)(2,1)S(1)}, u32[]{:S(2)}, u32[]{:S(2)}) collective-permute-start(bf16[768,256]{1,0:T(8,128)(2,1)S(1)} %constant_dynamic-update-slice_fusion.kv_own), channel_id=1, source_target_pairs={{0,8},{1,9},{2,10},{3,11},{4,12},{5,13},{6,14},{7,15},{8,16},{9,17... | collective-permute-start | bytes 1179656 | tf_op jit(solution)/shard_map/ppermute | solution.py:33
  6.7 13.1 %collective-permute-start.1 = (bf16[768,256]{1,0:T(8,128)(2,1)S(1)}, bf16[768,256]{1,0:T(8,128)(2,1)S(1)}, u32[]{:S(2)}, u32[]{:S(2)}) collective-permute-start(bf16[768,256]{1,0:T(8,128)(2,1)S(1)} %constant_dynamic-update-slice_fusion.kv_own), channel_id=1, source_target_pairs={{0,4},{1,5},{2,6},{3,7},{4,16},{5,17},{6,18},{7,19},{8,12},{9,13},... | collective-permute-start | bytes 1179656 | tf_op jit(solution)/shard_map/ppermute | solution.py:33
  11.9 8.7 %copy-start.8 = (bf16[2,16,1024]{2,1,0:T(8,128)(2,1)S(1)}, bf16[2,16,1024]{2,1,0:T(8,128)(2,1)}, u32[]{:S(2)}) copy-start(bf16[2,16,1024]{2,1,0:T(8,128)(2,1)} %up_ref.3) | copy-start | bytes 196612
  11.9 41.2 %copy-start.1 = (bf16[2,128,8192]{2,1,0:T(8,128)(2,1)S(1)}, bf16[2,128,8192]{2,1,0:T(8,128)(2,1)}, u32[]{:S(2)}) copy-start(bf16[2,128,8192]{2,1,0:T(8,128)(2,1)} %hidden_ref.1) | copy-start | bytes 12582916
  17.3 3.2 %collective-permute-start.2 = (bf16[768,256]{1,0:T(8,128)(2,1)S(1)}, bf16[768,256]{1,0:T(8,128)(2,1)S(1)}, u32[]{:S(2)}, u32[]{:S(2)}) collective-permute-start(bf16[768,256]{1,0:T(8,128)(2,1)S(1)} %collective-permute-done.kv_mid), channel_id=1, source_target_pairs={{0,4},{1,5},{2,6},{3,7},{4,0},{5,1},{6,2},{7,3},{8,12},{9,13},{10,... | collective-permute-start | bytes 1179656 | tf_op jit(solution)/shard_map/ppermute | solution.py:33
  17.4 0.7 copy-start.4
  19.8 0.7 copy-start.6
  20.6 1.0 copy-start.5
  21.6 1.0 copy-start.7
  53.1 4.0 %collective-permute-start.3 = (bf16[768,256]{1,0:T(8,128)(2,1)S(1)}, bf16[768,256]{1,0:T(8,128)(2,1)S(1)}, u32[]{:S(2)}, u32[]{:S(2)}) collective-permute-start(bf16[768,256]{1,0:T(8,128)(2,1)S(1)} %get-tuple-element.28), channel_id=1, source_target_pairs={{0,4},{1,5},{2,6},{3,7},{4,0},{5,1},{6,2},{7,3},{8,12},{9,13},{10,... | collective-permute-start | bytes 1179656 | tf_op jit(solution)/shard_map/ppermute | solution.py:33
  57.1 2.5 %collective-permute-start.4 = (bf16[36,32,128]{2,1,0:T(8,128)(2,1)S(1)}, bf16[36,32,128]{2,1,0:T(8,128)(2,1)S(1)}, u32[]{:S(2)}, u32[]{:S(2)}) collective-permute-start(bf16[36,32,128]{2,1,0:T(8,128)(2,1)S(1)} %get-tuple-element.33), channel_id=1, source_target_pairs={{0,4},{1,5},{2,6},{3,7},{4,0},{5,1},{6,2},{7,3},{8,12},{9,13},{10,... | collective-permute-start | bytes 884744 | tf_op jit(solution)/shard_map/ppermute | solution.py:33
  57.7 25.7 %collective-permute-start.5 = (bf16[768,256]{1,0:T(8,128)(2,1)}, bf16[768,256]{1,0:T(8,128)(2,1)S(1)}, u32[]{:S(2)}, u32[]{:S(2)}) collective-permute-start(bf16[768,256]{1,0:T(8,128)(2,1)} %get-tuple-element.34), channel_id=1, source_target_pairs={{4,0},{5,1},{6,2},{7,3},{12,8},{13,9},{14,10},{15,11},{16,4},{17,5... | collective-permute-start | bytes 1179656 | tf_op jit(solution)/shard_map/ppermute | solution.py:33
  60.6 29.6 %all-to-all-start = ((bf16[4,12,32,128]{3,2,1,0:T(8,128)(2,1)}), bf16[4,12,32,128]{3,2,1,0:T(8,128)(2,1)S(1)}, u32[]{:S(2)}, u32[]{:S(2)}) async-start(bf16[4,12,32,128]{3,2,1,0:T(8,128)(2,1)} %pad_maximum_fusion), calls=%async_computation | async-start | bytes 786432 | tf_op jit(solution)/shard_map/all_to_all | solution.py:37
  82.1 18.7 %collective-permute-start.6 = (bf16[768,256]{1,0:T(8,128)(2,1)}, bf16[768,256]{1,0:T(8,128)(2,1)S(1)}, u32[]{:S(2)}, u32[]{:S(2)}) collective-permute-start(bf16[768,256]{1,0:T(8,128)(2,1)} %add_convert_fusion), channel_id=1, source_target_pairs={{8,0},{9,1},{10,2},{11,3},{12,4},{13,5},{14,6},{15,7},{16,8},{17,9... | collective-permute-start | bytes 1179656 | tf_op jit(solution)/shard_map/ppermute | solution.py:33
  91.0 17.3 %all-to-all-start.1 = ((bf16[8,5,32,128]{3,2,1,0:T(8,128)(2,1)}), bf16[8,5,32,128]{3,2,1,0:T(8,128)(2,1)S(1)}, u32[]{:S(2)}, u32[]{:S(2)}) async-start(bf16[8,5,32,128]{3,2,1,0:T(8,128)(2,1)} %pad_maximum_fusion.1), calls=%async_computation.1 | async-start | bytes 655360 | tf_op jit(solution)/shard_map/all_to_all | solution.py:37
  100.9 5.2 %collective-permute-start.7 = (bf16[192,256]{1,0:T(8,128)(2,1)S(1)}, bf16[192,256]{1,0:T(8,128)(2,1)S(1)}, u32[]{:S(2)}, u32[]{:S(2)}) collective-permute-start(bf16[192,256]{1,0:T(8,128)(2,1)S(1)} %get-tuple-element.46), channel_id=1, source_target_pairs={{0,1},{1,0},{2,3},{3,2},{4,5},{5,4},{6,7},{7,6},{8,9},{9,8},{10,11... | collective-permute-start | bytes 294920 | tf_op jit(solution)/shard_map/ppermute | solution.py:371
  101.0 5.1 %collective-permute-start.8 = (bf16[192,256]{1,0:T(8,128)(2,1)S(1)}, bf16[192,256]{1,0:T(8,128)(2,1)S(1)}, u32[]{:S(2)}, u32[]{:S(2)}) collective-permute-start(bf16[192,256]{1,0:T(8,128)(2,1)S(1)} %get-tuple-element.45), channel_id=1, source_target_pairs={{0,2},{1,3},{2,0},{3,1},{4,6},{5,7},{6,4},{7,5},{8,10},{9,11},{10,... | collective-permute-start | bytes 294920 | tf_op jit(solution)/shard_map/ppermute | solution.py:371
  102.9 5.4 %collective-permute-start.9 = (bf16[192,256]{1,0:T(8,128)(2,1)S(1)}, bf16[192,256]{1,0:T(8,128)(2,1)S(1)}, u32[]{:S(2)}, u32[]{:S(2)}) collective-permute-start(bf16[192,256]{1,0:T(8,128)(2,1)S(1)} %get-tuple-element.44), channel_id=1, source_target_pairs={{0,3},{1,2},{2,1},{3,0},{4,7},{5,6},{6,5},{7,4},{8,11},{9,10},{10,... | collective-permute-start | bytes 294920 | tf_op jit(solution)/shard_map/ppermute | solution.py:371
  108.4 11.0 %collective-permute-start.10 = (f32[4,32,128]{2,1,0:T(8,128)S(1)}, f32[4,32,128]{2,1,0:T(8,128)S(1)}, u32[]{:S(2)}, u32[]{:S(2)}) collective-permute-start(f32[4,32,128]{2,1,0:T(8,128)S(1)} %slice.37), channel_id=1, source_target_pairs={{0,4},{1,5},{2,6},{3,7},{4,0},{5,1},{6,2},{7,3},{8,12},{9,13},{10,... | collective-permute-start | bytes 196616 | tf_op jit(solution)/shard_map/ppermute | solution.py:33

commit v3 on v2

v3 whole, which is shorter than its diff:
```python
import functools

import jax
import jax.numpy as jnp
from jax import lax
from jax.experimental import pallas as pl
from jax.experimental.pallas import tpu as pltpu
from jax.sharding import PartitionSpec as P

adapter_scale = 2.0
masked_score = -1.0e30
log2_e = 1.4426950408889634
both_axes = ("seq", "adapter")
row_n_seq = 8

NN = ((1,), (0,))
NT = ((1,), (1,))


def dot(a, b, dims):
    return lax.dot_general(a, b, (dims, ((), ())), preferred_element_type=jnp.float32)


def moved(value, by_even, by_odd):
    peers, planes = lax.axis_size("seq"), lax.axis_size("adapter")
    pairs = []
    for s in range(peers):
        t = s + (by_odd if s % 2 else by_even)
        if 0 <= t < peers:
            for a in range(planes):
                b = a if t // row_n_seq == s // row_n_seq else planes - 1 - a
                pairs.append((s * planes + a, t * planes + b))
    return lax.ppermute(value, both_axes, pairs)


def grouped(value, groups):
    return lax.all_to_all(value, "seq", 0, 0, axis_index_groups=groups, tiled=True)


def fold(x, op):
    return op(x.reshape(x.shape[0] // 8, 8, x.shape[1]), axis=0)


def chunks(stretch, chunk):
    for d in range(3):
        for c in range(0, stretch, chunk):
            yield d, slice(c, c + chunk), slice(d * stretch + c, d * stretch + c + chunk)


def attention_kernel(
    where_ref, rel_ref, base_ref, grad_ref, low_ref, up_ref, up_whole_ref, own_in, mid_in, far_in, swap_in, hidden_in,
    own_ref, mid_ref, far_ref, swap_ref, keep_ref, send_ref,
    window_k, window_v, key_t, score, dprob, dscore_low, acc_k, acc_v, hidden, dquery, pieces, block_sems, hidden_sem,
    *, stretch, chunk, rows, adapters, head_dim, heads, per_step, rank, chips, outer,
):
    step = pl.program_id(0)
    factor = head_dim**-0.5
    shift = factor * log2_e
    wide = rows * adapters
    block = where_ref[0]
    odd = lax.rem(block, 2)
    far_slot = 3 - 2 * odd
    swap_slot = 1 + 2 * odd

    def fills():
        sources = ((0, own_in), (2, mid_in), (far_slot, far_in), (swap_slot, swap_in))
        for i, (slot, source) in enumerate(sources):
            yield pltpu.make_async_copy(source.at[0], window_k.at[slot], block_sems.at[2 * i])
            yield pltpu.make_async_copy(source.at[1], window_v.at[slot], block_sems.at[2 * i + 1])

    hidden_copy = pltpu.make_async_copy(hidden_in, hidden, hidden_sem)

    @pl.when(step == 0)
    def _():
        for copy in fills():
            copy.start()
        hidden_copy.start()
        acc_k[...] = jnp.zeros_like(acc_k)
        acc_v[...] = jnp.zeros_like(acc_v)
        for copy in fills():
            copy.wait()
        for d in range(4):
            key_t[:, d * stretch : (d + 1) * stretch] = window_k[d].T

    rel = rel_ref[...]
    place = lax.broadcasted_iota(jnp.int32, (chunk, wide), 0)
    line = block * rows + lax.broadcasted_iota(jnp.int32, (rows, head_dim), 0)
    bias3 = jnp.where(block >= 3, 0.0, masked_score)

    def scores_of(j):
        cols = slice(j * head_dim, (j + 1) * head_dim)
        query_list = []
        grad_list = []
        for a in range(adapters):
            raised = dot(low_ref[a], up_ref[a, :, cols], NN)
            query_list.append(
                (base_ref[a, :, cols].astype(jnp.float32) + adapter_scale * raised).astype(jnp.bfloat16)
            )
            live = line < where_ref[1 + a]
            grad_list.append(
                jnp.where(live, grad_ref[a, :, cols].astype(jnp.float32), 0.0).astype(jnp.bfloat16)
            )
        query = jnp.concatenate(query_list, axis=0)
        grad = jnp.concatenate(grad_list, axis=0)
        highs = [None] * 3
        for d, part, at in chunks(stretch, chunk):
            s = dot(window_k[d, part, :], query, NT)
            dp = dot(window_v[d, part, :], grad, NT)
            if d == 0:
                early = rel >= place + part.start
                s = jnp.where(early, s, dot(window_k[3, part, :], query, NT) + bias3)
                dp = jnp.where(early, dp, dot(window_v[3, part, :], grad, NT))
            score[j, at, :] = s
            dprob[j, at, :] = dp
            top = fold(s, jnp.max)
            highs[d] = top if highs[d] is None else jnp.maximum(highs[d], top)
        peak = highs[0]
        for d in (1, 2):
            peak = jnp.maximum(peak, jnp.where(block >= d, highs[d], masked_score))
        return query, grad, jnp.max(peak, axis=0, keepdims=True)

    def sums_of(j, query, grad, peak):
        levels = [peak] + [jnp.where(block >= d, peak, -masked_score) for d in (1, 2)]
        total = jnp.zeros((8, wide), jnp.float32)
        delta = jnp.zeros((8, wide), jnp.float32)
        for d, part, at in chunks(stretch, chunk):
            e = jnp.exp2((score[j, at, :] - levels[d]) * shift)
            score[j, at, :] = e
            total = total + fold(e, jnp.sum)
            delta = delta + fold(e * dprob[j, at, :], jnp.sum)
        scale = 1.0 / jnp.sum(total, axis=0, keepdims=True)
        return query, grad, scale, jnp.sum(delta, axis=0, keepdims=True) * scale

    def grads_of(j, query, grad, scale, delta):
        for d, part, at in chunks(stretch, chunk):
            p = score[j, at, :] * scale
            ds = p * (dprob[j, at, :] - delta)
            if d == 0:
                early = rel >= place + part.start
                zero = jnp.zeros_like(p)
                split = (
                    (0, jnp.where(early, p, zero), jnp.where(early, ds, zero)),
                    (3, jnp.where(early, zero, p), jnp.where(early, zero, ds)),
                )
            else:
                split = ((d, p, ds),)
            for e, p_e, ds_e in split:
                ds_e = ds_e.astype(jnp.bfloat16)
                dscore_low[j, e * stretch + part.start : e * stretch + part.stop, :] = ds_e
                acc_k[e, part, :] += dot(ds_e, query, NN)
                acc_v[e, part, :] += dot(p_e.astype(jnp.bfloat16), grad, NN)
        part = (dot(key_t[...], dscore_low[j], NN).T * factor).astype(jnp.bfloat16)
        for a in range(adapters):
            dquery[step * per_step + j, a] = part[a * rows : (a + 1) * rows]

    states = [scores_of(j) for j in range(per_step)]
    for j in range(per_step):
        grads_of(j, *sums_of(j, *states[j]))

    @pl.when(step == heads // per_step - 1)
    def _():
        def put(out, slot):
            out[0] = (acc_k[slot] * factor).astype(out.dtype)
            out[1] = acc_v[slot].astype(out.dtype)

        put(own_ref, 0)
        put(mid_ref, 2)
        put(far_ref, far_slot)
        put(swap_ref, swap_slot)
        hidden_copy.wait()
        span = 2 * chips * head_dim
        for a in range(adapters):
            at = slice(a * rank, (a + 1) * rank)
            low_t = low_ref[a].astype(jnp.float32).T.astype(jnp.bfloat16)
            small = jnp.zeros((rank, rows), jnp.float32)
            for h in range(heads):
                mine = dquery[h, a]
                small += dot(up_whole_ref[a, :, h * head_dim : (h + 1) * head_dim], mine, NT)
                pieces[h // chips, chips * outer + h % chips, at, :] = adapter_scale * dot(
                    low_t, mine, NN
                )
            small_low = small.astype(jnp.bfloat16)
            for g in range(outer):
                piece = dot(small_low, hidden[a, :, g * span : (g + 1) * span], NN) * adapter_scale
                for i in range(2 * chips):
                    pieces[i % 2, (i // 2) * outer + g, at, :] = piece[
                        :, i * head_dim : (i + 1) * head_dim
                    ]
        keep_ref[...] = pieces[odd]
        send_ref[...] = pieces[1 - odd].astype(send_ref.dtype)


def whole(*shape):
    return pl.BlockSpec(shape, lambda h, w: (0,) * len(shape))


def attention_grads(where, rel, base, grad, low, up, own, mid, far, swap, hidden, chips, outer):
    adapters, rows, features = base.shape
    _, stretch, head_dim = own.shape
    heads = features // head_dim
    rank, wide, width = low.shape[2], rows * adapters, hidden.shape[2]
    per_step = 2
    assert heads == 2 * chips and width == 2 * chips * outer * head_dim
    body = functools.partial(
        attention_kernel,
        stretch=stretch,
        chunk=384,
        rows=rows,
        adapters=adapters,
        head_dim=head_dim,
        heads=heads,
        per_step=per_step,
        rank=rank,
        chips=chips,
        outer=outer,
    )
    per_head = pl.BlockSpec((adapters, rows, per_step * head_dim), lambda h, w: (0, 0, h))
    anywhere = pl.BlockSpec(memory_space=pltpu.HBM)
    blocks = (chips * outer + chips, adapters * rank, head_dim)
    pair = (2, stretch, head_dim)
    return pl.pallas_call(
        body,
        grid_spec=pltpu.PrefetchScalarGridSpec(
            num_scalar_prefetch=1,
            grid=(heads // per_step,),
            in_specs=[
                whole(1, wide),
                per_head,
                per_head,
                whole(adapters, rows, rank),
                pl.BlockSpec((adapters, rank, per_step * head_dim), lambda h, w: (0, 0, h)),
                whole(adapters, rank, features),
            ]
            + [anywhere] * 5,
            out_specs=[whole(*pair)] * 4 + [whole(*blocks)] * 2,
            scratch_shapes=[
                pltpu.VMEM((4, stretch, head_dim), jnp.bfloat16),
                pltpu.VMEM((4, stretch, head_dim), jnp.bfloat16),
                pltpu.VMEM((head_dim, 4 * stretch), jnp.bfloat16),
                pltpu.VMEM((per_step, 3 * stretch, wide), jnp.float32),
                pltpu.VMEM((per_step, 3 * stretch, wide), jnp.float32),
                pltpu.VMEM((per_step, 4 * stretch, wide), jnp.bfloat16),
                pltpu.VMEM((4, stretch, head_dim), jnp.float32),
                pltpu.VMEM((4, stretch, head_dim), jnp.float32),
                pltpu.VMEM((adapters, rows, width), jnp.bfloat16),
                pltpu.VMEM((heads, adapters, rows, head_dim), jnp.bfloat16),
                pltpu.VMEM((2,) + blocks, jnp.float32),
                pltpu.SemaphoreType.DMA((8,)),
                pltpu.SemaphoreType.DMA,
            ],
        ),
        out_shape=[
            jax.ShapeDtypeStruct(pair, kind)
            for kind in (jnp.float32, jnp.float32, jnp.bfloat16, jnp.bfloat16)
        ]
        + [jax.ShapeDtypeStruct(blocks, jnp.float32), jax.ShapeDtypeStruct(blocks, jnp.bfloat16)],
        compiler_params=pltpu.CompilerParams(
            dimension_semantics=("arbitrary",), vmem_limit_bytes=58 * 1024 * 1024
        ),
        name="attention_grads",
    )(where, rel, base, grad, low, up, up, own, mid, far, swap, hidden)


def local(
    hidden,
    response_base_queries,
    attention_output_gradient,
    keys,
    values,
    adapter_down_weight,
    adapter_up_weight,
    lengths,
    offsets,
):
    adapt_n, row_n, feature_n = response_base_queries.shape
    rank = adapter_down_weight.shape[1]
    stretch_n, head_dim = keys.shape
    seq_index = lax.axis_index("seq")
    odd = seq_index % 2 == 1
    planes = lax.axis_size("adapter")
    chips = row_n_seq // 2
    outer = lax.axis_size("seq") // row_n_seq

    own = jnp.stack([keys, values])
    far = moved(own, 1, 3)
    mid = moved(own, 2, 2)
    low = jnp.einsum(
        "tbu,tyu->tby", hidden, adapter_down_weight, preferred_element_type=jnp.float32
    ).astype(jnp.bfloat16)
    where = jnp.concatenate([seq_index[None].astype(jnp.int32), lengths])
    rel = (offsets - seq_index * stretch_n).reshape(1, adapt_n * row_n)
    mid, low, where, rel = lax.optimization_barrier((mid, low, where, rel))
    swap = moved(mid, 1, -1)
    own_part, mid_part, far_part, swap_part, keep, send = attention_grads(
        where,
        rel,
        response_base_queries,
        attention_output_gradient,
        low,
        adapter_up_weight,
        own,
        mid,
        far,
        swap,
        hidden,
        chips,
        outer,
    )
    far_back = moved(far_part, -3, -1)
    swap_back = moved(swap_part, 1, -1)
    mid_part = (mid_part + swap_back.astype(jnp.float32)).astype(jnp.bfloat16)
    mid_back = moved(mid_part, -2, -2)

    n_down = chips * outer
    lanes = keep.shape[2]
    at_core = keep + moved(send, 1, -1).astype(jnp.float32)
    at_core = at_core.astype(jnp.bfloat16)
    up_copies = jnp.broadcast_to(at_core[None, n_down:], (chips, chips) + at_core.shape[1:])
    at_core = jnp.concatenate(
        [at_core[:n_down].reshape(chips, outer, adapt_n * rank, lanes), up_copies], axis=1
    )
    along_x = [[(g * chips + x) * 2 + c for x in range(chips)] for g in range(outer) for c in range(2)]
    at_chip = grouped(at_core, along_x)
    at_chip, far_back = lax.optimization_barrier((at_chip, far_back))
    at_chip = at_chip.astype(jnp.float32).sum(0).astype(jnp.bfloat16)
    up_copies = jnp.broadcast_to(at_chip[None, outer:], (outer, chips) + at_chip.shape[1:])
    at_chip = jnp.concatenate([at_chip[:outer, None], up_copies], axis=1)
    across = [[g * row_n_seq + i for g in range(outer)] for i in range(row_n_seq)]
    summed = grouped(at_chip, across)
    prompt = own_part + far_back.astype(jnp.float32) + mid_back.astype(jnp.float32)
    prompt = prompt.reshape(2, planes, stretch_n // planes, head_dim)
    plane = lax.axis_index("adapter")
    total = lax.dynamic_index_in_dim(prompt, plane, 1, False)
    shares = []
    for other in range(1, planes):
        share = lax.dynamic_index_in_dim(prompt, plane ^ other, 1, False).astype(jnp.bfloat16)
        shares.append(lax.ppermute(share, "adapter", [(a, a ^ other) for a in range(planes)]))
    summed, shares = lax.optimization_barrier((summed, shares))
    prompt = total + sum(share.astype(jnp.float32) for share in shares)
    summed = summed.astype(jnp.float32).sum(0)

    down = summed[0].reshape(adapt_n, rank, lanes)
    up_mine = summed[1:]
    up_other = moved(up_mine, 1, -1)
    up_blocks = jnp.concatenate(
        [jnp.where(odd, up_other, up_mine), jnp.where(odd, up_mine, up_other)], axis=0
    )
    up_blocks = up_blocks.reshape(2 * chips, adapt_n, rank, lanes).transpose(1, 2, 0, 3)
    return (
        down,
        up_blocks.reshape(adapt_n, rank, feature_n),
        prompt[0],
        prompt[1],
    )


def solution(mesh):
    return jax.shard_map(
        local,
        mesh=mesh,
        in_specs=(
            P("adapter", "seq", None),
            P("adapter", "seq", None),
            P("adapter", "seq", None),
            P("seq", None),
            P("seq", None),
            P("adapter", None, None),
            P("adapter", None, None),
            P("adapter"),
            P("adapter", "seq"),
        ),
        out_specs=(
            P("adapter", None, "seq"),
            P("adapter", None, None),
            P(("seq", "adapter"), None),
            P(("seq", "adapter"), None),
        ),
        check_vma=False,
    )
```

time: 121 us -> 115 us (0.950)
  the two profiles are of different devices: /device:TPU:1 before, /device:TPU:25 now
where the time goes in v3:
time: 115 us
  starting transfers between devices  36.5 us (32%)
  waiting for transfers between devices  33.8 us (29%)
  Pallas kernels  28.9 us (25%)
  other arithmetic  7.79 us (7%)
  matrix products  4.03 us (4%)
  local copies, waits for them, and re-layouts  2.88 us (3%)
    ppermute x8, waiting for transfers between devices, moved(): return lax.ppermute(value, both_axes, pairs)  28.9 us
    pallas_call x1, Pallas kernels, attention_grads(): pl.pallas_call(body, grid_spec=pltpu.PrefetchScalarGridSpec(num_scalar_pr...  28.9 us
    ppermute x8, starting transfers between devices, moved(): return lax.ppermute(value, both_axes, pairs)  22.6 us
    all_to_all x2, starting transfers between devices, grouped(): lax.all_to_all(value, 'seq', 0, 0, axis_index_groups=groups, tiled=True)  10.3 us
    ppermute x3, waiting for transfers between devices, local(): lax.ppermute(share, 'adapter', [(a, a ^ other) for a in range(planes)])  4.84 us
    dot_general x1, matrix products, local(): jnp.einsum('tbu,tyu->tby', hidden, adapter_down_weight, preferred_element...  4.03 us
    ppermute x3, starting transfers between devices, local(): lax.ppermute(share, 'adapter', [(a, a ^ other) for a in range(planes)])  3.63 us
  transfers between devices with their start and end apart: 13, of which 5 were waited for; matrix products, arithmetic and copies ran while one was open for 11% of the time, Pallas kernels for 0%

profile of v3, /device:TPU:25, one launch (start us, length us, event | category | flops | bytes accessed | tf_op | source)
XLA Modules:
  0.0 114.7 jit_solution(13550765544086473443)
XLA Ops:
  0.6 0.0 copy-start
  0.6 1.1 pad_maximum_fusion.own_in
  1.8 0.0 copy-start.1
  1.8 3.1 %collective-permute-start = (bf16[2,768,128]{2,1,0:T(8,128)(2,1)S(1)}, bf16[2,768,128]{2,1,0:T(8,128)(2,1)S(1)}, u32[]{:S(2)}, u32[]{:S(2)}) collective-permute-start(bf16[2,768,128]{2,1,0:T(8,128)(2,1)S(1)} %pad_maximum_fusion.own_in), channel_id=1, source_target_pairs={{0,8},{1,9},{2,10},{3,11},{4,12},{5,13},{6,14},{7,15},{8,16},{9,17... | collective-permute-start | bytes 1179656 | tf_op jit(solution)/shard_map/ppermute | solution.py:33
  4.9 5.2 %collective-permute-start.1 = (bf16[2,768,128]{2,1,0:T(8,128)(2,1)S(1)}, bf16[2,768,128]{2,1,0:T(8,128)(2,1)S(1)}, u32[]{:S(2)}, u32[]{:S(2)}) collective-permute-start(bf16[2,768,128]{2,1,0:T(8,128)(2,1)S(1)} %pad_maximum_fusion.own_in), channel_id=1, source_target_pairs={{0,4},{1,5},{2,6},{3,7},{4,16},{5,17},{6,18},{7,19},{8,12},{9,13},... | collective-permute-start | bytes 1179656 | tf_op jit(solution)/shard_map/ppermute | solution.py:33
  10.1 1.2 %broadcast_subtract_fusion = s32[2,128]{1,0:T(2,128)} fusion(s32[2,128]{1,0:T(2,128)} %param.17, s32[]{:T(128)S(6)} %mul.3), kind=kLoop, calls=%fused_computation.23 | loop fusion | flops 256 | bytes 2052 | tf_op jit(solution)/shard_map/sub | solution.py:291
  11.4 1.2 %pad_add_fusion.where_ref = s32[3]{0:T(128)} fusion(s32[2]{0:T(128)} %param.16, s32[1]{0:T(128)} %bitcast.2), kind=kLoop, calls=%fused_computation.22 | loop fusion | flops 3 | bytes 24 | tf_op jit(solution)/shard_map/concatenate | solution.py:290
  12.6 0.0 copy-done
  12.6 4.0 %convolution_convert_fusion.low_ref = bf16[2,128,16]{2,1,0:T(8,128)(2,1)} fusion(bf16[2,128,8192]{2,1,0:T(8,128)(2,1)} %hidden_in.1, bf16[2,16,8192]{2,1,0:T(8,128)(2,1)S(1)} %copy-done), kind=kOutput, calls=%fused_computation | convolution fusion | flops 67112960 | bytes 4726784 | tf_op jit(solution)/shard_map/tbu,tyu->tby/dot_general | solution.py:287
  16.6 16.8 %collective-permute-done.mid_in = bf16[2,768,128]{2,1,0:T(8,128)(2,1)S(1)} collective-permute-done((bf16[2,768,128]{2,1,0:T(8,128)(2,1)S(1)}, bf16[2,768,128]{2,1,0:T(8,128)(2,1)S(1)}, u32[]{:S(2)}, u32[]{:S(2)}) %collective-permute-start) | collective-permute-done | bytes 393248 | tf_op jit(solution)/shard_map/ppermute | solution.py:33
  33.4 0.0 copy-start.3
  33.4 1.4 %collective-permute-start.2 = (bf16[2,768,128]{2,1,0:T(8,128)(2,1)S(1)}, bf16[2,768,128]{2,1,0:T(8,128)(2,1)S(1)}, u32[]{:S(2)}, u32[]{:S(2)}) collective-permute-start(bf16[2,768,128]{2,1,0:T(8,128)(2,1)S(1)} %collective-permute-done.mid_in), channel_id=1, source_target_pairs={{0,4},{1,5},{2,6},{3,7},{4,0},{5,1},{6,2},{7,3},{8,12},{9,13},{10,... | collective-permute-start | bytes 1179656 | tf_op jit(solution)/shard_map/ppermute | solution.py:33
  34.9 0.0 collective-permute-done.1.far_in
  34.9 0.0 copy-start.4
  34.9 1.3 %collective-permute-done.2.swap_in = bf16[2,768,128]{2,1,0:T(8,128)(2,1)S(1)} collective-permute-done((bf16[2,768,128]{2,1,0:T(8,128)(2,1)S(1)}, bf16[2,768,128]{2,1,0:T(8,128)(2,1)S(1)}, u32[]{:S(2)}, u32[]{:S(2)}) %collective-permute-start.2) | collective-permute-done | bytes 393248 | tf_op jit(solution)/shard_map/ppermute | solution.py:33
  36.2 0.0 copy-done.1
  36.2 0.0 copy-done.3
  36.2 0.0 copy-done.4
  36.2 0.0 copy-start.5
  36.2 0.8 copy-done.5
  37.0 28.9 %attention_grads.1 = (f32[2,768,128]{2,1,0:T(8,128)}, f32[2,768,128]{2,1,0:T(8,128)}, bf16[2,768,128]{2,1,0:T(8,128)(2,1)}, bf16[2,768,128]{2,1,0:T(8,128)(2,1)}...) custom-call(s32[3]{0:T(128)} %pad_add_fusion.where_ref, s32[1,256]{1,0:T(1,128)} %bitcast.50, ...), custom_call_target="tpu_custom_call" | custom-call | tf_op jit(solution)/shard_map/attention_grads/pallas_call | solution.py:221
  65.9 0.0 copy-start.2
  65.9 0.4 collective-permute-start.3
  66.3 0.1 collective-permute-start.5
  66.5 2.3 %collective-permute-start.4 = (bf16[2,768,128]{2,1,0:T(8,128)(2,1)}, bf16[2,768,128]{2,1,0:T(8,128)(2,1)S(1)}, u32[]{:S(2)}, u32[]{:S(2)}) collective-permute-start(bf16[2,768,128]{2,1,0:T(8,128)(2,1)} %get-tuple-element.26), channel_id=1, source_target_pairs={{4,0},{5,1},{6,2},{7,3},{12,8},{13,9},{14,10},{15,11},{16,4},{17,5... | collective-permute-start | bytes 1179656 | tf_op jit(solution)/shard_map/ppermute | solution.py:33
  68.7 0.0 collective-permute-done.3
  68.7 1.1 %add_convert_fusion.1 = bf16[36,32,128]{2,1,0:T(8,128)(2,1)S(1)} fusion(f32[36,32,128]{2,1,0:T(8,128)} %get-tuple-element.24, bf16[36,32,128]{2,1,0:T(8,128)(2,1)S(1)} %collective-permute-done.3), kind=kLoop, calls=%fused_computation.4 | loop fusion | flops 442368 | bytes 1179648 | tf_op jit(solution)/shard_map/convert_element_type | solution.py:317
  70.0 0.8 pad_maximum_fusion.1
  70.8 4.5 %all-to-all-start = ((bf16[4,12,32,128]{3,2,1,0:T(8,128)(2,1)}), bf16[4,12,32,128]{3,2,1,0:T(8,128)(2,1)S(1)}, u32[]{:S(2)}, u32[]{:S(2)}) async-start(bf16[4,12,32,128]{3,2,1,0:T(8,128)(2,1)} %pad_maximum_fusion.1), calls=%async_computation | async-start | bytes 786432 | tf_op jit(solution)/shard_map/all_to_all | solution.py:37
  75.3 0.0 collective-permute-done.5
  75.3 1.2 %add_convert_fusion = bf16[2,768,128]{2,1,0:T(8,128)(2,1)S(1)} fusion(f32[2,768,128]{2,1,0:T(8,128)} %get-tuple-element.30, bf16[2,768,128]{2,1,0:T(8,128)(2,1)S(1)} %collective-permute-done.5), kind=kLoop, calls=%fused_computation.2 | loop fusion | flops 589824 | bytes 1572864 | tf_op jit(solution)/shard_map/convert_element_type | solution.py:311
  76.5 6.9 %collective-permute-start.6 = (bf16[2,768,128]{2,1,0:T(8,128)(2,1)S(1)}, bf16[2,768,128]{2,1,0:T(8,128)(2,1)S(1)}, u32[]{:S(2)}, u32[]{:S(2)}) collective-permute-start(bf16[2,768,128]{2,1,0:T(8,128)(2,1)S(1)} %add_convert_fusion), channel_id=1, source_target_pairs={{8,0},{9,1},{10,2},{11,3},{12,4},{13,5},{14,6},{15,7},{16,8},{17,9... | collective-permute-start | bytes 1179656 | tf_op jit(solution)/shard_map/ppermute | solution.py:33
  83.4 0.0 collective-permute-done.4
  83.4 0.0 all-to-all-done
  83.4 0.1 reduce_sum.21
  83.6 0.8 pad_maximum_fusion.2
  84.3 5.7 %all-to-all-start.1 = ((bf16[8,5,32,128]{3,2,1,0:T(8,128)(2,1)}), bf16[8,5,32,128]{3,2,1,0:T(8,128)(2,1)S(1)}, u32[]{:S(2)}, u32[]{:S(2)}) async-start(bf16[8,5,32,128]{3,2,1,0:T(8,128)(2,1)} %pad_maximum_fusion.2), calls=%async_computation.1 | async-start | bytes 655360 | tf_op jit(solution)/shard_map/all_to_all | solution.py:37
  90.1 10.8 %collective-permute-done.6 = bf16[2,768,128]{2,1,0:T(8,128)(2,1)S(1)} collective-permute-done((bf16[2,768,128]{2,1,0:T(8,128)(2,1)S(1)}, bf16[2,768,128]{2,1,0:T(8,128)(2,1)S(1)}, u32[]{:S(2)}, u32[]{:S(2)}) %collective-permute-start.6) | collective-permute-done | bytes 393248 | tf_op jit(solution)/shard_map/ppermute | solution.py:33
  100.9 0.0 copy-done.2
  100.9 0.1 convert_add_fusion
  101.0 0.1 fusion.2
  101.0 0.1 collective-permute-start.7
  101.1 1.9 %collective-permute-start.8 = (bf16[2,192,128]{2,1,0:T(8,128)(2,1)S(1)}, bf16[2,192,128]{2,1,0:T(8,128)(2,1)S(1)}, u32[]{:S(2)}, u32[]{:S(2)}) collective-permute-start(bf16[2,192,128]{2,1,0:T(8,128)(2,1)S(1)} %get-tuple-element.37), channel_id=1, source_target_pairs={{0,2},{1,3},{2,0},{3,1},{4,6},{5,7},{6,4},{7,5},{8,10},{9,11},{10,... | collective-permute-start | bytes 294920 | tf_op jit(solution)/shard_map/ppermute | solution.py:337
  103.0 1.6 %collective-permute-start.9 = (bf16[2,192,128]{2,1,0:T(8,128)(2,1)S(1)}, bf16[2,192,128]{2,1,0:T(8,128)(2,1)S(1)}, u32[]{:S(2)}, u32[]{:S(2)}) collective-permute-start(bf16[2,192,128]{2,1,0:T(8,128)(2,1)S(1)} %get-tuple-element.36), channel_id=1, source_target_pairs={{0,3},{1,2},{2,1},{3,0},{4,7},{5,6},{6,5},{7,4},{8,11},{9,10},{10,... | collective-permute-start | bytes 294920 | tf_op jit(solution)/shard_map/ppermute | solution.py:337
  104.7 1.5 %collective-permute-done.7 = bf16[2,192,128]{2,1,0:T(8,128)(2,1)S(1)} collective-permute-done((bf16[2,192,128]{2,1,0:T(8,128)(2,1)S(1)}, bf16[2,192,128]{2,1,0:T(8,128)(2,1)S(1)}, u32[]{:S(2)}, u32[]{:S(2)}) %collective-permute-start.7) | collective-permute-done | bytes 98336 | tf_op jit(solution)/shard_map/ppermute | solution.py:337
  106.2 0.0 collective-permute-done.8
  106.2 3.3 %collective-permute-done.9 = bf16[2,192,128]{2,1,0:T(8,128)(2,1)S(1)} collective-permute-done((bf16[2,192,128]{2,1,0:T(8,128)(2,1)S(1)}, bf16[2,192,128]{2,1,0:T(8,128)(2,1)S(1)}, u32[]{:S(2)}, u32[]{:S(2)}) %collective-permute-start.9) | collective-permute-done | bytes 98336 | tf_op jit(solution)/shard_map/ppermute | solution.py:337
  109.5 0.0 all-to-all-done.1
  109.6 3.1 %collective-permute-start.10 = (f32[4,32,128]{2,1,0:T(8,128)S(1)}, f32[4,32,128]{2,1,0:T(8,128)S(1)}, u32[]{:S(2)}, u32[]{:S(2)}) collective-permute-start(f32[4,32,128]{2,1,0:T(8,128)S(1)} %slice.37), channel_id=1, source_target_pairs={{0,4},{1,5},{2,6},{3,7},{4,0},{5,1},{6,2},{7,3},{8,12},{9,13},{10,... | collective-permute-start | bytes 196616 | tf_op jit(solution)/shard_map/ppermute | solution.py:33
  112.7 0.7 slice_bitcast_fusion
  113.4 0.6 slice.36
  114.0 0.0 collective-permute-done.10
  114.1 0.7 copy.30
  (11 shorter events, 0.2 us)
Async XLA Ops:
  0.6 12.0 %copy-start = (bf16[2,16,8192]{2,1,0:T(8,128)(2,1)S(1)}, bf16[2,16,8192]{2,1,0:T(8,128)(2,1)}, u32[]{:S(2)}) copy-start(bf16[2,16,8192]{2,1,0:T(8,128)(2,1)} %param.14) | copy-start | bytes 1572868
  1.8 34.4 %copy-start.1 = (bf16[2,768,128]{2,1,0:T(8,128)(2,1)}, bf16[2,768,128]{2,1,0:T(8,128)(2,1)S(1)}, u32[]{:S(2)}) copy-start(bf16[2,768,128]{2,1,0:T(8,128)(2,1)S(1)} %pad_maximum_fusion.own_in) | copy-start | bytes 1179652
  1.8 31.6 %collective-permute-start = (bf16[2,768,128]{2,1,0:T(8,128)(2,1)S(1)}, bf16[2,768,128]{2,1,0:T(8,128)(2,1)S(1)}, u32[]{:S(2)}, u32[]{:S(2)}) collective-permute-start(bf16[2,768,128]{2,1,0:T(8,128)(2,1)S(1)} %pad_maximum_fusion.own_in), channel_id=1, source_target_pairs={{0,8},{1,9},{2,10},{3,11},{4,12},{5,13},{6,14},{7,15},{8,16},{9,17... | collective-permute-start | bytes 1179656 | tf_op jit(solution)/shard_map/ppermute | solution.py:33
  4.9 30.0 %collective-permute-start.1 = (bf16[2,768,128]{2,1,0:T(8,128)(2,1)S(1)}, bf16[2,768,128]{2,1,0:T(8,128)(2,1)S(1)}, u32[]{:S(2)}, u32[]{:S(2)}) collective-permute-start(bf16[2,768,128]{2,1,0:T(8,128)(2,1)S(1)} %pad_maximum_fusion.own_in), channel_id=1, source_target_pairs={{0,4},{1,5},{2,6},{3,7},{4,16},{5,17},{6,18},{7,19},{8,12},{9,13},... | collective-permute-start | bytes 1179656 | tf_op jit(solution)/shard_map/ppermute | solution.py:33
  33.4 2.8 %copy-start.3 = (bf16[2,768,128]{2,1,0:T(8,128)(2,1)}, bf16[2,768,128]{2,1,0:T(8,128)(2,1)S(1)}, u32[]{:S(2)}) copy-start(bf16[2,768,128]{2,1,0:T(8,128)(2,1)S(1)} %collective-permute-done.mid_in) | copy-start | bytes 1179652
  33.4 2.8 %collective-permute-start.2 = (bf16[2,768,128]{2,1,0:T(8,128)(2,1)S(1)}, bf16[2,768,128]{2,1,0:T(8,128)(2,1)S(1)}, u32[]{:S(2)}, u32[]{:S(2)}) collective-permute-start(bf16[2,768,128]{2,1,0:T(8,128)(2,1)S(1)} %collective-permute-done.mid_in), channel_id=1, source_target_pairs={{0,4},{1,5},{2,6},{3,7},{4,0},{5,1},{6,2},{7,3},{8,12},{9,13},{10,... | collective-permute-start | bytes 1179656 | tf_op jit(solution)/shard_map/ppermute | solution.py:33
  34.9 1.4 %copy-start.4 = (bf16[2,768,128]{2,1,0:T(8,128)(2,1)}, bf16[2,768,128]{2,1,0:T(8,128)(2,1)S(1)}, u32[]{:S(2)}) copy-start(bf16[2,768,128]{2,1,0:T(8,128)(2,1)S(1)} %collective-permute-done.1.far_in) | copy-start | bytes 1179652
  36.2 0.8 copy-start.5
  65.9 35.0 %copy-start.2 = (f32[2,768,128]{2,1,0:T(8,128)S(1)}, f32[2,768,128]{2,1,0:T(8,128)}, u32[]{:S(2)}) copy-start(f32[2,768,128]{2,1,0:T(8,128)} %get-tuple-element.28) | copy-start | bytes 2359300
  65.9 2.9 %collective-permute-start.3 = (bf16[36,32,128]{2,1,0:T(8,128)(2,1)}, bf16[36,32,128]{2,1,0:T(8,128)(2,1)S(1)}, u32[]{:S(2)}, u32[]{:S(2)}) collective-permute-start(bf16[36,32,128]{2,1,0:T(8,128)(2,1)} %get-tuple-element.25), channel_id=1, source_target_pairs={{0,4},{1,5},{2,6},{3,7},{4,0},{5,1},{6,2},{7,3},{8,12},{9,13},{10,... | collective-permute-start | bytes 884744 | tf_op jit(solution)/shard_map/ppermute | solution.py:33
  66.3 9.0 %collective-permute-start.5 = (bf16[2,768,128]{2,1,0:T(8,128)(2,1)}, bf16[2,768,128]{2,1,0:T(8,128)(2,1)S(1)}, u32[]{:S(2)}, u32[]{:S(2)}) collective-permute-start(bf16[2,768,128]{2,1,0:T(8,128)(2,1)} %get-tuple-element.31), channel_id=1, source_target_pairs={{0,4},{1,5},{2,6},{3,7},{4,0},{5,1},{6,2},{7,3},{8,12},{9,13},{10,... | collective-permute-start | bytes 1179656 | tf_op jit(solution)/shard_map/ppermute | solution.py:33
  66.5 16.9 %collective-permute-start.4 = (bf16[2,768,128]{2,1,0:T(8,128)(2,1)}, bf16[2,768,128]{2,1,0:T(8,128)(2,1)S(1)}, u32[]{:S(2)}, u32[]{:S(2)}) collective-permute-start(bf16[2,768,128]{2,1,0:T(8,128)(2,1)} %get-tuple-element.26), channel_id=1, source_target_pairs={{4,0},{5,1},{6,2},{7,3},{12,8},{13,9},{14,10},{15,11},{16,4},{17,5... | collective-permute-start | bytes 1179656 | tf_op jit(solution)/shard_map/ppermute | solution.py:33
  70.8 12.7 %all-to-all-start = ((bf16[4,12,32,128]{3,2,1,0:T(8,128)(2,1)}), bf16[4,12,32,128]{3,2,1,0:T(8,128)(2,1)S(1)}, u32[]{:S(2)}, u32[]{:S(2)}) async-start(bf16[4,12,32,128]{3,2,1,0:T(8,128)(2,1)} %pad_maximum_fusion.1), calls=%async_computation | async-start | bytes 786432 | tf_op jit(solution)/shard_map/all_to_all | solution.py:37
  76.5 24.3 %collective-permute-start.6 = (bf16[2,768,128]{2,1,0:T(8,128)(2,1)S(1)}, bf16[2,768,128]{2,1,0:T(8,128)(2,1)S(1)}, u32[]{:S(2)}, u32[]{:S(2)}) collective-permute-start(bf16[2,768,128]{2,1,0:T(8,128)(2,1)S(1)} %add_convert_fusion), channel_id=1, source_target_pairs={{8,0},{9,1},{10,2},{11,3},{12,4},{13,5},{14,6},{15,7},{16,8},{17,9... | collective-permute-start | bytes 1179656 | tf_op jit(solution)/shard_map/ppermute | solution.py:33
  84.3 25.2 %all-to-all-start.1 = ((bf16[8,5,32,128]{3,2,1,0:T(8,128)(2,1)}), bf16[8,5,32,128]{3,2,1,0:T(8,128)(2,1)S(1)}, u32[]{:S(2)}, u32[]{:S(2)}) async-start(bf16[8,5,32,128]{3,2,1,0:T(8,128)(2,1)} %pad_maximum_fusion.2), calls=%async_computation.1 | async-start | bytes 655360 | tf_op jit(solution)/shard_map/all_to_all | solution.py:37
  101.0 5.1 %collective-permute-start.7 = (bf16[2,192,128]{2,1,0:T(8,128)(2,1)S(1)}, bf16[2,192,128]{2,1,0:T(8,128)(2,1)S(1)}, u32[]{:S(2)}, u32[]{:S(2)}) collective-permute-start(bf16[2,192,128]{2,1,0:T(8,128)(2,1)S(1)} %get-tuple-element.38), channel_id=1, source_target_pairs={{0,1},{1,0},{2,3},{3,2},{4,5},{5,4},{6,7},{7,6},{8,9},{9,8},{10,11... | collective-permute-start | bytes 294920 | tf_op jit(solution)/shard_map/ppermute | solution.py:337
  101.1 5.0 %collective-permute-start.8 = (bf16[2,192,128]{2,1,0:T(8,128)(2,1)S(1)}, bf16[2,192,128]{2,1,0:T(8,128)(2,1)S(1)}, u32[]{:S(2)}, u32[]{:S(2)}) collective-permute-start(bf16[2,192,128]{2,1,0:T(8,128)(2,1)S(1)} %get-tuple-element.37), channel_id=1, source_target_pairs={{0,2},{1,3},{2,0},{3,1},{4,6},{5,7},{6,4},{7,5},{8,10},{9,11},{10,... | collective-permute-start | bytes 294920 | tf_op jit(solution)/shard_map/ppermute | solution.py:337
  103.0 6.5 %collective-permute-start.9 = (bf16[2,192,128]{2,1,0:T(8,128)(2,1)S(1)}, bf16[2,192,128]{2,1,0:T(8,128)(2,1)S(1)}, u32[]{:S(2)}, u32[]{:S(2)}) collective-permute-start(bf16[2,192,128]{2,1,0:T(8,128)(2,1)S(1)} %get-tuple-element.36), channel_id=1, source_target_pairs={{0,3},{1,2},{2,1},{3,0},{4,7},{5,6},{6,5},{7,4},{8,11},{9,10},{10,... | collective-permute-start | bytes 294920 | tf_op jit(solution)/shard_map/ppermute | solution.py:337
  109.6 4.5 %collective-permute-start.10 = (f32[4,32,128]{2,1,0:T(8,128)S(1)}, f32[4,32,128]{2,1,0:T(8,128)S(1)}, u32[]{:S(2)}, u32[]{:S(2)}) collective-permute-start(f32[4,32,128]{2,1,0:T(8,128)S(1)} %slice.37), channel_id=1, source_target_pairs={{0,4},{1,5},{2,6},{3,7},{4,0},{5,1},{6,2},{7,3},{8,12},{9,13},{10,... | collective-permute-start | bytes 196616 | tf_op jit(solution)/shard_map/ppermute | solution.py:33

commit v4 on v3

--- a/solution.py
+++ b/solution.py
@@ -33,6 +33,44 @@
     return lax.ppermute(value, both_axes, pairs)
 
 
+def moved_two_ahead(value):
+    peers, planes = lax.axis_size("seq"), lax.axis_size("adapter")
+    last = row_n_seq - 2
+    onward, over = [], []
+    for s in range(peers):
+        t = s - last if s % row_n_seq >= last else s + 2
+        for a in range(planes):
+            onward.append((s * planes + a, t * planes + a))
+            if s % row_n_seq < 2 and s + row_n_seq < peers:
+                over.append((s * planes + a, (s + row_n_seq) * planes + planes - 1 - a))
+    value = lax.ppermute(value, both_axes, onward)
+    relayed = lax.ppermute(value, both_axes, over)
+    return jnp.where(lax.axis_index("seq") % row_n_seq < 2, relayed, value)
+
+
+def round_x_back(value):
+    peers, planes = lax.axis_size("seq"), lax.axis_size("adapter")
+    last = row_n_seq - 2
+    pairs = []
+    for s in range(peers):
+        t = s + last if s % row_n_seq < 2 else s - 2
+        pairs += [(s * planes + a, t * planes + a) for a in range(planes)]
+    return lax.ppermute(value, both_axes, pairs)
+
+
+def along_z_back(value):
+    peers, planes = lax.axis_size("seq"), lax.axis_size("adapter")
+    last = row_n_seq - 2
+    pairs = [
+        (s * planes + a, (s - row_n_seq) * planes + planes - 1 - a)
+        for s in range(row_n_seq, peers)
+        if s % row_n_seq >= last
+        for a in range(planes)
+    ]
+    relayed = lax.ppermute(value, both_axes, pairs)
+    return jnp.where(lax.axis_index("seq") % row_n_seq >= last, relayed, value)
+
+
 def grouped(value, groups):
     return lax.all_to_all(value, "seq", 0, 0, axis_index_groups=groups, tiled=True)
 
@@ -48,7 +86,7 @@
 
 
 def attention_kernel(
-    where_ref, rel_ref, base_ref, grad_ref, low_ref, up_ref, up_whole_ref, own_in, mid_in, far_in, swap_in, hidden_in,
+    where_ref, rel_ref, base_ref, grad_ref, low_ref, up_ref, up_whole_ref, own_in, mid_k_in, mid_v_in, far_in, swap_k_in, swap_v_in, hidden_in,
     own_ref, mid_ref, far_ref, swap_ref, keep_ref, send_ref,
     window_k, window_v, key_t, score, dprob, dscore_low, acc_k, acc_v, hidden, dquery, pieces, block_sems, hidden_sem,
     *, stretch, chunk, rows, adapters, head_dim, heads, per_step, rank, chips, outer,
@@ -63,10 +101,15 @@
     swap_slot = 1 + 2 * odd
 
     def fills():
-        sources = ((0, own_in), (2, mid_in), (far_slot, far_in), (swap_slot, swap_in))
-        for i, (slot, source) in enumerate(sources):
-            yield pltpu.make_async_copy(source.at[0], window_k.at[slot], block_sems.at[2 * i])
-            yield pltpu.make_async_copy(source.at[1], window_v.at[slot], block_sems.at[2 * i + 1])
+        sources = (
+            (0, own_in.at[0], own_in.at[1]),
+            (2, mid_k_in, mid_v_in),
+            (far_slot, far_in.at[0], far_in.at[1]),
+            (swap_slot, swap_k_in, swap_v_in),
+        )
+        for i, (slot, source_k, source_v) in enumerate(sources):
+            yield pltpu.make_async_copy(source_k, window_k.at[slot], block_sems.at[2 * i])
+            yield pltpu.make_async_copy(source_v, window_v.at[slot], block_sems.at[2 * i + 1])
 
     hidden_copy = pltpu.make_async_copy(hidden_in, hidden, hidden_sem)
 
@@ -194,7 +237,7 @@
     return pl.BlockSpec(shape, lambda h, w: (0,) * len(shape))
 
 
-def attention_grads(where, rel, base, grad, low, up, own, mid, far, swap, hidden, chips, outer):
+def attention_grads(where, rel, base, grad, low, up, own, mids, far, swaps, hidden, chips, outer):
     adapters, rows, features = base.shape
     _, stretch, head_dim = own.shape
     heads = features // head_dim
@@ -231,7 +274,7 @@
                 pl.BlockSpec((adapters, rank, per_step * head_dim), lambda h, w: (0, 0, h)),
                 whole(adapters, rank, features),
             ]
-            + [anywhere] * 5,
+            + [anywhere] * 7,
             out_specs=[whole(*pair)] * 4 + [whole(*blocks)] * 2,
             scratch_shapes=[
                 pltpu.VMEM((4, stretch, head_dim), jnp.bfloat16),
@@ -258,7 +301,7 @@
             dimension_semantics=("arbitrary",), vmem_limit_bytes=58 * 1024 * 1024
         ),
         name="attention_grads",
-    )(where, rel, base, grad, low, up, up, own, mid, far, swap, hidden)
+    )(where, rel, base, grad, low, up, up, own, *mids, far, *swaps, hidden)
 
 
 def local(
@@ -283,14 +326,14 @@
 
     own = jnp.stack([keys, values])
     far = moved(own, 1, 3)
-    mid = moved(own, 2, 2)
+    mid_k, mid_v = moved(keys, 2, 2), moved_two_ahead(values)
     low = jnp.einsum(
         "tbu,tyu->tby", hidden, adapter_down_weight, preferred_element_type=jnp.float32
     ).astype(jnp.bfloat16)
     where = jnp.concatenate([seq_index[None].astype(jnp.int32), lengths])
     rel = (offsets - seq_index * stretch_n).reshape(1, adapt_n * row_n)
-    mid, low, where, rel = lax.optimization_barrier((mid, low, where, rel))
-    swap = moved(mid, 1, -1)
+    mid_k, low, where, rel = lax.optimization_barrier((mid_k, low, where, rel))
+    swap_k, swap_v = moved(mid_k, 1, -1), moved(mid_v, 1, -1)
     own_part, mid_part, far_part, swap_part, keep, send = attention_grads(
         where,
         rel,
@@ -299,17 +342,19 @@
         low,
         adapter_up_weight,
         own,
-        mid,
+        (mid_k, mid_v),
         far,
-        swap,
+        (swap_k, swap_v),
         hidden,
         chips,
         outer,
     )
     far_back = moved(far_part, -3, -1)
     swap_back = moved(swap_part, 1, -1)
-    mid_part = (mid_part + swap_back.astype(jnp.float32)).astype(jnp.bfloat16)
-    mid_back = moved(mid_part, -2, -2)
+    mid_dk = (mid_part[0] + swap_back[0].astype(jnp.float32)).astype(jnp.bfloat16)
+    mid_dv = (mid_part[1] + swap_back[1].astype(jnp.float32)).astype(jnp.bfloat16)
+    mid_dv = round_x_back(mid_dv)
+    mid_dk = moved(mid_dk, -2, -2)
 
     n_down = chips * outer
     lanes = keep.shape[2]
@@ -321,7 +366,8 @@
     )
     along_x = [[(g * chips + x) * 2 + c for x in range(chips)] for g in range(outer) for c in range(2)]
     at_chip = grouped(at_core, along_x)
-    at_chip, far_back = lax.optimization_barrier((at_chip, far_back))
+    at_chip, far_back, mid_dv = lax.optimization_barrier((at_chip, far_back, mid_dv))
+    mid_back = jnp.stack([mid_dk, along_z_back(mid_dv)])
     at_chip = at_chip.astype(jnp.float32).sum(0).astype(jnp.bfloat16)
     up_copies = jnp.broadcast_to(at_chip[None, outer:], (outer, chips) + at_chip.shape[1:])
     at_chip = jnp.concatenate([at_chip[:outer, None], up_copies], axis=1)

time: 115 us -> 112 us (0.974)
  the two profiles are of different devices: /device:TPU:25 before, /device:TPU:1 now
where the time goes in v4:
time: 112 us; the launch traced here: 111 us
  starting transfers between devices  45.2 us (40%)
  Pallas kernels  28.9 us (26%)
  waiting for transfers between devices  22.2 us (20%)
  other arithmetic  6.46 us (6%)
  matrix products  4.04 us (4%)
  local copies, waits for them, and re-layouts  2.82 us (3%)
    pallas_call x1, Pallas kernels, attention_grads(): pl.pallas_call(body, grid_spec=pltpu.PrefetchScalarGridSpec(num_scalar_pr...  28.9 us
    ppermute x9, starting transfers between devices, moved(): return lax.ppermute(value, both_axes, pairs)  19 us
    all_to_all x2, starting transfers between devices, grouped(): lax.all_to_all(value, 'seq', 0, 0, axis_index_groups=groups, tiled=True)  11.3 us
    ppermute x3, waiting for transfers between devices, local(): lax.ppermute(share, 'adapter', [(a, a ^ other) for a in range(planes)])  8.63 us
    ppermute x1, waiting for transfers between devices, moved_two_ahead(): relayed = lax.ppermute(value, both_axes, over)  7.46 us
    ppermute x1, starting transfers between devices, moved_two_ahead(): relayed = lax.ppermute(value, both_axes, over)  5.74 us
    ppermute x1, waiting for transfers between devices, round_x_back(): return lax.ppermute(value, both_axes, pairs)  4.67 us
    dot_general x1, matrix products, local(): jnp.einsum('tbu,tyu->tby', hidden, adapter_down_weight, preferred_element...  4.04 us
  transfers between devices with their start and end apart: 18, of which 6 were waited for; matrix products, arithmetic and copies ran while one was open for 11% of the time, Pallas kernels for 0%

profile of v4, /device:TPU:1, one launch (start us, length us, event | category | flops | bytes accessed | tf_op | source)
XLA Modules:
  0.0 110.6 jit_solution(2545021081597493690)
XLA Ops:
  0.6 0.0 copy-start
  0.6 0.0 copy-start.9
  0.7 0.0 copy-start.8
  0.7 2.1 %collective-permute-start.1 = (bf16[768,128]{1,0:T(8,128)(2,1)}, bf16[768,128]{1,0:T(8,128)(2,1)S(1)}, u32[]{:S(2)}, u32[]{:S(2)}) collective-permute-start(bf16[768,128]{1,0:T(8,128)(2,1)} %param.13), channel_id=1, source_target_pairs={{0,8},{1,9},{2,10},{3,11},{4,12},{5,13},{6,14},{7,15},{8,16},{9,17... | collective-permute-start | bytes 589832 | tf_op jit(solution)/shard_map/ppermute | solution.py:46
  2.8 3.1 %collective-permute-start = (bf16[768,128]{1,0:T(8,128)(2,1)}, bf16[768,128]{1,0:T(8,128)(2,1)S(1)}, u32[]{:S(2)}, u32[]{:S(2)}) collective-permute-start(bf16[768,128]{1,0:T(8,128)(2,1)} %param.12), channel_id=1, source_target_pairs={{0,8},{1,9},{2,10},{3,11},{4,12},{5,13},{6,14},{7,15},{8,16},{9,17... | collective-permute-start | bytes 589832 | tf_op jit(solution)/shard_map/ppermute | solution.py:33
  5.9 1.1 pad_maximum_fusion.own_in
  7.0 0.0 copy-start.1
  7.0 6.2 %collective-permute-start.3 = (bf16[2,768,128]{2,1,0:T(8,128)(2,1)S(1)}, bf16[2,768,128]{2,1,0:T(8,128)(2,1)S(1)}, u32[]{:S(2)}, u32[]{:S(2)}) collective-permute-start(bf16[2,768,128]{2,1,0:T(8,128)(2,1)S(1)} %pad_maximum_fusion.own_in), channel_id=1, source_target_pairs={{0,4},{1,5},{2,6},{3,7},{4,16},{5,17},{6,18},{7,19},{8,12},{9,13},... | collective-permute-start | bytes 1179656 | tf_op jit(solution)/shard_map/ppermute | solution.py:33
  13.2 0.0 copy-done
  13.2 4.0 %convolution_convert_fusion.low_ref = bf16[2,128,16]{2,1,0:T(8,128)(2,1)} fusion(bf16[2,128,8192]{2,1,0:T(8,128)(2,1)} %hidden_in.1, bf16[2,16,8192]{2,1,0:T(8,128)(2,1)S(1)} %copy-done), kind=kOutput, calls=%fused_computation | convolution fusion | flops 67112960 | bytes 4726784 | tf_op jit(solution)/shard_map/tbu,tyu->tby/dot_general | solution.py:330
  17.2 0.0 copy-done.9
  17.2 0.6 pad_add_fusion.where_ref
  17.8 0.0 collective-permute-done.1
  17.8 5.7 %collective-permute-start.2 = (bf16[768,128]{1,0:T(8,128)(2,1)S(1)}, bf16[768,128]{1,0:T(8,128)(2,1)S(1)}, u32[]{:S(2)}, u32[]{:S(2)}) collective-permute-start(bf16[768,128]{1,0:T(8,128)(2,1)S(1)} %collective-permute-done.1), channel_id=1, source_target_pairs={{0,35},{1,34},{2,33},{3,32},{4,39},{5,38},{6,37},{7,36},{32,67},{3... | collective-permute-start | bytes 589832 | tf_op jit(solution)/shard_map/ppermute | solution.py:47
  23.6 0.0 copy-done.8
  23.6 0.6 broadcast_subtract_fusion
  24.2 0.0 collective-permute-done.mid_k_in
  24.2 0.0 collective-permute-start.4
  24.2 7.5 %collective-permute-done.2 = bf16[768,128]{1,0:T(8,128)(2,1)S(1)} collective-permute-done((bf16[768,128]{1,0:T(8,128)(2,1)S(1)}, bf16[768,128]{1,0:T(8,128)(2,1)S(1)}, u32[]{:S(2)}, u32[]{:S(2)}) %collective-permute-start.2) | collective-permute-done | bytes 196640 | tf_op jit(solution)/shard_map/ppermute | solution.py:47
  31.7 0.0 copy-start.2
  31.7 0.1 collective-permute-start.5
  31.8 0.0 collective-permute-done.4.swap_k_in
  31.8 0.0 copy-start.6
  31.8 0.0 collective-permute-done.3.far_in
  31.8 0.0 copy-start.4
  31.8 1.4 %collective-permute-done.5.swap_v_in = bf16[768,128]{1,0:T(8,128)(2,1)S(1)} collective-permute-done((bf16[768,128]{1,0:T(8,128)(2,1)S(1)}, bf16[768,128]{1,0:T(8,128)(2,1)S(1)}, u32[]{:S(2)}, u32[]{:S(2)}) %collective-permute-start.5) | collective-permute-done | bytes 196640 | tf_op jit(solution)/shard_map/ppermute | solution.py:33
  33.2 0.0 copy-done.1
  33.2 0.0 copy-done.5
  33.2 0.7 copy-done.7
  33.9 28.9 %attention_grads.1 = (f32[2,768,128]{2,1,0:T(8,128)}, f32[2,768,128]{2,1,0:T(8,128)}, bf16[2,768,128]{2,1,0:T(8,128)(2,1)}, bf16[2,768,128]{2,1,0:T(8,128)(2,1)}...) custom-call(s32[3]{0:T(128)} %pad_add_fusion.where_ref, s32[1,256]{1,0:T(1,128)} %bitcast.58, ...), custom_call_target="tpu_custom_call" | custom-call | tf_op jit(solution)/shard_map/attention_grads/pallas_call | solution.py:264
  62.8 0.2 collective-permute-start.6
  63.0 0.4 collective-permute-start.8
  63.4 2.2 %collective-permute-start.7 = (bf16[2,768,128]{2,1,0:T(8,128)(2,1)}, bf16[2,768,128]{2,1,0:T(8,128)(2,1)S(1)}, u32[]{:S(2)}, u32[]{:S(2)}) collective-permute-start(bf16[2,768,128]{2,1,0:T(8,128)(2,1)} %get-tuple-element.27), channel_id=1, source_target_pairs={{4,0},{5,1},{6,2},{7,3},{12,8},{13,9},{14,10},{15,11},{16,4},{17,5... | collective-permute-start | bytes 1179656 | tf_op jit(solution)/shard_map/ppermute | solution.py:33
  65.6 0.0 collective-permute-done.6
  65.6 1.1 %add_convert_fusion = bf16[36,32,128]{2,1,0:T(8,128)(2,1)S(1)} fusion(f32[36,32,128]{2,1,0:T(8,128)} %get-tuple-element.25, bf16[36,32,128]{2,1,0:T(8,128)(2,1)S(1)} %collective-permute-done.6), kind=kLoop, calls=%fused_computation.3 | loop fusion | flops 442368 | bytes 1179648 | tf_op jit(solution)/shard_map/convert_element_type | solution.py:362
  66.8 0.8 pad_maximum_fusion.1
  67.7 3.5 %all-to-all-start = ((bf16[4,12,32,128]{3,2,1,0:T(8,128)(2,1)}), bf16[4,12,32,128]{3,2,1,0:T(8,128)(2,1)S(1)}, u32[]{:S(2)}, u32[]{:S(2)}) async-start(bf16[4,12,32,128]{3,2,1,0:T(8,128)(2,1)} %pad_maximum_fusion.1), calls=%async_computation | async-start | bytes 786432 | tf_op jit(solution)/shard_map/all_to_all | solution.py:75
  71.1 0.0 collective-permute-done.8
  71.1 1.2 %fusion.1 = (bf16[768,128]{1,0:T(8,128)(2,1)S(1)}, bf16[768,128]{1,0:T(8,128)(2,1)S(1)}) fusion(f32[2,768,128]{2,1,0:T(8,128)} %get-tuple-element.28, bf16[2,768,128]{2,1,0:T(8,128)(2,1)S(1)} %collective-permute-done.8), kind=kLoop, calls=%fused_computation.10 | loop fusion | flops 589824 | bytes 1572864 | tf_op jit(solution)/shard_map/convert_element_type | solution.py:354
  72.3 2.7 %collective-permute-start.9 = (bf16[768,128]{1,0:T(8,128)(2,1)S(1)}, bf16[768,128]{1,0:T(8,128)(2,1)S(1)}, u32[]{:S(2)}, u32[]{:S(2)}) collective-permute-start(bf16[768,128]{1,0:T(8,128)(2,1)S(1)} %get-tuple-element.39), channel_id=1, source_target_pairs={{0,24},{1,25},{2,26},{3,27},{4,28},{5,29},{6,30},{7,31},{8,0},{9,1... | collective-permute-start | bytes 589832 | tf_op jit(solution)/shard_map/ppermute | solution.py:58
  75.1 1.3 %collective-permute-start.10 = (bf16[768,128]{1,0:T(8,128)(2,1)S(1)}, bf16[768,128]{1,0:T(8,128)(2,1)S(1)}, u32[]{:S(2)}, u32[]{:S(2)}) collective-permute-start(bf16[768,128]{1,0:T(8,128)(2,1)S(1)} %get-tuple-element.38), channel_id=1, source_target_pairs={{8,0},{9,1},{10,2},{11,3},{12,4},{13,5},{14,6},{15,7},{16,8},{17,9... | collective-permute-start | bytes 589832 | tf_op jit(solution)/shard_map/ppermute | solution.py:33
  76.3 0.0 collective-permute-done.7
  76.3 4.7 %collective-permute-done.9 = bf16[768,128]{1,0:T(8,128)(2,1)S(1)} collective-permute-done((bf16[768,128]{1,0:T(8,128)(2,1)S(1)}, bf16[768,128]{1,0:T(8,128)(2,1)S(1)}, u32[]{:S(2)}, u32[]{:S(2)}) %collective-permute-start.9) | collective-permute-done | bytes 196640 | tf_op jit(solution)/shard_map/ppermute | solution.py:58
  81.0 0.0 all-to-all-done
  81.0 0.7 collective-permute-start.11
  81.7 0.1 reduce_sum.21
  81.8 0.8 pad_maximum_fusion.2
  82.6 7.9 %all-to-all-start.1 = ((bf16[8,5,32,128]{3,2,1,0:T(8,128)(2,1)}), bf16[8,5,32,128]{3,2,1,0:T(8,128)(2,1)S(1)}, u32[]{:S(2)}, u32[]{:S(2)}) async-start(bf16[8,5,32,128]{3,2,1,0:T(8,128)(2,1)} %pad_maximum_fusion.2), calls=%async_computation.1 | async-start | bytes 655360 | tf_op jit(solution)/shard_map/all_to_all | solution.py:75
  90.5 0.0 collective-permute-done.11
  90.5 0.0 collective-permute-done.10
  90.5 0.1 convert_add_fusion
  90.6 0.1 fusion.4
  90.7 0.1 collective-permute-start.12
  90.8 1.9 %collective-permute-start.13 = (bf16[2,192,128]{2,1,0:T(8,128)(2,1)S(1)}, bf16[2,192,128]{2,1,0:T(8,128)(2,1)S(1)}, u32[]{:S(2)}, u32[]{:S(2)}) collective-permute-start(bf16[2,192,128]{2,1,0:T(8,128)(2,1)S(1)} %get-tuple-element.41), channel_id=1, source_target_pairs={{0,2},{1,3},{2,0},{3,1},{4,6},{5,7},{6,4},{7,5},{8,10},{9,11},{10,... | collective-permute-start | bytes 294920 | tf_op jit(solution)/shard_map/ppermute | solution.py:383
  92.7 1.6 %collective-permute-start.14 = (bf16[2,192,128]{2,1,0:T(8,128)(2,1)S(1)}, bf16[2,192,128]{2,1,0:T(8,128)(2,1)S(1)}, u32[]{:S(2)}, u32[]{:S(2)}) collective-permute-start(bf16[2,192,128]{2,1,0:T(8,128)(2,1)S(1)} %get-tuple-element.40), channel_id=1, source_target_pairs={{0,3},{1,2},{2,1},{3,0},{4,7},{5,6},{6,5},{7,4},{8,11},{9,10},{10,... | collective-permute-start | bytes 294920 | tf_op jit(solution)/shard_map/ppermute | solution.py:383
  94.3 2.7 %collective-permute-done.12 = bf16[2,192,128]{2,1,0:T(8,128)(2,1)S(1)} collective-permute-done((bf16[2,192,128]{2,1,0:T(8,128)(2,1)S(1)}, bf16[2,192,128]{2,1,0:T(8,128)(2,1)S(1)}, u32[]{:S(2)}, u32[]{:S(2)}) %collective-permute-start.12) | collective-permute-done | bytes 98336 | tf_op jit(solution)/shard_map/ppermute | solution.py:383
  97.1 0.9 collective-permute-done.13
  98.0 5.0 %collective-permute-done.14 = bf16[2,192,128]{2,1,0:T(8,128)(2,1)S(1)} collective-permute-done((bf16[2,192,128]{2,1,0:T(8,128)(2,1)S(1)}, bf16[2,192,128]{2,1,0:T(8,128)(2,1)S(1)}, u32[]{:S(2)}, u32[]{:S(2)}) %collective-permute-start.14) | collective-permute-done | bytes 98336 | tf_op jit(solution)/shard_map/ppermute | solution.py:383
  103.0 0.0 all-to-all-done.1
  103.0 5.5 %collective-permute-start.15 = (f32[4,32,128]{2,1,0:T(8,128)S(1)}, f32[4,32,128]{2,1,0:T(8,128)S(1)}, u32[]{:S(2)}, u32[]{:S(2)}) collective-permute-start(f32[4,32,128]{2,1,0:T(8,128)S(1)} %slice.55), channel_id=1, source_target_pairs={{0,4},{1,5},{2,6},{3,7},{4,0},{5,1},{6,2},{7,3},{8,12},{9,13},{10,... | collective-permute-start | bytes 196616 | tf_op jit(solution)/shard_map/ppermute | solution.py:33
  108.6 0.7 slice_bitcast_fusion
  109.3 0.6 slice.54
  109.9 0.0 collective-permute-done.15
  110.0 0.7 copy.30
  (20 shorter events, 0.3 us)
Async XLA Ops:
  0.6 12.6 %copy-start = (bf16[2,16,8192]{2,1,0:T(8,128)(2,1)S(1)}, bf16[2,16,8192]{2,1,0:T(8,128)(2,1)}, u32[]{:S(2)}) copy-start(bf16[2,16,8192]{2,1,0:T(8,128)(2,1)} %param.14) | copy-start | bytes 1572868
  0.6 16.6 %copy-start.9 = (s32[2]{0:T(128)S(1)}, s32[2]{0:T(128)}, u32[]{:S(2)}) copy-start(s32[2]{0:T(128)} %param.16) | copy-start | bytes 28
  0.7 22.9 %copy-start.8 = (s32[2,128]{1,0:T(2,128)S(1)}, s32[2,128]{1,0:T(2,128)}, u32[]{:S(2)}) copy-start(s32[2,128]{1,0:T(2,128)} %param.17) | copy-start | bytes 3076
  0.7 17.2 %collective-permute-start.1 = (bf16[768,128]{1,0:T(8,128)(2,1)}, bf16[768,128]{1,0:T(8,128)(2,1)S(1)}, u32[]{:S(2)}, u32[]{:S(2)}) collective-permute-start(bf16[768,128]{1,0:T(8,128)(2,1)} %param.13), channel_id=1, source_target_pairs={{0,8},{1,9},{2,10},{3,11},{4,12},{5,13},{6,14},{7,15},{8,16},{9,17... | collective-permute-start | bytes 589832 | tf_op jit(solution)/shard_map/ppermute | solution.py:46
  2.8 21.4 %collective-permute-start = (bf16[768,128]{1,0:T(8,128)(2,1)}, bf16[768,128]{1,0:T(8,128)(2,1)S(1)}, u32[]{:S(2)}, u32[]{:S(2)}) collective-permute-start(bf16[768,128]{1,0:T(8,128)(2,1)} %param.12), channel_id=1, source_target_pairs={{0,8},{1,9},{2,10},{3,11},{4,12},{5,13},{6,14},{7,15},{8,16},{9,17... | collective-permute-start | bytes 589832 | tf_op jit(solution)/shard_map/ppermute | solution.py:33
  7.0 26.2 %copy-start.1 = (bf16[2,768,128]{2,1,0:T(8,128)(2,1)}, bf16[2,768,128]{2,1,0:T(8,128)(2,1)S(1)}, u32[]{:S(2)}) copy-start(bf16[2,768,128]{2,1,0:T(8,128)(2,1)S(1)} %pad_maximum_fusion.own_in) | copy-start | bytes 1179652
  7.0 24.8 %collective-permute-start.3 = (bf16[2,768,128]{2,1,0:T(8,128)(2,1)S(1)}, bf16[2,768,128]{2,1,0:T(8,128)(2,1)S(1)}, u32[]{:S(2)}, u32[]{:S(2)}) collective-permute-start(bf16[2,768,128]{2,1,0:T(8,128)(2,1)S(1)} %pad_maximum_fusion.own_in), channel_id=1, source_target_pairs={{0,4},{1,5},{2,6},{3,7},{4,16},{5,17},{6,18},{7,19},{8,12},{9,13},... | collective-permute-start | bytes 1179656 | tf_op jit(solution)/shard_map/ppermute | solution.py:33
  17.8 13.8 %collective-permute-start.2 = (bf16[768,128]{1,0:T(8,128)(2,1)S(1)}, bf16[768,128]{1,0:T(8,128)(2,1)S(1)}, u32[]{:S(2)}, u32[]{:S(2)}) collective-permute-start(bf16[768,128]{1,0:T(8,128)(2,1)S(1)} %collective-permute-done.1), channel_id=1, source_target_pairs={{0,35},{1,34},{2,33},{3,32},{4,39},{5,38},{6,37},{7,36},{32,67},{3... | collective-permute-start | bytes 589832 | tf_op jit(solution)/shard_map/ppermute | solution.py:47
  24.2 9.0 %copy-start.5 = (bf16[768,128]{1,0:T(8,128)(2,1)}, bf16[768,128]{1,0:T(8,128)(2,1)S(1)}, u32[]{:S(2)}) copy-start(bf16[768,128]{1,0:T(8,128)(2,1)S(1)} %collective-permute-done.mid_k_in) | copy-start | bytes 589828
  24.2 7.6 %collective-permute-start.4 = (bf16[768,128]{1,0:T(8,128)(2,1)S(1)}, bf16[768,128]{1,0:T(8,128)(2,1)S(1)}, u32[]{:S(2)}, u32[]{:S(2)}) collective-permute-start(bf16[768,128]{1,0:T(8,128)(2,1)S(1)} %collective-permute-done.mid_k_in), channel_id=1, source_target_pairs={{0,4},{1,5},{2,6},{3,7},{4,0},{5,1},{6,2},{7,3},{8,12},{9,13},{10,... | collective-permute-start | bytes 589832 | tf_op jit(solution)/shard_map/ppermute | solution.py:33
  31.7 1.5 %copy-start.2 = (bf16[768,128]{1,0:T(8,128)(2,1)}, bf16[768,128]{1,0:T(8,128)(2,1)S(1)}, u32[]{:S(2)}) copy-start(bf16[768,128]{1,0:T(8,128)(2,1)S(1)} %broadcast_select_fusion.mid_v_in) | copy-start | bytes 589828
  31.7 1.5 %collective-permute-start.5 = (bf16[768,128]{1,0:T(8,128)(2,1)S(1)}, bf16[768,128]{1,0:T(8,128)(2,1)S(1)}, u32[]{:S(2)}, u32[]{:S(2)}) collective-permute-start(bf16[768,128]{1,0:T(8,128)(2,1)S(1)} %broadcast_select_fusion.mid_v_in), channel_id=1, source_target_pairs={{0,4},{1,5},{2,6},{3,7},{4,0},{5,1},{6,2},{7,3},{8,12},{9,13},{10,... | collective-permute-start | bytes 589832 | tf_op jit(solution)/shard_map/ppermute | solution.py:33
  31.8 1.4 %copy-start.6 = (bf16[768,128]{1,0:T(8,128)(2,1)}, bf16[768,128]{1,0:T(8,128)(2,1)S(1)}, u32[]{:S(2)}) copy-start(bf16[768,128]{1,0:T(8,128)(2,1)S(1)} %collective-permute-done.4.swap_k_in) | copy-start | bytes 589828
  31.8 1.4 %copy-start.4 = (bf16[2,768,128]{2,1,0:T(8,128)(2,1)}, bf16[2,768,128]{2,1,0:T(8,128)(2,1)S(1)}, u32[]{:S(2)}) copy-start(bf16[2,768,128]{2,1,0:T(8,128)(2,1)S(1)} %collective-permute-done.3.far_in) | copy-start | bytes 1179652
  33.2 0.7 copy-start.7
  62.8 27.7 %copy-start.3 = (f32[2,768,128]{2,1,0:T(8,128)S(1)}, f32[2,768,128]{2,1,0:T(8,128)}, u32[]{:S(2)}) copy-start(f32[2,768,128]{2,1,0:T(8,128)} %get-tuple-element.31) | copy-start | bytes 2359300
  62.8 2.8 %collective-permute-start.6 = (bf16[36,32,128]{2,1,0:T(8,128)(2,1)}, bf16[36,32,128]{2,1,0:T(8,128)(2,1)S(1)}, u32[]{:S(2)}, u32[]{:S(2)}) collective-permute-start(bf16[36,32,128]{2,1,0:T(8,128)(2,1)} %get-tuple-element.26), channel_id=1, source_target_pairs={{0,4},{1,5},{2,6},{3,7},{4,0},{5,1},{6,2},{7,3},{8,12},{9,13},{10,... | collective-permute-start | bytes 884744 | tf_op jit(solution)/shard_map/ppermute | solution.py:33
  63.0 8.1 %collective-permute-start.8 = (bf16[2,768,128]{2,1,0:T(8,128)(2,1)}, bf16[2,768,128]{2,1,0:T(8,128)(2,1)S(1)}, u32[]{:S(2)}, u32[]{:S(2)}) collective-permute-start(bf16[2,768,128]{2,1,0:T(8,128)(2,1)} %get-tuple-element.29), channel_id=1, source_target_pairs={{0,4},{1,5},{2,6},{3,7},{4,0},{5,1},{6,2},{7,3},{8,12},{9,13},{10,... | collective-permute-start | bytes 1179656 | tf_op jit(solution)/shard_map/ppermute | solution.py:33
  63.4 12.9 %collective-permute-start.7 = (bf16[2,768,128]{2,1,0:T(8,128)(2,1)}, bf16[2,768,128]{2,1,0:T(8,128)(2,1)S(1)}, u32[]{:S(2)}, u32[]{:S(2)}) collective-permute-start(bf16[2,768,128]{2,1,0:T(8,128)(2,1)} %get-tuple-element.27), channel_id=1, source_target_pairs={{4,0},{5,1},{6,2},{7,3},{12,8},{13,9},{14,10},{15,11},{16,4},{17,5... | collective-permute-start | bytes 1179656 | tf_op jit(solution)/shard_map/ppermute | solution.py:33
  67.7 13.4 %all-to-all-start = ((bf16[4,12,32,128]{3,2,1,0:T(8,128)(2,1)}), bf16[4,12,32,128]{3,2,1,0:T(8,128)(2,1)S(1)}, u32[]{:S(2)}, u32[]{:S(2)}) async-start(bf16[4,12,32,128]{3,2,1,0:T(8,128)(2,1)} %pad_maximum_fusion.1), calls=%async_computation | async-start | bytes 786432 | tf_op jit(solution)/shard_map/all_to_all | solution.py:75
  72.3 8.7 %collective-permute-start.9 = (bf16[768,128]{1,0:T(8,128)(2,1)S(1)}, bf16[768,128]{1,0:T(8,128)(2,1)S(1)}, u32[]{:S(2)}, u32[]{:S(2)}) collective-permute-start(bf16[768,128]{1,0:T(8,128)(2,1)S(1)} %get-tuple-element.39), channel_id=1, source_target_pairs={{0,24},{1,25},{2,26},{3,27},{4,28},{5,29},{6,30},{7,31},{8,0},{9,1... | collective-permute-start | bytes 589832 | tf_op jit(solution)/shard_map/ppermute | solution.py:58
  75.1 15.5 %collective-permute-start.10 = (bf16[768,128]{1,0:T(8,128)(2,1)S(1)}, bf16[768,128]{1,0:T(8,128)(2,1)S(1)}, u32[]{:S(2)}, u32[]{:S(2)}) collective-permute-start(bf16[768,128]{1,0:T(8,128)(2,1)S(1)} %get-tuple-element.38), channel_id=1, source_target_pairs={{8,0},{9,1},{10,2},{11,3},{12,4},{13,5},{14,6},{15,7},{16,8},{17,9... | collective-permute-start | bytes 589832 | tf_op jit(solution)/shard_map/ppermute | solution.py:33
  81.0 9.5 %collective-permute-start.11 = (bf16[768,128]{1,0:T(8,128)(2,1)S(1)}, bf16[768,128]{1,0:T(8,128)(2,1)S(1)}, u32[]{:S(2)}, u32[]{:S(2)}) collective-permute-start(bf16[768,128]{1,0:T(8,128)(2,1)S(1)} %collective-permute-done.9), channel_id=1, source_target_pairs={{56,27},{57,26},{58,25},{59,24},{60,31},{61,30},{62,29},{63,28},{8... | collective-permute-start | bytes 589832 | tf_op jit(solution)/shard_map/ppermute | solution.py:70
  82.6 20.4 %all-to-all-start.1 = ((bf16[8,5,32,128]{3,2,1,0:T(8,128)(2,1)}), bf16[8,5,32,128]{3,2,1,0:T(8,128)(2,1)S(1)}, u32[]{:S(2)}, u32[]{:S(2)}) async-start(bf16[8,5,32,128]{3,2,1,0:T(8,128)(2,1)} %pad_maximum_fusion.2), calls=%async_computation.1 | async-start | bytes 655360 | tf_op jit(solution)/shard_map/all_to_all | solution.py:75
  90.7 6.4 %collective-permute-start.12 = (bf16[2,192,128]{2,1,0:T(8,128)(2,1)S(1)}, bf16[2,192,128]{2,1,0:T(8,128)(2,1)S(1)}, u32[]{:S(2)}, u32[]{:S(2)}) collective-permute-start(bf16[2,192,128]{2,1,0:T(8,128)(2,1)S(1)} %get-tuple-element.42), channel_id=1, source_target_pairs={{0,1},{1,0},{2,3},{3,2},{4,5},{5,4},{6,7},{7,6},{8,9},{9,8},{10,11... | collective-permute-start | bytes 294920 | tf_op jit(solution)/shard_map/ppermute | solution.py:383
  90.8 7.2 %collective-permute-start.13 = (bf16[2,192,128]{2,1,0:T(8,128)(2,1)S(1)}, bf16[2,192,128]{2,1,0:T(8,128)(2,1)S(1)}, u32[]{:S(2)}, u32[]{:S(2)}) collective-permute-start(bf16[2,192,128]{2,1,0:T(8,128)(2,1)S(1)} %get-tuple-element.41), channel_id=1, source_target_pairs={{0,2},{1,3},{2,0},{3,1},{4,6},{5,7},{6,4},{7,5},{8,10},{9,11},{10,... | collective-permute-start | bytes 294920 | tf_op jit(solution)/shard_map/ppermute | solution.py:383
  92.7 10.2 %collective-permute-start.14 = (bf16[2,192,128]{2,1,0:T(8,128)(2,1)S(1)}, bf16[2,192,128]{2,1,0:T(8,128)(2,1)S(1)}, u32[]{:S(2)}, u32[]{:S(2)}) collective-permute-start(bf16[2,192,128]{2,1,0:T(8,128)(2,1)S(1)} %get-tuple-element.40), channel_id=1, source_target_pairs={{0,3},{1,2},{2,1},{3,0},{4,7},{5,6},{6,5},{7,4},{8,11},{9,10},{10,... | collective-permute-start | bytes 294920 | tf_op jit(solution)/shard_map/ppermute | solution.py:383
  103.0 6.9 %collective-permute-start.15 = (f32[4,32,128]{2,1,0:T(8,128)S(1)}, f32[4,32,128]{2,1,0:T(8,128)S(1)}, u32[]{:S(2)}, u32[]{:S(2)}) collective-permute-start(f32[4,32,128]{2,1,0:T(8,128)S(1)} %slice.55), channel_id=1, source_target_pairs={{0,4},{1,5},{2,6},{3,7},{4,0},{5,1},{6,2},{7,3},{8,12},{9,13},{10,... | collective-permute-start | bytes 196616 | tf_op jit(solution)/shard_map/ppermute | solution.py:33

commit v5 on v4

--- a/solution.py
+++ b/solution.py
@@ -177,21 +177,18 @@
     def grads_of(j, query, grad, scale, delta):
         for d, part, at in chunks(stretch, chunk):
             p = score[j, at, :] * scale
-            ds = p * (dprob[j, at, :] - delta)
+            ds = (p * (dprob[j, at, :] - delta)).astype(jnp.bfloat16)
+            p = p.astype(jnp.bfloat16)
             if d == 0:
-                early = rel >= place + part.start
-                zero = jnp.zeros_like(p)
-                split = (
-                    (0, jnp.where(early, p, zero), jnp.where(early, ds, zero)),
-                    (3, jnp.where(early, zero, p), jnp.where(early, zero, ds)),
-                )
+                early = jnp.where(rel >= place + part.start, 1.0, 0.0).astype(jnp.bfloat16)
+                p_own, ds_own = p * early, ds * early
+                split = ((0, p_own, ds_own), (3, p - p_own, ds - ds_own))
             else:
                 split = ((d, p, ds),)
             for e, p_e, ds_e in split:
-                ds_e = ds_e.astype(jnp.bfloat16)
                 dscore_low[j, e * stretch + part.start : e * stretch + part.stop, :] = ds_e
                 acc_k[e, part, :] += dot(ds_e, query, NN)
-                acc_v[e, part, :] += dot(p_e.astype(jnp.bfloat16), grad, NN)
+                acc_v[e, part, :] += dot(p_e, grad, NN)
         part = (dot(key_t[...], dscore_low[j], NN).T * factor).astype(jnp.bfloat16)
         for a in range(adapters):
             dquery[step * per_step + j, a] = part[a * rows : (a + 1) * rows]
@@ -242,7 +239,7 @@
     _, stretch, head_dim = own.shape
     heads = features // head_dim
     rank, wide, width = low.shape[2], rows * adapters, hidden.shape[2]
-    per_step = 2
+    per_step = 4
     assert heads == 2 * chips and width == 2 * chips * outer * head_dim
     body = functools.partial(
         attention_kernel,

time: 112 us -> 112 us (level)
  no operation moved by 1% of the time
where the time goes in v5:
time: 112 us; the launch traced here: 110 us
  starting transfers between devices  44.7 us (40%)
  Pallas kernels  28.8 us (26%)
  waiting for transfers between devices  22.5 us (20%)
  other arithmetic  6.46 us (6%)
  matrix products  4.04 us (4%)
  local copies, waits for them, and re-layouts  2.82 us (3%)
    pallas_call x1, Pallas kernels, attention_grads(): pl.pallas_call(body, grid_spec=pltpu.PrefetchScalarGridSpec(num_scalar_pr...  28.8 us
    ppermute x9, starting transfers between devices, moved(): return lax.ppermute(value, both_axes, pairs)  18.9 us
    all_to_all x2, starting transfers between devices, grouped(): lax.all_to_all(value, 'seq', 0, 0, axis_index_groups=groups, tiled=True)  11 us
    ppermute x3, waiting for transfers between devices, local(): lax.ppermute(share, 'adapter', [(a, a ^ other) for a in range(planes)])  8.57 us
    ppermute x1, waiting for transfers between devices, moved_two_ahead(): relayed = lax.ppermute(value, both_axes, over)  7.46 us
    ppermute x1, starting transfers between devices, moved_two_ahead(): relayed = lax.ppermute(value, both_axes, over)  5.74 us
    ppermute x1, waiting for transfers between devices, round_x_back(): return lax.ppermute(value, both_axes, pairs)  5.05 us
    dot_general x1, matrix products, local(): jnp.einsum('tbu,tyu->tby', hidden, adapter_down_weight, preferred_element...  4.04 us
  transfers between devices with their start and end apart: 18, of which 6 were waited for; matrix products, arithmetic and copies ran while one was open for 11% of the time, Pallas kernels for 0%

profile of v5, /device:TPU:1, one launch (start us, length us, event | category | flops | bytes accessed | tf_op | source)
XLA Modules:
  0.0 110.4 jit_solution(5327711192083518880)
XLA Ops:
  0.6 0.0 copy-start
  0.6 0.0 copy-start.9
  0.7 0.0 copy-start.8
  0.7 2.1 %collective-permute-start.1 = (bf16[768,128]{1,0:T(8,128)(2,1)}, bf16[768,128]{1,0:T(8,128)(2,1)S(1)}, u32[]{:S(2)}, u32[]{:S(2)}) collective-permute-start(bf16[768,128]{1,0:T(8,128)(2,1)} %param.13), channel_id=1, source_target_pairs={{0,8},{1,9},{2,10},{3,11},{4,12},{5,13},{6,14},{7,15},{8,16},{9,17... | collective-permute-start | bytes 589832 | tf_op jit(solution)/shard_map/ppermute | solution.py:46
  2.8 3.1 %collective-permute-start = (bf16[768,128]{1,0:T(8,128)(2,1)}, bf16[768,128]{1,0:T(8,128)(2,1)S(1)}, u32[]{:S(2)}, u32[]{:S(2)}) collective-permute-start(bf16[768,128]{1,0:T(8,128)(2,1)} %param.12), channel_id=1, source_target_pairs={{0,8},{1,9},{2,10},{3,11},{4,12},{5,13},{6,14},{7,15},{8,16},{9,17... | collective-permute-start | bytes 589832 | tf_op jit(solution)/shard_map/ppermute | solution.py:33
  5.9 1.1 pad_maximum_fusion.own_in
  7.0 0.0 copy-start.1
  7.0 6.2 %collective-permute-start.3 = (bf16[2,768,128]{2,1,0:T(8,128)(2,1)S(1)}, bf16[2,768,128]{2,1,0:T(8,128)(2,1)S(1)}, u32[]{:S(2)}, u32[]{:S(2)}) collective-permute-start(bf16[2,768,128]{2,1,0:T(8,128)(2,1)S(1)} %pad_maximum_fusion.own_in), channel_id=1, source_target_pairs={{0,4},{1,5},{2,6},{3,7},{4,16},{5,17},{6,18},{7,19},{8,12},{9,13},... | collective-permute-start | bytes 1179656 | tf_op jit(solution)/shard_map/ppermute | solution.py:33
  13.2 0.0 copy-done
  13.2 4.0 %convolution_convert_fusion.low_ref = bf16[2,128,16]{2,1,0:T(8,128)(2,1)} fusion(bf16[2,128,8192]{2,1,0:T(8,128)(2,1)} %hidden_in.1, bf16[2,16,8192]{2,1,0:T(8,128)(2,1)S(1)} %copy-done), kind=kOutput, calls=%fused_computation | convolution fusion | flops 67112960 | bytes 4726784 | tf_op jit(solution)/shard_map/tbu,tyu->tby/dot_general | solution.py:327
  17.2 0.0 copy-done.9
  17.2 0.6 pad_add_fusion.where_ref
  17.8 0.0 collective-permute-done.1
  17.8 5.7 %collective-permute-start.2 = (bf16[768,128]{1,0:T(8,128)(2,1)S(1)}, bf16[768,128]{1,0:T(8,128)(2,1)S(1)}, u32[]{:S(2)}, u32[]{:S(2)}) collective-permute-start(bf16[768,128]{1,0:T(8,128)(2,1)S(1)} %collective-permute-done.1), channel_id=1, source_target_pairs={{0,35},{1,34},{2,33},{3,32},{4,39},{5,38},{6,37},{7,36},{32,67},{3... | collective-permute-start | bytes 589832 | tf_op jit(solution)/shard_map/ppermute | solution.py:47
  23.6 0.0 copy-done.8
  23.6 0.6 broadcast_subtract_fusion
  24.2 0.0 collective-permute-done.mid_k_in
  24.2 0.0 collective-permute-start.4
  24.2 7.5 %collective-permute-done.2 = bf16[768,128]{1,0:T(8,128)(2,1)S(1)} collective-permute-done((bf16[768,128]{1,0:T(8,128)(2,1)S(1)}, bf16[768,128]{1,0:T(8,128)(2,1)S(1)}, u32[]{:S(2)}, u32[]{:S(2)}) %collective-permute-start.2) | collective-permute-done | bytes 196640 | tf_op jit(solution)/shard_map/ppermute | solution.py:47
  31.7 0.0 copy-start.2
  31.7 0.1 collective-permute-start.5
  31.8 0.0 collective-permute-done.4.swap_k_in
  31.8 0.0 copy-start.6
  31.8 0.0 collective-permute-done.3.far_in
  31.8 0.0 copy-start.4
  31.8 1.4 %collective-permute-done.5.swap_v_in = bf16[768,128]{1,0:T(8,128)(2,1)S(1)} collective-permute-done((bf16[768,128]{1,0:T(8,128)(2,1)S(1)}, bf16[768,128]{1,0:T(8,128)(2,1)S(1)}, u32[]{:S(2)}, u32[]{:S(2)}) %collective-permute-start.5) | collective-permute-done | bytes 196640 | tf_op jit(solution)/shard_map/ppermute | solution.py:33
  33.2 0.0 copy-done.1
  33.2 0.7 copy-done.7
  33.9 28.8 %attention_grads.1 = (f32[2,768,128]{2,1,0:T(8,128)}, f32[2,768,128]{2,1,0:T(8,128)}, bf16[2,768,128]{2,1,0:T(8,128)(2,1)}, bf16[2,768,128]{2,1,0:T(8,128)(2,1)}...) custom-call(s32[3]{0:T(128)} %pad_add_fusion.where_ref, s32[1,256]{1,0:T(1,128)} %bitcast.58, ...), custom_call_target="tpu_custom_call" | custom-call | tf_op jit(solution)/shard_map/attention_grads/pallas_call | solution.py:261
  62.8 0.0 copy-start.3
  62.8 0.2 collective-permute-start.6
  63.0 0.4 collective-permute-start.8
  63.4 2.0 %collective-permute-start.7 = (bf16[2,768,128]{2,1,0:T(8,128)(2,1)}, bf16[2,768,128]{2,1,0:T(8,128)(2,1)S(1)}, u32[]{:S(2)}, u32[]{:S(2)}) collective-permute-start(bf16[2,768,128]{2,1,0:T(8,128)(2,1)} %get-tuple-element.27), channel_id=1, source_target_pairs={{4,0},{5,1},{6,2},{7,3},{12,8},{13,9},{14,10},{15,11},{16,4},{17,5... | collective-permute-start | bytes 1179656 | tf_op jit(solution)/shard_map/ppermute | solution.py:33
  65.4 0.0 collective-permute-done.6
  65.4 1.1 %add_convert_fusion = bf16[36,32,128]{2,1,0:T(8,128)(2,1)S(1)} fusion(f32[36,32,128]{2,1,0:T(8,128)} %get-tuple-element.25, bf16[36,32,128]{2,1,0:T(8,128)(2,1)S(1)} %collective-permute-done.6), kind=kLoop, calls=%fused_computation.3 | loop fusion | flops 442368 | bytes 1179648 | tf_op jit(solution)/shard_map/convert_element_type | solution.py:359
  66.6 0.8 pad_maximum_fusion.1
  67.4 3.5 %all-to-all-start = ((bf16[4,12,32,128]{3,2,1,0:T(8,128)(2,1)}), bf16[4,12,32,128]{3,2,1,0:T(8,128)(2,1)S(1)}, u32[]{:S(2)}, u32[]{:S(2)}) async-start(bf16[4,12,32,128]{3,2,1,0:T(8,128)(2,1)} %pad_maximum_fusion.1), calls=%async_computation | async-start | bytes 786432 | tf_op jit(solution)/shard_map/all_to_all | solution.py:75
  70.9 0.0 collective-permute-done.8
  70.9 1.2 %fusion.1 = (bf16[768,128]{1,0:T(8,128)(2,1)S(1)}, bf16[768,128]{1,0:T(8,128)(2,1)S(1)}) fusion(f32[2,768,128]{2,1,0:T(8,128)} %get-tuple-element.28, bf16[2,768,128]{2,1,0:T(8,128)(2,1)S(1)} %collective-permute-done.8), kind=kLoop, calls=%fused_computation.10 | loop fusion | flops 589824 | bytes 1572864 | tf_op jit(solution)/shard_map/convert_element_type | solution.py:351
  72.1 2.7 %collective-permute-start.9 = (bf16[768,128]{1,0:T(8,128)(2,1)S(1)}, bf16[768,128]{1,0:T(8,128)(2,1)S(1)}, u32[]{:S(2)}, u32[]{:S(2)}) collective-permute-start(bf16[768,128]{1,0:T(8,128)(2,1)S(1)} %get-tuple-element.39), channel_id=1, source_target_pairs={{0,24},{1,25},{2,26},{3,27},{4,28},{5,29},{6,30},{7,31},{8,0},{9,1... | collective-permute-start | bytes 589832 | tf_op jit(solution)/shard_map/ppermute | solution.py:58
  74.8 1.3 %collective-permute-start.10 = (bf16[768,128]{1,0:T(8,128)(2,1)S(1)}, bf16[768,128]{1,0:T(8,128)(2,1)S(1)}, u32[]{:S(2)}, u32[]{:S(2)}) collective-permute-start(bf16[768,128]{1,0:T(8,128)(2,1)S(1)} %get-tuple-element.38), channel_id=1, source_target_pairs={{8,0},{9,1},{10,2},{11,3},{12,4},{13,5},{14,6},{15,7},{16,8},{17,9... | collective-permute-start | bytes 589832 | tf_op jit(solution)/shard_map/ppermute | solution.py:33
  76.1 0.0 collective-permute-done.7
  76.1 5.1 %collective-permute-done.9 = bf16[768,128]{1,0:T(8,128)(2,1)S(1)} collective-permute-done((bf16[768,128]{1,0:T(8,128)(2,1)S(1)}, bf16[768,128]{1,0:T(8,128)(2,1)S(1)}, u32[]{:S(2)}, u32[]{:S(2)}) %collective-permute-start.9) | collective-permute-done | bytes 196640 | tf_op jit(solution)/shard_map/ppermute | solution.py:58
  81.1 0.0 all-to-all-done
  81.1 0.7 collective-permute-start.11
  81.8 0.1 reduce_sum.21
  82.0 0.8 pad_maximum_fusion.2
  82.7 7.5 %all-to-all-start.1 = ((bf16[8,5,32,128]{3,2,1,0:T(8,128)(2,1)}), bf16[8,5,32,128]{3,2,1,0:T(8,128)(2,1)S(1)}, u32[]{:S(2)}, u32[]{:S(2)}) async-start(bf16[8,5,32,128]{3,2,1,0:T(8,128)(2,1)} %pad_maximum_fusion.2), calls=%async_computation.1 | async-start | bytes 655360 | tf_op jit(solution)/shard_map/all_to_all | solution.py:75
  90.2 0.0 collective-permute-done.11
  90.3 0.0 collective-permute-done.10
  90.3 0.1 convert_add_fusion
  90.4 0.1 fusion.4
  90.5 0.1 collective-permute-start.12
  90.6 1.9 %collective-permute-start.13 = (bf16[2,192,128]{2,1,0:T(8,128)(2,1)S(1)}, bf16[2,192,128]{2,1,0:T(8,128)(2,1)S(1)}, u32[]{:S(2)}, u32[]{:S(2)}) collective-permute-start(bf16[2,192,128]{2,1,0:T(8,128)(2,1)S(1)} %get-tuple-element.41), channel_id=1, source_target_pairs={{0,2},{1,3},{2,0},{3,1},{4,6},{5,7},{6,4},{7,5},{8,10},{9,11},{10,... | collective-permute-start | bytes 294920 | tf_op jit(solution)/shard_map/ppermute | solution.py:380
  92.5 1.6 %collective-permute-start.14 = (bf16[2,192,128]{2,1,0:T(8,128)(2,1)S(1)}, bf16[2,192,128]{2,1,0:T(8,128)(2,1)S(1)}, u32[]{:S(2)}, u32[]{:S(2)}) collective-permute-start(bf16[2,192,128]{2,1,0:T(8,128)(2,1)S(1)} %get-tuple-element.40), channel_id=1, source_target_pairs={{0,3},{1,2},{2,1},{3,0},{4,7},{5,6},{6,5},{7,4},{8,11},{9,10},{10,... | collective-permute-start | bytes 294920 | tf_op jit(solution)/shard_map/ppermute | solution.py:380
  94.1 2.8 %collective-permute-done.12 = bf16[2,192,128]{2,1,0:T(8,128)(2,1)S(1)} collective-permute-done((bf16[2,192,128]{2,1,0:T(8,128)(2,1)S(1)}, bf16[2,192,128]{2,1,0:T(8,128)(2,1)S(1)}, u32[]{:S(2)}, u32[]{:S(2)}) %collective-permute-start.12) | collective-permute-done | bytes 98336 | tf_op jit(solution)/shard_map/ppermute | solution.py:380
  96.9 0.9 collective-permute-done.13
  97.7 4.9 %collective-permute-done.14 = bf16[2,192,128]{2,1,0:T(8,128)(2,1)S(1)} collective-permute-done((bf16[2,192,128]{2,1,0:T(8,128)(2,1)S(1)}, bf16[2,192,128]{2,1,0:T(8,128)(2,1)S(1)}, u32[]{:S(2)}, u32[]{:S(2)}) %collective-permute-start.14) | collective-permute-done | bytes 98336 | tf_op jit(solution)/shard_map/ppermute | solution.py:380
  102.7 0.0 all-to-all-done.1
  102.7 5.6 %collective-permute-start.15 = (f32[4,32,128]{2,1,0:T(8,128)S(1)}, f32[4,32,128]{2,1,0:T(8,128)S(1)}, u32[]{:S(2)}, u32[]{:S(2)}) collective-permute-start(f32[4,32,128]{2,1,0:T(8,128)S(1)} %slice.55), channel_id=1, source_target_pairs={{0,4},{1,5},{2,6},{3,7},{4,0},{5,1},{6,2},{7,3},{8,12},{9,13},{10,... | collective-permute-start | bytes 196616 | tf_op jit(solution)/shard_map/ppermute | solution.py:33
  108.4 0.7 slice_bitcast_fusion
  109.0 0.6 slice.54
  109.6 0.0 collective-permute-done.15
  109.7 0.7 copy.30
  (20 shorter events, 0.3 us)
Async XLA Ops:
  0.6 12.6 %copy-start = (bf16[2,16,8192]{2,1,0:T(8,128)(2,1)S(1)}, bf16[2,16,8192]{2,1,0:T(8,128)(2,1)}, u32[]{:S(2)}) copy-start(bf16[2,16,8192]{2,1,0:T(8,128)(2,1)} %param.14) | copy-start | bytes 1572868
  0.6 16.6 %copy-start.9 = (s32[2]{0:T(128)S(1)}, s32[2]{0:T(128)}, u32[]{:S(2)}) copy-start(s32[2]{0:T(128)} %param.16) | copy-start | bytes 28
  0.7 22.9 %copy-start.8 = (s32[2,128]{1,0:T(2,128)S(1)}, s32[2,128]{1,0:T(2,128)}, u32[]{:S(2)}) copy-start(s32[2,128]{1,0:T(2,128)} %param.17) | copy-start | bytes 3076
  0.7 17.2 %collective-permute-start.1 = (bf16[768,128]{1,0:T(8,128)(2,1)}, bf16[768,128]{1,0:T(8,128)(2,1)S(1)}, u32[]{:S(2)}, u32[]{:S(2)}) collective-permute-start(bf16[768,128]{1,0:T(8,128)(2,1)} %param.13), channel_id=1, source_target_pairs={{0,8},{1,9},{2,10},{3,11},{4,12},{5,13},{6,14},{7,15},{8,16},{9,17... | collective-permute-start | bytes 589832 | tf_op jit(solution)/shard_map/ppermute | solution.py:46
  2.8 21.4 %collective-permute-start = (bf16[768,128]{1,0:T(8,128)(2,1)}, bf16[768,128]{1,0:T(8,128)(2,1)S(1)}, u32[]{:S(2)}, u32[]{:S(2)}) collective-permute-start(bf16[768,128]{1,0:T(8,128)(2,1)} %param.12), channel_id=1, source_target_pairs={{0,8},{1,9},{2,10},{3,11},{4,12},{5,13},{6,14},{7,15},{8,16},{9,17... | collective-permute-start | bytes 589832 | tf_op jit(solution)/shard_map/ppermute | solution.py:33
  7.0 26.2 %copy-start.1 = (bf16[2,768,128]{2,1,0:T(8,128)(2,1)}, bf16[2,768,128]{2,1,0:T(8,128)(2,1)S(1)}, u32[]{:S(2)}) copy-start(bf16[2,768,128]{2,1,0:T(8,128)(2,1)S(1)} %pad_maximum_fusion.own_in) | copy-start | bytes 1179652
  7.0 24.8 %collective-permute-start.3 = (bf16[2,768,128]{2,1,0:T(8,128)(2,1)S(1)}, bf16[2,768,128]{2,1,0:T(8,128)(2,1)S(1)}, u32[]{:S(2)}, u32[]{:S(2)}) collective-permute-start(bf16[2,768,128]{2,1,0:T(8,128)(2,1)S(1)} %pad_maximum_fusion.own_in), channel_id=1, source_target_pairs={{0,4},{1,5},{2,6},{3,7},{4,16},{5,17},{6,18},{7,19},{8,12},{9,13},... | collective-permute-start | bytes 1179656 | tf_op jit(solution)/shard_map/ppermute | solution.py:33
  17.8 13.8 %collective-permute-start.2 = (bf16[768,128]{1,0:T(8,128)(2,1)S(1)}, bf16[768,128]{1,0:T(8,128)(2,1)S(1)}, u32[]{:S(2)}, u32[]{:S(2)}) collective-permute-start(bf16[768,128]{1,0:T(8,128)(2,1)S(1)} %collective-permute-done.1), channel_id=1, source_target_pairs={{0,35},{1,34},{2,33},{3,32},{4,39},{5,38},{6,37},{7,36},{32,67},{3... | collective-permute-start | bytes 589832 | tf_op jit(solution)/shard_map/ppermute | solution.py:47
  24.2 9.0 %copy-start.5 = (bf16[768,128]{1,0:T(8,128)(2,1)}, bf16[768,128]{1,0:T(8,128)(2,1)S(1)}, u32[]{:S(2)}) copy-start(bf16[768,128]{1,0:T(8,128)(2,1)S(1)} %collective-permute-done.mid_k_in) | copy-start | bytes 589828
  24.2 7.6 %collective-permute-start.4 = (bf16[768,128]{1,0:T(8,128)(2,1)S(1)}, bf16[768,128]{1,0:T(8,128)(2,1)S(1)}, u32[]{:S(2)}, u32[]{:S(2)}) collective-permute-start(bf16[768,128]{1,0:T(8,128)(2,1)S(1)} %collective-permute-done.mid_k_in), channel_id=1, source_target_pairs={{0,4},{1,5},{2,6},{3,7},{4,0},{5,1},{6,2},{7,3},{8,12},{9,13},{10,... | collective-permute-start | bytes 589832 | tf_op jit(solution)/shard_map/ppermute | solution.py:33
  31.7 1.5 %copy-start.2 = (bf16[768,128]{1,0:T(8,128)(2,1)}, bf16[768,128]{1,0:T(8,128)(2,1)S(1)}, u32[]{:S(2)}) copy-start(bf16[768,128]{1,0:T(8,128)(2,1)S(1)} %broadcast_select_fusion.mid_v_in) | copy-start | bytes 589828
  31.7 1.5 %collective-permute-start.5 = (bf16[768,128]{1,0:T(8,128)(2,1)S(1)}, bf16[768,128]{1,0:T(8,128)(2,1)S(1)}, u32[]{:S(2)}, u32[]{:S(2)}) collective-permute-start(bf16[768,128]{1,0:T(8,128)(2,1)S(1)} %broadcast_select_fusion.mid_v_in), channel_id=1, source_target_pairs={{0,4},{1,5},{2,6},{3,7},{4,0},{5,1},{6,2},{7,3},{8,12},{9,13},{10,... | collective-permute-start | bytes 589832 | tf_op jit(solution)/shard_map/ppermute | solution.py:33
  31.8 1.4 %copy-start.6 = (bf16[768,128]{1,0:T(8,128)(2,1)}, bf16[768,128]{1,0:T(8,128)(2,1)S(1)}, u32[]{:S(2)}) copy-start(bf16[768,128]{1,0:T(8,128)(2,1)S(1)} %collective-permute-done.4.swap_k_in) | copy-start | bytes 589828
  31.8 1.4 %copy-start.4 = (bf16[2,768,128]{2,1,0:T(8,128)(2,1)}, bf16[2,768,128]{2,1,0:T(8,128)(2,1)S(1)}, u32[]{:S(2)}) copy-start(bf16[2,768,128]{2,1,0:T(8,128)(2,1)S(1)} %collective-permute-done.3.far_in) | copy-start | bytes 1179652
  33.2 0.7 copy-start.7
  62.8 27.5 %copy-start.3 = (f32[2,768,128]{2,1,0:T(8,128)S(1)}, f32[2,768,128]{2,1,0:T(8,128)}, u32[]{:S(2)}) copy-start(f32[2,768,128]{2,1,0:T(8,128)} %get-tuple-element.31) | copy-start | bytes 2359300
  62.8 2.6 %collective-permute-start.6 = (bf16[36,32,128]{2,1,0:T(8,128)(2,1)}, bf16[36,32,128]{2,1,0:T(8,128)(2,1)S(1)}, u32[]{:S(2)}, u32[]{:S(2)}) collective-permute-start(bf16[36,32,128]{2,1,0:T(8,128)(2,1)} %get-tuple-element.26), channel_id=1, source_target_pairs={{0,4},{1,5},{2,6},{3,7},{4,0},{5,1},{6,2},{7,3},{8,12},{9,13},{10,... | collective-permute-start | bytes 884744 | tf_op jit(solution)/shard_map/ppermute | solution.py:33
  63.0 7.9 %collective-permute-start.8 = (bf16[2,768,128]{2,1,0:T(8,128)(2,1)}, bf16[2,768,128]{2,1,0:T(8,128)(2,1)S(1)}, u32[]{:S(2)}, u32[]{:S(2)}) collective-permute-start(bf16[2,768,128]{2,1,0:T(8,128)(2,1)} %get-tuple-element.29), channel_id=1, source_target_pairs={{0,4},{1,5},{2,6},{3,7},{4,0},{5,1},{6,2},{7,3},{8,12},{9,13},{10,... | collective-permute-start | bytes 1179656 | tf_op jit(solution)/shard_map/ppermute | solution.py:33
  63.4 12.7 %collective-permute-start.7 = (bf16[2,768,128]{2,1,0:T(8,128)(2,1)}, bf16[2,768,128]{2,1,0:T(8,128)(2,1)S(1)}, u32[]{:S(2)}, u32[]{:S(2)}) collective-permute-start(bf16[2,768,128]{2,1,0:T(8,128)(2,1)} %get-tuple-element.27), channel_id=1, source_target_pairs={{4,0},{5,1},{6,2},{7,3},{12,8},{13,9},{14,10},{15,11},{16,4},{17,5... | collective-permute-start | bytes 1179656 | tf_op jit(solution)/shard_map/ppermute | solution.py:33
  67.4 13.7 %all-to-all-start = ((bf16[4,12,32,128]{3,2,1,0:T(8,128)(2,1)}), bf16[4,12,32,128]{3,2,1,0:T(8,128)(2,1)S(1)}, u32[]{:S(2)}, u32[]{:S(2)}) async-start(bf16[4,12,32,128]{3,2,1,0:T(8,128)(2,1)} %pad_maximum_fusion.1), calls=%async_computation | async-start | bytes 786432 | tf_op jit(solution)/shard_map/all_to_all | solution.py:75
  72.1 9.1 %collective-permute-start.9 = (bf16[768,128]{1,0:T(8,128)(2,1)S(1)}, bf16[768,128]{1,0:T(8,128)(2,1)S(1)}, u32[]{:S(2)}, u32[]{:S(2)}) collective-permute-start(bf16[768,128]{1,0:T(8,128)(2,1)S(1)} %get-tuple-element.39), channel_id=1, source_target_pairs={{0,24},{1,25},{2,26},{3,27},{4,28},{5,29},{6,30},{7,31},{8,0},{9,1... | collective-permute-start | bytes 589832 | tf_op jit(solution)/shard_map/ppermute | solution.py:58
  74.8 15.5 %collective-permute-start.10 = (bf16[768,128]{1,0:T(8,128)(2,1)S(1)}, bf16[768,128]{1,0:T(8,128)(2,1)S(1)}, u32[]{:S(2)}, u32[]{:S(2)}) collective-permute-start(bf16[768,128]{1,0:T(8,128)(2,1)S(1)} %get-tuple-element.38), channel_id=1, source_target_pairs={{8,0},{9,1},{10,2},{11,3},{12,4},{13,5},{14,6},{15,7},{16,8},{17,9... | collective-permute-start | bytes 589832 | tf_op jit(solution)/shard_map/ppermute | solution.py:33
  81.1 9.1 %collective-permute-start.11 = (bf16[768,128]{1,0:T(8,128)(2,1)S(1)}, bf16[768,128]{1,0:T(8,128)(2,1)S(1)}, u32[]{:S(2)}, u32[]{:S(2)}) collective-permute-start(bf16[768,128]{1,0:T(8,128)(2,1)S(1)} %collective-permute-done.9), channel_id=1, source_target_pairs={{56,27},{57,26},{58,25},{59,24},{60,31},{61,30},{62,29},{63,28},{8... | collective-permute-start | bytes 589832 | tf_op jit(solution)/shard_map/ppermute | solution.py:70
  82.7 19.9 %all-to-all-start.1 = ((bf16[8,5,32,128]{3,2,1,0:T(8,128)(2,1)}), bf16[8,5,32,128]{3,2,1,0:T(8,128)(2,1)S(1)}, u32[]{:S(2)}, u32[]{:S(2)}) async-start(bf16[8,5,32,128]{3,2,1,0:T(8,128)(2,1)} %pad_maximum_fusion.2), calls=%async_computation.1 | async-start | bytes 655360 | tf_op jit(solution)/shard_map/all_to_all | solution.py:75
  90.5 6.4 %collective-permute-start.12 = (bf16[2,192,128]{2,1,0:T(8,128)(2,1)S(1)}, bf16[2,192,128]{2,1,0:T(8,128)(2,1)S(1)}, u32[]{:S(2)}, u32[]{:S(2)}) collective-permute-start(bf16[2,192,128]{2,1,0:T(8,128)(2,1)S(1)} %get-tuple-element.42), channel_id=1, source_target_pairs={{0,1},{1,0},{2,3},{3,2},{4,5},{5,4},{6,7},{7,6},{8,9},{9,8},{10,11... | collective-permute-start | bytes 294920 | tf_op jit(solution)/shard_map/ppermute | solution.py:380
  90.6 7.2 %collective-permute-start.13 = (bf16[2,192,128]{2,1,0:T(8,128)(2,1)S(1)}, bf16[2,192,128]{2,1,0:T(8,128)(2,1)S(1)}, u32[]{:S(2)}, u32[]{:S(2)}) collective-permute-start(bf16[2,192,128]{2,1,0:T(8,128)(2,1)S(1)} %get-tuple-element.41), channel_id=1, source_target_pairs={{0,2},{1,3},{2,0},{3,1},{4,6},{5,7},{6,4},{7,5},{8,10},{9,11},{10,... | collective-permute-start | bytes 294920 | tf_op jit(solution)/shard_map/ppermute | solution.py:380
  92.5 10.2 %collective-permute-start.14 = (bf16[2,192,128]{2,1,0:T(8,128)(2,1)S(1)}, bf16[2,192,128]{2,1,0:T(8,128)(2,1)S(1)}, u32[]{:S(2)}, u32[]{:S(2)}) collective-permute-start(bf16[2,192,128]{2,1,0:T(8,128)(2,1)S(1)} %get-tuple-element.40), channel_id=1, source_target_pairs={{0,3},{1,2},{2,1},{3,0},{4,7},{5,6},{6,5},{7,4},{8,11},{9,10},{10,... | collective-permute-start | bytes 294920 | tf_op jit(solution)/shard_map/ppermute | solution.py:380
  102.7 6.9 %collective-permute-start.15 = (f32[4,32,128]{2,1,0:T(8,128)S(1)}, f32[4,32,128]{2,1,0:T(8,128)S(1)}, u32[]{:S(2)}, u32[]{:S(2)}) collective-permute-start(f32[4,32,128]{2,1,0:T(8,128)S(1)} %slice.55), channel_id=1, source_target_pairs={{0,4},{1,5},{2,6},{3,7},{4,0},{5,1},{6,2},{7,3},{8,12},{9,13},{10,... | collective-permute-start | bytes 196616 | tf_op jit(solution)/shard_map/ppermute | solution.py:33
